TPU v7x, 32 devices: a whole 2x2x4 slice. The times are simulated.
32 devices in a mesh: reg: 16 (over z, y, x), col: 2 (over core).
Axes of the slice: x: 2, y: 2, z: 4, core: 2. Of those that a mesh axis runs over, the one named last changes fastest.
Arguments:
- innovation: float32 [64, 131072], P(None, ('reg', 'col')), may hold values from -6 to 6
- obs_along: float32 [131072], P(('reg', 'col')), may hold values from 0 to 2
- obs_across: float32 [131072], P(('reg', 'col')), may hold values from 0 to 32
- obs_scale: float32 [131072], P(('reg', 'col')), may hold values from 0.5 to 2
- obs_error: float32 [131072], P(('reg', 'col')), may hold values from 0.1 to 1
- obs_gain: float32 [131072], P(('reg', 'col')), may hold values from 0.3 to 3
- pair_live: int32 [128, 2], P(('reg', 'col')), may hold values 0 or 1
- obs_count: int32 [128], P(('reg', 'col')), may hold values from 256 to 1024, as said below
- col_owner: int32 [131072], P(('reg', 'col')), may hold values from 0 to 32767, as said below
Outputs:
- weights: float32 [64, 131072], P(None, ('reg', 'col'))
- increments: float32 [64, 32768], P(None, ('reg', 'col'))
Inputs may be any that keep to these rules, and one draw needn't show every extreme that they name: `obs_count`: slots of a region block at or after its count are empty. Some region holds 1024 observations and some holds 256. `col_owner`: observation slot o lies in device block k = o // 4096, and its column is one of k * 1024 to k * 1024 + 2 * 1024 - 1, taken modulo 32768; column block k belongs to the same position k in the order of devices.
All inputs are finite; a program needn't handle non-finite values. No bound on the sum of `pair_live` on one device may be relied on, other than what follows from the above.
Results may differ from a plain program's by a relative error of at most 0.0003.
Values sent between devices are 32-bit elements; how exact they have to be, the bound alone decides.
A program may use at most 64 MiB of HBM per device.

v0:
```python
import functools

import jax
import jax.numpy as jnp
from jax import lax
from jax.experimental import pallas as pl
from jax.experimental.pallas import tpu as pltpu
from jax.sharding import PartitionSpec as P

ROWS = 1024
REACH = 2
COLS_DEV = 1024
META = 16
KB = 128
NB = 128
UNROLL = 4
DEAD = 1e9
VMEM_LIMIT = 60 * 1024 * 1024

highest = lax.Precision.HIGHEST
f32 = jnp.float32
bf16 = jnp.bfloat16
NT = (((1,), (1,)), ((), ()))
NN = (((1,), (0,)), ((), ()))
TN = (((0,), (0,)), ((), ()))
vmem = pl.BlockSpec(memory_space=pltpu.VMEM)
smem = pl.BlockSpec(memory_space=pltpu.SMEM)


def shift(block, distance):
    axis = ("reg", "col")
    n = lax.axis_size(axis)
    return lax.ppermute(block, axis, [((i - distance) % n, i) for i in range(n)])


def dot(a, b, dims=NN):
    return lax.dot_general(a, b, dims, preferred_element_type=f32)


def two(x):
    hi = x.astype(bf16)
    return hi, (x - hi.astype(f32)).astype(bf16)


def three(x):
    hi = x.astype(bf16)
    rest = x - hi.astype(f32)
    mid = rest.astype(bf16)
    return hi, mid, (rest - mid.astype(f32)).astype(bf16)


def combine(coef_t, blocks):
    chi, clo = two(coef_t)
    bhi, blo = two(blocks)
    return dot(
        jnp.concatenate([chi, chi, clo], axis=1), jnp.concatenate([bhi, blo, bhi], axis=0)
    )


def params():
    return pltpu.CompilerParams(vmem_limit_bytes=VMEM_LIMIT)


def sort_kernel(innov_ref, meta_ref, first_ref, last_ref, rank_ref, own_ref):
    regions = innov_ref.shape[1] // ROWS
    kept = first_ref.shape[0]
    sub = lax.broadcasted_iota(jnp.int32, (ROWS, 128), 0)
    lane = lax.broadcasted_iota(jnp.int32, (ROWS, 128), 1)
    for g in range(regions):
        cols = pl.ds(g * ROWS, ROWS)
        meta = meta_ref[:, cols]
        key = meta[6:7]
        live = (key < 0.5 * DEAD).astype(f32)
        key_col = jnp.broadcast_to(key, (128, ROWS)).T
        ranks = []
        for b in range(ROWS // 128):
            mine = key[:, b * 128 : (b + 1) * 128]
            before = (key_col < mine) | ((key_col == mine) & (sub < lane + b * 128))
            ranks.append(jnp.sum(before.astype(f32), axis=0, keepdims=True))
        rank = jnp.concatenate(ranks, axis=1)
        rank_ref[:, cols] = jnp.broadcast_to(rank, (8, ROWS))
        stack = jnp.concatenate([innov_ref[:, cols] * live, meta], axis=0)
        lhs = jnp.concatenate(three(stack), axis=0)
        n = stack.shape[0]
        rank_i = rank.astype(jnp.int32)
        out_ref = first_ref if g < regions // 2 else last_ref
        for c in range(ROWS // 256):
            slot = lax.broadcasted_iota(jnp.int32, (256, ROWS), 0) + c * 256
            place = (slot == rank_i).astype(f32).astype(bf16)
            got = dot(lhs, place, NT)
            start = (g % (regions // 2)) * ROWS + c * 256
            got = (got[:n] + got[n : 2 * n] + got[2 * n :])[:kept]
            out_ref[:, start : start + 256] = got
            own_ref[:, g * ROWS + c * 256 : g * ROWS + (c + 1) * 256] = got[kept - 8 :]


def sort_call(innov, meta):
    ens, n = innov.shape
    half = jax.ShapeDtypeStruct((ens + 8, n // 2), f32)
    return pl.pallas_call(
        sort_kernel,
        out_shape=(half, half) + (jax.ShapeDtypeStruct((8, n), f32),) * 2,
        in_specs=[vmem, vmem],
        out_specs=(vmem,) * 4,
        compiler_params=params(),
        name="sort_slots",
    )(innov, meta)


def build_list(bounds_ref, list_ref, tile_ref, count_ref, tiles):
    per = ROWS // NB
    zero_block = (tiles // per + 2 * REACH) * (ROWS // KB)

    def one(t, trip):
        g = t // per
        base = trip * UNROLL

        def put(dh, jb, n):
            list_ref[n] = (g + dh) * (ROWS // KB) + jb
            return n + 1

        n = base
        for dh in range(2 * REACH + 1):
            lo = bounds_ref[0, dh * tiles + t]
            hi = bounds_ref[1, dh * tiles + t]
            n = lax.fori_loop(lo, hi, functools.partial(put, dh), n)
        for p in range(UNROLL):
            list_ref[n + p] = zero_block
        end = (n + UNROLL - 1) // UNROLL

        def mark(k, carry):
            tile_ref[k] = t
            return carry

        lax.fori_loop(trip, end, mark, 0)
        return end

    trips = lax.fori_loop(0, tiles, one, 0)
    tile_ref[trips] = 0
    for p in range(UNROLL):
        list_ref[trips * UNROLL + p] = zero_block
    count_ref[0] = trips


def prepare(chunks, row_ref, along_ref, across_ref):
    width = chunks[0].shape[1]
    per = width // ROWS
    for c, ref in enumerate(chunks):
        row_ref[:, c * width : (c + 1) * width] = ref[ref.shape[0] - 8 :, :]
        for r in range(per):
            h = c * per + r
            at = slice(h * ROWS, (h + 1) * ROWS)
            row_ref[0:1, at] = row_ref[0:1, at] + float(h)
            col = row_ref[:, at].T
            along_ref[at, :] = jnp.broadcast_to(col[:, 0:1], (ROWS, NB))
            across_ref[at, :] = jnp.broadcast_to(col[:, 1:2], (ROWS, NB))
    wide = width * len(chunks)
    along_ref[wide : wide + KB, :] = jnp.zeros((KB, NB), f32)
    across_ref[wide : wide + KB, :] = jnp.zeros((KB, NB), f32)


def apply_cov(list_ref, tile_ref, count_ref, row_ref, along_ref, across_ref, v_ref, img_ref, stack_ref, s_ref):
    ens, wide = v_ref.shape
    own = img_ref.shape[1]
    lead = REACH * ROWS
    chunk = 2048
    for c in range(wide // chunk):
        at = pl.ds(c * chunk, chunk)
        hi, lo = two(v_ref[:, at] * row_ref[2:3, at])
        stack_ref[0:ens, at] = hi
        stack_ref[ens : 2 * ens, at] = lo
    stack_ref[:, wide : wide + KB] = jnp.zeros((2 * ens, KB), bf16)
    s_ref[...] = jnp.zeros_like(s_ref)
    img_ref[...] = jnp.zeros_like(img_ref)
    depth = UNROLL * KB

    def step(k, carry):
        before = jnp.maximum(k - 1, 0)
        vhi, vlo = [], []
        for p in range(UNROLL):
            block = list_ref[before * UNROLL + p]
            part = stack_ref[:, pl.ds(pl.multiple_of(block * KB, KB), KB)]
            vhi.append(part[:ens])
            vlo.append(part[ens:])
        lhs = jnp.concatenate(vhi + vlo + vhi, axis=1)
        shi = s_ref[:depth]
        rhs = jnp.concatenate([shi, shi, s_ref[depth:]], axis=0)
        o_at = pl.ds(pl.multiple_of(tile_ref[before] * NB, NB), NB)
        img_ref[:, o_at] += dot(lhs, rhs)
        i_at = pl.ds(pl.multiple_of(lead + tile_ref[k] * NB, NB), NB)
        a_i = row_ref[0:1, i_at]
        b_i = row_ref[1:2, i_at]
        for p in range(UNROLL):
            block = list_ref[k * UNROLL + p]
            j_at = pl.ds(pl.multiple_of(block * KB, KB), KB)
            da = along_ref[j_at, :] - a_i
            db = across_ref[j_at, :] - b_i
            r2 = da * da + db * db
            r = r2 * lax.rsqrt(jnp.maximum(r2, 1e-30))
            u = jnp.maximum(1.0 - r, 0.0)
            u2 = u * u
            hi, lo = two((u2 * u2) * (r + 0.25))
            s_ref[p * KB : (p + 1) * KB] = hi
            s_ref[depth + p * KB : depth + (p + 1) * KB] = lo
        return carry

    lax.fori_loop(0, count_ref[0] + 1, step, 0)
    for c in range(own // chunk):
        at = slice(c * chunk, (c + 1) * chunk)
        e_at = slice(lead + c * chunk, lead + (c + 1) * chunk)
        img_ref[:, at] = (
            img_ref[:, at] * (row_ref[2:3, e_at] * 0.25) + row_ref[3:4, e_at] * v_ref[:, e_at]
        )


def gram(a, b):
    ahi, alo = two(a)
    bhi, blo = two(b)
    return dot(
        jnp.concatenate([ahi, ahi, alo], axis=1), jnp.concatenate([bhi, blo, bhi], axis=1), NT
    )


def first_kernel(
    bounds_ref,
    c0,
    c1,
    c2,
    c3,
    imga_ref,
    imgb_ref,
    gram_ref,
    list_ref,
    tile_ref,
    count_ref,
    row_ref,
    along_ref,
    across_ref,
    v_ref,
    img_ref,
    stack_ref,
    s_ref,
):
    ens, own = img_ref.shape
    lead = REACH * ROWS
    chunks = [c0, c1, c2, c3]
    build_list(bounds_ref, list_ref, tile_ref, count_ref, own // NB)
    prepare(chunks, row_ref, along_ref, across_ref)
    for c, ref in enumerate(chunks):
        v_ref[:, c * lead : (c + 1) * lead] = ref[:ens, :]
    apply_cov(
        list_ref, tile_ref, count_ref, row_ref, along_ref, across_ref, v_ref, img_ref, stack_ref, s_ref
    )
    imga_ref[...] = img_ref[:, :lead]
    imgb_ref[...] = img_ref[:, lead:]
    r = v_ref[:, lead : lead + own]
    gram_ref[...] = gram(r, jnp.concatenate([r, img_ref[...]], axis=0))


def second_kernel(
    list_ref,
    tile_ref,
    count_ref,
    step_ref,
    c0,
    c1,
    c2,
    c3,
    i0,
    i1,
    i2,
    i3,
    gram_ref,
    row_ref,
    along_ref,
    across_ref,
    v_ref,
    img_ref,
    stack_ref,
    s_ref,
):
    ens, own = img_ref.shape
    lead = REACH * ROWS
    chunks = [c0, c1, c2, c3]
    prepare(chunks, row_ref, along_ref, across_ref)
    step_t = step_ref[...].T
    for c, (ref, image) in enumerate(zip(chunks, [i0, i1, i2, i3])):
        v_ref[:, c * lead : (c + 1) * lead] = ref[:ens, :] - combine(step_t, image[...])
    apply_cov(
        list_ref, tile_ref, count_ref, row_ref, along_ref, across_ref, v_ref, img_ref, stack_ref, s_ref
    )
    r = v_ref[:, lead : lead + own]
    gram_ref[:ens] = gram(r, jnp.concatenate([r, img_ref[...]], axis=0))
    mixed = gram(r, jnp.concatenate([i1[...], i2[...]], axis=1))
    gram_ref[ens:] = jnp.concatenate([mixed, mixed], axis=1)


def scratch(ens, own):
    wide = own + 2 * REACH * ROWS
    return [
        pltpu.VMEM((8, wide), f32),
        pltpu.VMEM((wide + KB, NB), f32),
        pltpu.VMEM((wide + KB, NB), f32),
        pltpu.VMEM((ens, wide), f32),
        pltpu.VMEM((ens, own), f32),
        pltpu.VMEM((2 * ens, wide + KB), bf16),
        pltpu.VMEM((2 * UNROLL * KB, NB), bf16),
    ]


def first_call(bounds, chunks, ens, own):
    tiles = own // NB
    trips = tiles * -(-(2 * REACH + 1) * (ROWS // KB) // UNROLL) + 2
    half = jax.ShapeDtypeStruct((ens, own // 2), f32)
    return pl.pallas_call(
        first_kernel,
        out_shape=(
            half,
            half,
            jax.ShapeDtypeStruct((ens, 2 * ens), f32),
            jax.ShapeDtypeStruct((trips * UNROLL,), jnp.int32),
            jax.ShapeDtypeStruct((trips,), jnp.int32),
            jax.ShapeDtypeStruct((1,), jnp.int32),
        ),
        in_specs=[smem] + [vmem] * 4,
        out_specs=(vmem, vmem, vmem, smem, smem, smem),
        scratch_shapes=scratch(ens, own),
        compiler_params=params(),
        name="operate_first",
    )(bounds, *chunks)


def second_call(lists, step, chunks, images, ens, own):
    return pl.pallas_call(
        second_kernel,
        out_shape=jax.ShapeDtypeStruct((2 * ens, 2 * ens), f32),
        in_specs=[smem] * 3 + [vmem] * 9,
        out_specs=vmem,
        scratch_shapes=scratch(ens, own),
        compiler_params=params(),
        name="operate_second",
    )(*lists, step, *chunks, *images)


def flip(me, size):
    return size * (1 - 2 * ((me // size) % 2))


def exchange_steps(total):
    bits = total.bit_length() - 1
    steps = [[1]] if bits % 2 else []
    for k in range(bits % 2, bits, 2):
        steps.append([2**k, 2 ** (k + 1)])
    return steps


def reduce_kernel(steps, n_col, x_ref, out_ref, send, recv, send_sem, recv_sem):
    me = lax.axis_index("reg") * n_col + lax.axis_index("col")
    partners = []
    for sizes in steps:
        others = [me + flip(me, size) for size in sizes]
        if len(sizes) == 2:
            others.append(others[0] + flip(me, sizes[1]))
        partners.append([(other // n_col, other % n_col) for other in others])
    barrier = pltpu.get_barrier_semaphore()
    for group in partners:
        for other in group:
            pl.semaphore_signal(
                barrier, inc=1, device_id=other, device_id_type=pl.DeviceIdType.MESH
            )
    pl.semaphore_wait(barrier, sum(len(group) for group in partners))
    total = x_ref[...]
    slot = 0
    for k, group in enumerate(partners):
        if k:
            send[k] = total
        copies = []
        for p, other in enumerate(group):
            copies.append(
                pltpu.make_async_remote_copy(
                    src_ref=send.at[k] if k else x_ref,
                    dst_ref=recv.at[slot + p],
                    send_sem=send_sem.at[slot + p],
                    recv_sem=recv_sem.at[slot + p],
                    device_id=other,
                    device_id_type=pl.DeviceIdType.MESH,
                )
            )
        for copy in copies:
            copy.start()
        for copy in copies:
            copy.wait()
        total = total + recv[slot]
        if len(group) == 3:
            total = total + (recv[slot + 1] + recv[slot + 2])
        slot += len(group)
    out_ref[...] = total


def sum_all(x, which):
    n_col = lax.axis_size("col")
    steps = exchange_steps(lax.axis_size("reg") * n_col)
    slots = sum(2 ** len(sizes) - 1 for sizes in steps)
    return pl.pallas_call(
        functools.partial(reduce_kernel, steps, n_col),
        out_shape=jax.ShapeDtypeStruct(x.shape, f32),
        in_specs=[vmem],
        out_specs=vmem,
        scratch_shapes=[
            pltpu.VMEM((len(steps),) + x.shape, f32),
            pltpu.VMEM((slots,) + x.shape, f32),
            pltpu.SemaphoreType.DMA((slots,)),
            pltpu.SemaphoreType.DMA((slots,)),
        ],
        compiler_params=pltpu.CompilerParams(collective_id=which, has_side_effects=True),
        name="sum_all",
    )(x)


def symmetric(matrix):
    return 0.5 * (matrix + matrix.T)


def mm(a, b, dims=NN):
    return lax.dot_general(a, b, dims, precision=highest, preferred_element_type=f32)


def eliminate(chains):
    ens, both = chains[0].shape
    rows = lax.broadcasted_iota(jnp.int32, (ens, both), 0)
    for k in range(ens):
        done = []
        for m in chains:
            col = jnp.broadcast_to(m[:, k : k + 1], (ens, both))
            pivot = m[k : k + 1] / col[k : k + 1]
            done.append(jnp.where(rows == k, pivot, m - col * pivot))
        chains = done
    return [m[:, ens:] for m in chains]


def solve_first_kernel(gram_ref, step_ref, inv_ref, curv_ref):
    ens = gram_ref.shape[0]
    norm = symmetric(gram_ref[:, :ens])
    curv = symmetric(gram_ref[:, ens:])
    rows = lax.broadcasted_iota(jnp.int32, (ens, ens), 0)
    eye = (rows == lax.broadcasted_iota(jnp.int32, (ens, ens), 1)).astype(f32)
    step, inv = eliminate(
        [jnp.concatenate([curv, norm], axis=1), jnp.concatenate([norm, eye], axis=1)]
    )
    step_ref[...] = step
    inv_ref[...] = inv
    curv_ref[...] = curv


def solve_second_kernel(gram_ref, step_ref, inv_ref, curv_ref, coef_ref):
    ens = step_ref.shape[0]
    norm = symmetric(gram_ref[:ens, :ens])
    cross = gram_ref[:ens, ens:]
    mixed = gram_ref[ens:, :ens]
    conj = mm(inv_ref[...], norm)
    coupled = mm(mixed, conj)
    quad = mm(conj, mm(curv_ref[...], conj), TN)
    curv = symmetric(cross + coupled + coupled.T + quad)
    (step,) = eliminate([jnp.concatenate([curv, norm], axis=1)])
    step0 = step_ref[...]
    keep = step0 + step + mm(conj, step)
    coef_ref[...] = jnp.concatenate([keep.T, -mm(step0, step).T], axis=1)


def solve_first(grams):
    ens = grams.shape[0]
    small = jax.ShapeDtypeStruct((ens, ens), f32)
    return pl.pallas_call(
        solve_first_kernel,
        out_shape=(small, small, small),
        in_specs=[vmem],
        out_specs=(vmem, vmem, vmem),
        name="solve_first",
    )(grams)


def solve_second(grams, step0, inv0, curv0):
    ens = step0.shape[0]
    return pl.pallas_call(
        solve_second_kernel,
        out_shape=jax.ShapeDtypeStruct((ens, 2 * ens), f32),
        in_specs=[vmem] * 4,
        out_specs=vmem,
        name="solve_second",
    )(grams, step0, inv0, curv0)


def add_columns(stack, owner, cols_ref):
    ens = cols_ref.shape[0]
    for c in range(2 * COLS_DEV // 256):
        slot = lax.broadcasted_iota(jnp.int32, (256, ROWS), 0) + c * 256
        hot = (slot == owner).astype(f32).astype(bf16)
        got = dot(stack, hot, NT)
        part = slice(c * 256, (c + 1) * 256)
        cols_ref[:, part] += got[:ens] + got[ens:]


def innov_columns_kernel(innov_ref, info_ref, cols_ref):
    cols_ref[...] = jnp.zeros_like(cols_ref)

    def one(g, carry):
        at = pl.ds(pl.multiple_of(g * ROWS, ROWS), ROWS)
        scale = info_ref[0:1, at] * info_ref[1:2, at]
        owner = info_ref[2:3, at].astype(jnp.int32)
        add_columns(jnp.concatenate(two(innov_ref[:, at] * scale), axis=0), owner, cols_ref)
        return carry

    lax.fori_loop(0, innov_ref.shape[1] // ROWS, one, 0)


def columns_kernel(info_ref, rank_ref, imga_ref, imgb_ref, back_ref, cols_ref):
    ens, own = back_ref.shape
    half = own // 2
    cols_ref[...] = jnp.zeros_like(cols_ref)
    for g in range(own // ROWS):
        at = slice(g * ROWS, (g + 1) * ROWS)
        rank = rank_ref[0:1, at].astype(jnp.int32)
        img_ref = imga_ref if g * ROWS < half else imgb_ref
        begin = (g * ROWS) % half
        lhs = jnp.concatenate(two(img_ref[:, begin : begin + ROWS]), axis=0)
        total = jnp.zeros((2 * ens, ROWS), f32)
        for c in range(ROWS // 256):
            slot = lax.broadcasted_iota(jnp.int32, (256, ROWS), 0) + c * 256
            place = (slot == rank).astype(f32).astype(bf16)
            total = total + dot(lhs[:, c * 256 : (c + 1) * 256], place)
        image = total[:ens] + total[ens:]
        back_ref[:, at] = image
        owner = info_ref[2:3, at].astype(jnp.int32)
        add_columns(jnp.concatenate(two(image * info_ref[0:1, at]), axis=0), owner, cols_ref)


def innov_columns_call(innov, info):
    ens, own = innov.shape
    return pl.pallas_call(
        innov_columns_kernel,
        out_shape=jax.ShapeDtypeStruct((ens, 2 * COLS_DEV), f32),
        in_specs=[vmem] * 2,
        out_specs=vmem,
        compiler_params=params(),
        cost_estimate=pl.CostEstimate(
            flops=2 * 256 * own * 2048, bytes_accessed=4 << 20, transcendentals=0
        ),
        name="innov_columns",
    )(innov, info)


def columns_call(info, rank, imga, imgb):
    ens, half = imga.shape
    return pl.pallas_call(
        columns_kernel,
        out_shape=(
            jax.ShapeDtypeStruct((ens, 2 * half), f32),
            jax.ShapeDtypeStruct((ens, 2 * COLS_DEV), f32),
        ),
        in_specs=[vmem] * 4,
        out_specs=(vmem, vmem),
        compiler_params=params(),
        cost_estimate=pl.CostEstimate(
            flops=2 * 256 * 2 * half * 3072, bytes_accessed=4 << 20, transcendentals=0
        ),
        name="columns",
    )(info, rank, imga, imgb)


def final_kernel(coef_ref, innov_ref, info_ref, back_ref, rc_ref, rin_ref, ic_ref, iin_ref, w_ref, inc_ref):
    coef = coef_ref[...]
    ens = coef.shape[0]
    own = innov_ref.shape[1]
    chunk = 1024
    first, second = coef[:, :ens], coef[:, ens:]
    for c in range(own // chunk):
        at = pl.ds(c * chunk, chunk)
        live = info_ref[1:2, at]
        w_ref[:, at] = combine(first, innov_ref[:, at] * live) + combine(second, back_ref[:, at])
    inc_ref[...] = combine(first, rc_ref[:, :COLS_DEV] + rin_ref[...]) + combine(
        second, ic_ref[:, :COLS_DEV] + iin_ref[...]
    )


def final_call(coef, innov, info, back, *cols):
    ens, own = innov.shape
    return pl.pallas_call(
        final_kernel,
        out_shape=(
            jax.ShapeDtypeStruct((ens, own), f32),
            jax.ShapeDtypeStruct((ens, COLS_DEV), f32),
        ),
        in_specs=[vmem] * 8,
        out_specs=(vmem, vmem),
        compiler_params=params(),
        name="final",
    )(coef, innov, info, back, *cols)


def block_bounds(key_ext, flags_ext, regions):
    wide = regions + 2 * REACH
    jkeys = key_ext.reshape(wide, ROWS // KB, KB)
    jmin = jkeys.min(axis=2)
    jmax = jnp.where(jkeys < 0.5 * DEAD, jkeys, -DEAD).max(axis=2)
    ikeys = key_ext.reshape(wide, ROWS // NB, NB)[REACH : REACH + regions]
    imin = ikeys.min(axis=2)
    imax = jnp.where(ikeys < 0.5 * DEAD, ikeys, -DEAD).max(axis=2)
    los, his = [], []
    ids = jnp.arange(ROWS // KB, dtype=jnp.int32)[None, None, :]
    for dh in range(2 * REACH + 1):
        lo_j = jmin[dh : dh + regions]
        hi_j = jmax[dh : dh + regions]
        d = dh - REACH
        if d == 0:
            flag = jnp.ones((regions,), jnp.bool_)
        elif d > 0:
            flag = flags_ext[d - 1, REACH : REACH + regions] > 0.5
        else:
            flag = flags_ext[-d - 1, REACH + d : REACH + d + regions] > 0.5
        near = (
            (hi_j[:, None, :] >= imin[:, :, None] - 1.001)
            & (lo_j[:, None, :] <= imax[:, :, None] + 1.001)
            & (imin[:, :, None] < 0.5 * DEAD)
            & flag[:, None, None]
        )
        los.append(jnp.where(near, ids, ROWS // KB).min(axis=2).reshape(-1))
        his.append(jnp.where(near, ids + 1, 0).max(axis=2).reshape(-1))
    return jnp.stack([jnp.concatenate(los), jnp.concatenate(his)])


def on_device(
    innovation,
    obs_along,
    obs_across,
    obs_scale,
    obs_error,
    obs_gain,
    pair_live,
    obs_count,
    col_owner,
):
    axes = ("reg", "col")
    regions = obs_count.shape[0]
    ens, own = innovation.shape
    live = (
        (jnp.arange(ROWS, dtype=jnp.int32)[None, :] < obs_count[:, None])
        .astype(f32)
        .reshape(own)
    )
    flags = jnp.repeat(pair_live.astype(f32).T, ROWS, axis=1)
    zero = jnp.zeros((own,), f32)
    meta = jnp.stack(
        [obs_along, obs_across, obs_scale * live, obs_error, flags[0], flags[1]]
        + [jnp.where(live > 0.5, obs_across, DEAD)]
        + [zero] * (META - 7)
    )
    total_cols = COLS_DEV * lax.axis_size(axes)
    local_col = (col_owner - lax.axis_index(axes) * COLS_DEV) % total_cols
    info = jnp.stack([obs_gain, live, local_col.astype(f32)] + [zero] * 5)

    first, last, rank, own_meta = sort_call(innovation, meta)
    after = shift(first, -1)
    before = shift(last, 1)
    chunks = [before, first, last, after]
    innov_cols = innov_columns_call(innovation, info)
    innov_came = shift(innov_cols[:, COLS_DEV:], 1)
    metas = [before[ens:], own_meta, after[ens:]]
    keys = jnp.concatenate([m[6] for m in metas])
    flags_ext = jnp.concatenate([m[4:6, ::ROWS] for m in metas], axis=1)
    bounds = block_bounds(keys, flags_ext, regions)

    imga, imgb, grams, *lists = first_call(bounds, chunks, ens, own)
    img_after = shift(imga, -1)
    img_before = shift(imgb, 1)
    step0, inv0, curv0 = solve_first(sum_all(grams, 0))
    back, img_cols = columns_call(info, rank, imga, imgb)
    img_came = shift(img_cols[:, COLS_DEV:], 1)
    grams = second_call(lists, step0, chunks, [img_before, imga, imgb, img_after], ens, own)
    coef = solve_second(sum_all(grams, 1), step0, inv0, curv0)
    return tuple(
        final_call(coef, innovation, info, back, innov_cols, innov_came, img_cols, img_came)
    )


def solution(mesh):
    one = P(("reg", "col"))
    in_specs = (P(None, ("reg", "col")), one, one, one, one, one, P(("reg", "col"), None), one, one)
    out_specs = (P(None, ("reg", "col")), P(None, ("reg", "col")))
    return jax.shard_map(
        on_device, mesh=mesh, in_specs=in_specs, out_specs=out_specs, check_vma=False
    )
```

profile of v0, /device:TPU:0, one launch (start us, length us, event | category | flops | bytes accessed | tf_op | source)
XLA Modules:
  0.0 157.3 jit_solution(17325346918918851862)
XLA Ops:
  0.6 0.7 convert_bitcast_fusion
  1.4 0.1 broadcast_bitcast_fusion
  1.5 0.0 copy-start.6
  1.5 0.0 copy-start.7
  1.6 0.7 copy-done.6
  2.2 0.0 copy-done.7
  2.3 0.0 copy-start.8
  2.3 0.0 copy-start.9
  2.3 0.7 copy-done.8
  3.0 0.0 copy-done.9
  3.0 1.5 stack.48.meta_ref
  4.5 6.7 %sort_slots.1 = (f32[72,2048]{1,0:T(8,128)}, f32[72,2048]{1,0:T(8,128)}, f32[8,4096]{1,0:T(8,128)}, f32[8,4096]{1,0:T(8,128)}) custom-call(f32[64,4096]{1,0:T(8,128)} %innov_ref.5, f32[16,4096]{1,0:T(8,128)} %stack.48.meta_ref), custom_call_target="tpu_custom_call" | custom-call | tf_op jit(solution)/shard_map/sort_slots/pallas_call | solution.py:100
  11.2 6.4 %collective-permute-start.1 = (f32[72,2048]{1,0:T(8,128)}, f32[72,2048]{1,0:T(8,128)S(1)}, u32[]{:S(2)}, u32[]{:S(2)}) collective-permute-start(f32[72,2048]{1,0:T(8,128)} %get-tuple-element.19.c1), channel_id=1, source_target_pairs={{1,0},{2,1},{3,2},{4,3},{5,4},{6,5},{7,6},{8,7},{9,8},{10,9},{11,1... | collective-permute-start | bytes 1769480 | tf_op jit(solution)/shard_map/ppermute | solution.py:33
  17.6 0.0 collective-permute-start
  17.7 0.7 copy-done.11
  18.4 0.0 copy-start.10
  18.4 0.7 copy-done.10
  19.1 0.8 stack.55.info_ref
  19.9 8.1 %innov_columns.1.rc_ref = f32[64,2048]{1,0:T(8,128)} custom-call(f32[64,4096]{1,0:T(8,128)} %innov_ref.5, f32[8,4096]{1,0:T(8,128)} %stack.55.info_ref), custom_call_target="tpu_custom_call" | custom-call | flops 4294967296 | bytes 4194304 | tf_op jit(solution)/shard_map/innov_columns/pallas_call | solution.py:539
  27.9 1.0 slice.120
  28.9 0.1 collective-permute-start.4
  29.0 0.9 slice.95
  29.9 1.0 slice.102
  30.9 0.1 fusion.7
  31.0 0.0 collective-permute-done.1.c3
  31.1 0.0 collective-permute-done.c0
  31.1 0.1 fusion
  31.2 0.1 slice.101
  31.3 0.1 pad_maximum_fusion
  31.4 0.1 compare_bitcast_fusion.2
  31.5 0.1 and_and_fusion
  31.6 0.8 select_reduce_fusion.5
  32.4 0.1 reshape.144
  32.5 0.1 reshape.145
  32.5 0.1 reshape.146
  32.6 0.1 reshape.147
  32.7 0.1 reshape.148
  32.8 0.1 reshape.139
  32.9 0.1 reshape.140
  33.0 0.1 reshape.141
  33.0 0.1 reshape.142
  33.1 0.1 reshape.143
  33.2 0.1 concatenate.17
  33.3 0.1 concatenate.16
  33.4 0.6 pad_add_fusion.bounds_ref
  34.0 21.9 %operate_first.1 = (f32[64,2048]{1,0:T(8,128)}, f32[64,2048]{1,0:T(8,128)}, f32[64,128]{1,0:T(8,128)}, s32[1288]{0:T(1024)}, s32[322]{0:T(512)}, /*index=5*/s32[1]{0:T(128)}) custom-call(s32[2,160]{1,0:T(2,128)} %pad_add_fusion.bounds_ref, f32[72,2048]{1,0:T(8,128)} %copy-done, f32[72,2048]{1,0:T(8,128)} %get-tuple-element.19.c1, ...), custom_call_target="tpu_custom_call" | custom-call | tf_op jit(solution)/shard_map/operate_first/pallas_call | solution.py:315
  55.9 10.0 %collective-permute-start.2 = (f32[64,2048]{1,0:T(8,128)}, f32[64,2048]{1,0:T(8,128)S(1)}, u32[]{:S(2)}, u32[]{:S(2)}) collective-permute-start(f32[64,2048]{1,0:T(8,128)} %get-tuple-element.25.i2.imgb_ref), channel_id=1, source_target_pairs={{31,0},{0,1},{1,2},{2,3},{3,4},{4,5},{5,6},{6,7},{7,8},{8,9},{9,10... | collective-permute-start | bytes 1572872 | tf_op jit(solution)/shard_map/ppermute | solution.py:33
  65.9 0.0 collective-permute-start.3
  65.9 9.0 %columns.1 = (f32[64,4096]{1,0:T(8,128)}, f32[64,2048]{1,0:T(8,128)}) custom-call(f32[8,4096]{1,0:T(8,128)} %stack.55.info_ref, f32[8,4096]{1,0:T(8,128)} %get-tuple-element.29.rank_ref, f32[64,2048]{1,0:T(8,128)} %get-tuple-element.26.i1.imga_ref, f32[64,2048]{1,0:T(8,128)} %get-tuple-element.25.i2.imgb_ref), custom_call_target="tpu_custom_call" | custom-call | flops 6442450944 | bytes 4194304 | tf_op jit(solution)/shard_map/columns/pallas_call | solution.py:554
  74.9 1.0 slice.116
  75.9 0.6 collective-permute-start.5
  76.4 13.6 %sum_all.2.gram_ref = f32[64,128]{1,0:T(8,128)} custom-call(f32[64,128]{1,0:T(8,128)} %get-tuple-element.23.x_ref), custom_call_target="tpu_custom_call" | custom-call | tf_op jit(solution)/shard_map/sum_all/pallas_call | solution.py:404
  90.1 7.2 %solve_first.1 = (f32[64,64]{1,0:T(8,128)}, f32[64,64]{1,0:T(8,128)}, f32[64,64]{1,0:T(8,128)}) custom-call(f32[64,128]{1,0:T(8,128)} %sum_all.2.gram_ref), custom_call_target="tpu_custom_call" | custom-call | tf_op jit(solution)/shard_map/solve_first/pallas_call | solution.py:473
  97.3 0.0 collective-permute-done.2.i0
  97.3 0.8 copy-done.2
  98.1 0.2 copy-done.3
  98.3 20.8 %operate_second.1.x_ref = f32[128,128]{1,0:T(8,128)} custom-call(s32[1288]{0:T(1024)} %get-tuple-element.20.list_ref, s32[322]{0:T(512)} %get-tuple-element.21.tile_ref, s32[1]{0:T(128)} %get-tuple-element.22.count_ref, f32[64,64]{1,0:T(8,128)} %get-tuple-element.24.step_ref, f32[72,2048]{1,0:T(8,128)} %copy-done, f32[72,2048]{1,0:T(8,128)} %get-tuple-element.19.c1, ...), custom_call_target="tpu_custom_call" | custom-call | tf_op jit(solution)/shard_map/operate_second/pallas_call | solution.py:334
  119.1 25.3 %sum_all.3.gram_ref = f32[128,128]{1,0:T(8,128)} custom-call(f32[128,128]{1,0:T(8,128)} %operate_second.1.x_ref), custom_call_target="tpu_custom_call" | custom-call | tf_op jit(solution)/shard_map/sum_all/pallas_call | solution.py:404
  144.3 8.2 %solve_second.1.coef_ref = f32[64,128]{1,0:T(8,128)} custom-call(f32[128,128]{1,0:T(8,128)} %sum_all.3.gram_ref, f32[64,64]{1,0:T(8,128)} %get-tuple-element.24.step_ref, f32[64,64]{1,0:T(8,128)} %get-tuple-element.27.inv_ref, f32[64,64]{1,0:T(8,128)} %get-tuple-element.28.curv_ref), custom_call_target="tpu_custom_call" | custom-call | tf_op jit(solution)/shard_map/solve_second/pallas_call | solution.py:484
  152.6 0.0 collective-permute-done.4.rin_ref
  152.6 0.0 collective-permute-done.5.iin_ref
  152.6 0.7 copy-done.4
  153.3 0.1 copy-done.5
  153.4 3.9 %final.1 = (f32[64,4096]{1,0:T(8,128)}, f32[64,1024]{1,0:T(8,128)}) custom-call(f32[64,128]{1,0:T(8,128)} %solve_second.1.coef_ref, f32[64,4096]{1,0:T(8,128)} %innov_ref.5, f32[8,4096]{1,0:T(8,128)} %stack.55.info_ref, f32[64,4096]{1,0:T(8,128)} %get-tuple-element.30.back_ref, f32[64,2048]{1,0:T(8,128)} %innov_columns.1.rc_ref, f32[64,1024]{1,0:T(8,128)} %copy-done.4, ...), custom_call_target="tpu_custom_call" | custom-call | tf_op jit(solution)/shard_map/final/pallas_call | solution.py:587
  (32 shorter events, 0.2 us)
Async XLA Ops:
  0.6 0.8 copy-start.12
  1.5 0.7 copy-start.6
  1.5 0.7 copy-start.7
  2.3 0.7 copy-start.8
  2.3 0.7 copy-start.9
  11.2 19.8 %collective-permute-start.1 = (f32[72,2048]{1,0:T(8,128)}, f32[72,2048]{1,0:T(8,128)S(1)}, u32[]{:S(2)}, u32[]{:S(2)}) collective-permute-start(f32[72,2048]{1,0:T(8,128)} %get-tuple-element.19.c1), channel_id=1, source_target_pairs={{1,0},{2,1},{3,2},{4,3},{5,4},{6,5},{7,6},{8,7},{9,8},{10,9},{11,1... | collective-permute-start | bytes 1769480 | tf_op jit(solution)/shard_map/ppermute | solution.py:33
  17.6 13.4 %collective-permute-start = (f32[72,2048]{1,0:T(8,128)}, f32[72,2048]{1,0:T(8,128)S(1)}, u32[]{:S(2)}, u32[]{:S(2)}) collective-permute-start(f32[72,2048]{1,0:T(8,128)} %get-tuple-element.17.c2), channel_id=1, source_target_pairs={{31,0},{0,1},{1,2},{2,3},{3,4},{4,5},{5,6},{6,7},{7,8},{8,9},{9,10... | collective-permute-start | bytes 1769480 | tf_op jit(solution)/shard_map/ppermute | solution.py:33
  17.6 0.7 copy-start.11
  18.4 0.7 copy-start.10
  28.9 123.7 %collective-permute-start.4 = (f32[64,1024]{1,0:T(8,128)S(1)}, f32[64,1024]{1,0:T(8,128)S(1)}, u32[]{:S(2)}, u32[]{:S(2)}) collective-permute-start(f32[64,1024]{1,0:T(8,128)S(1)} %slice.120), channel_id=1, source_target_pairs={{31,0},{0,1},{1,2},{2,3},{3,4},{4,5},{5,6},{6,7},{7,8},{8,9},{9,10... | collective-permute-start | bytes 786440 | tf_op jit(solution)/shard_map/ppermute | solution.py:33
  31.0 2.9 %copy-start.1 = (f32[72,2048]{1,0:T(8,128)}, f32[72,2048]{1,0:T(8,128)S(1)}, u32[]{:S(2)}) copy-start(f32[72,2048]{1,0:T(8,128)S(1)} %collective-permute-done.1.c3) | copy-start | bytes 1769476
  31.1 2.9 %copy-start = (f32[72,2048]{1,0:T(8,128)}, f32[72,2048]{1,0:T(8,128)S(1)}, u32[]{:S(2)}) copy-start(f32[72,2048]{1,0:T(8,128)S(1)} %collective-permute-done.c0) | copy-start | bytes 1769476
  55.9 41.4 %collective-permute-start.2 = (f32[64,2048]{1,0:T(8,128)}, f32[64,2048]{1,0:T(8,128)S(1)}, u32[]{:S(2)}, u32[]{:S(2)}) collective-permute-start(f32[64,2048]{1,0:T(8,128)} %get-tuple-element.25.i2.imgb_ref), channel_id=1, source_target_pairs={{31,0},{0,1},{1,2},{2,3},{3,4},{4,5},{5,6},{6,7},{7,8},{8,9},{9,10... | collective-permute-start | bytes 1572872 | tf_op jit(solution)/shard_map/ppermute | solution.py:33
  65.9 31.4 %collective-permute-start.3 = (f32[64,2048]{1,0:T(8,128)}, f32[64,2048]{1,0:T(8,128)S(1)}, u32[]{:S(2)}, u32[]{:S(2)}) collective-permute-start(f32[64,2048]{1,0:T(8,128)} %get-tuple-element.26.i1.imga_ref), channel_id=1, source_target_pairs={{1,0},{2,1},{3,2},{4,3},{5,4},{6,5},{7,6},{8,7},{9,8},{10,9},{11,1... | collective-permute-start | bytes 1572872 | tf_op jit(solution)/shard_map/ppermute | solution.py:33
  75.9 76.7 %collective-permute-start.5 = (f32[64,1024]{1,0:T(8,128)S(1)}, f32[64,1024]{1,0:T(8,128)S(1)}, u32[]{:S(2)}, u32[]{:S(2)}) collective-permute-start(f32[64,1024]{1,0:T(8,128)S(1)} %slice.116), channel_id=1, source_target_pairs={{31,0},{0,1},{1,2},{2,3},{3,4},{4,5},{5,6},{6,7},{7,8},{8,9},{9,10... | collective-permute-start | bytes 786440 | tf_op jit(solution)/shard_map/ppermute | solution.py:33
  97.3 0.8 copy-start.2
  97.3 1.0 copy-start.3
  152.6 0.7 copy-start.4
  152.6 0.8 copy-start.5
where the time goes:
time: 158 us; the launch traced here: 157 us
  Pallas kernels  125 us (79%)
  starting transfers between devices  17 us (11%)
  local copies, waits for them, and re-layouts  12 us (8%)
  other arithmetic  2.61 us (2%)
    pallas_call x2, Pallas kernels, sum_all(): pl.pallas_call(functools.partial(reduce_kernel, steps, n_col), out_shape=...  38.9 us
    pallas_call x1, Pallas kernels, first_call(): pl.pallas_call(first_kernel, out_shape=(half, half, jax.ShapeDtypeStruct(...  21.9 us
    pallas_call x1, Pallas kernels, second_call(): pl.pallas_call(second_kernel, out_shape=jax.ShapeDtypeStruct((2 * ens, 2...  20.8 us
    ppermute x6, starting transfers between devices, shift(): lax.ppermute(block, axis, [((i - distance) % n, i) for i in range(n)])  17 us
    pallas_call x1, Pallas kernels, columns_call(): pl.pallas_call(columns_kernel, out_shape=(jax.ShapeDtypeStruct((ens, 2 *...  9.04 us
    pallas_call x1, Pallas kernels, solve_second(): pl.pallas_call(solve_second_kernel, out_shape=jax.ShapeDtypeStruct((ens,...  8.24 us
    pallas_call x1, Pallas kernels, innov_columns_call(): pl.pallas_call(innov_columns_kernel, out_shape=jax.ShapeDtypeStruct((ens,...  8.06 us
    pallas_call x1, Pallas kernels, solve_first(): pl.pallas_call(solve_first_kernel, out_shape=(small, small, small), in_sp...  7.2 us
  transfers between devices with their start and end apart: 6, of which 0 were waited for; matrix products, arithmetic and copies ran while one was open for 5% of the time, Pallas kernels for 73%

commit v1 on v0

--- a/solution.py
+++ b/solution.py
@@ -11,10 +11,12 @@
 REACH = 2
 COLS_DEV = 1024
 META = 16
-KB = 128
-NB = 128
-UNROLL = 4
+TILE = 32
+STEP = 16
+PAIR = 4
+EMPTY = ROWS // STEP
 DEAD = 1e9
+FAR = 1e6
 VMEM_LIMIT = 60 * 1024 * 1024
 
 highest = lax.Precision.HIGHEST
@@ -61,7 +63,7 @@
     return pltpu.CompilerParams(vmem_limit_bytes=VMEM_LIMIT)
 
 
-def sort_kernel(innov_ref, meta_ref, first_ref, last_ref, rank_ref, own_ref):
+def sort_kernel(innov_ref, meta_ref, first_ref, last_ref, rank_ref):
     regions = innov_ref.shape[1] // ROWS
     kept = first_ref.shape[0]
     sub = lax.broadcasted_iota(jnp.int32, (ROWS, 128), 0)
@@ -91,7 +93,6 @@
             start = (g % (regions // 2)) * ROWS + c * 256
             got = (got[:n] + got[n : 2 * n] + got[2 * n :])[:kept]
             out_ref[:, start : start + 256] = got
-            own_ref[:, g * ROWS + c * 256 : g * ROWS + (c + 1) * 256] = got[kept - 8 :]
 
 
 def sort_call(innov, meta):
@@ -99,117 +100,209 @@
     half = jax.ShapeDtypeStruct((ens + 8, n // 2), f32)
     return pl.pallas_call(
         sort_kernel,
-        out_shape=(half, half) + (jax.ShapeDtypeStruct((8, n), f32),) * 2,
+        out_shape=(half, half, jax.ShapeDtypeStruct((8, n), f32)),
         in_specs=[vmem, vmem],
-        out_specs=(vmem,) * 4,
+        out_specs=(vmem,) * 3,
         compiler_params=params(),
         name="sort_slots",
     )(innov, meta)
 
 
-def build_list(bounds_ref, list_ref, tile_ref, count_ref, tiles):
-    per = ROWS // NB
-    zero_block = (tiles // per + 2 * REACH) * (ROWS // KB)
-
-    def one(t, trip):
-        g = t // per
-        base = trip * UNROLL
-
-        def put(dh, jb, n):
-            list_ref[n] = (g + dh) * (ROWS // KB) + jb
-            return n + 1
-
-        n = base
-        for dh in range(2 * REACH + 1):
-            lo = bounds_ref[0, dh * tiles + t]
-            hi = bounds_ref[1, dh * tiles + t]
-            n = lax.fori_loop(lo, hi, functools.partial(put, dh), n)
-        for p in range(UNROLL):
-            list_ref[n + p] = zero_block
-        end = (n + UNROLL - 1) // UNROLL
-
-        def mark(k, carry):
-            tile_ref[k] = t
-            return carry
-
-        lax.fori_loop(trip, end, mark, 0)
-        return end
-
-    trips = lax.fori_loop(0, tiles, one, 0)
-    tile_ref[trips] = 0
-    for p in range(UNROLL):
-        list_ref[trips * UNROLL + p] = zero_block
-    count_ref[0] = trips
-
-
-def prepare(chunks, row_ref, along_ref, across_ref):
+def lay_grid(chunks, row_ref, grid_ref):
     width = chunks[0].shape[1]
     per = width // ROWS
+    blocks = ROWS // 128
+    grid_ref[...] = jnp.full(grid_ref.shape, FAR, f32)
     for c, ref in enumerate(chunks):
         row_ref[:, c * width : (c + 1) * width] = ref[ref.shape[0] - 8 :, :]
         for r in range(per):
             h = c * per + r
             at = slice(h * ROWS, (h + 1) * ROWS)
             row_ref[0:1, at] = row_ref[0:1, at] + float(h)
-            col = row_ref[:, at].T
-            along_ref[at, :] = jnp.broadcast_to(col[:, 0:1], (ROWS, NB))
-            across_ref[at, :] = jnp.broadcast_to(col[:, 1:2], (ROWS, NB))
-    wide = width * len(chunks)
-    along_ref[wide : wide + KB, :] = jnp.zeros((KB, NB), f32)
-    across_ref[wide : wide + KB, :] = jnp.zeros((KB, NB), f32)
-
-
-def apply_cov(list_ref, tile_ref, count_ref, row_ref, along_ref, across_ref, v_ref, img_ref, stack_ref, s_ref):
+            for q, source in enumerate((0, 1, 6)):
+                for b in range(blocks):
+                    line = h * (blocks + 1) + b
+                    begin = h * ROWS + b * 128
+                    grid_ref[q, line : line + 1, :] = row_ref[source : source + 1, begin : begin + 128]
+
+
+def lay_tables(grid_ref, table_refs, spread_refs):
+    own = spread_refs[0].shape[0]
+    blocks = ROWS // 128
+    count = (own // ROWS + 2 * REACH) * (blocks + 1)
+    ways = 128 // STEP
+    lane = lax.broadcasted_iota(jnp.int32, (count, 128), 1)
+    for q in range(2):
+        here = grid_ref[q, :count, :]
+        later = grid_ref[q, 1 : count + 1, :]
+        table_refs[q][pl.ds(0, count, stride=ways), :] = here
+        for k in range(1, ways):
+            joined = jnp.where(lane < k * STEP, later, here)
+            table_refs[q][pl.ds(k, count, stride=ways), :] = pltpu.roll(joined, 128 - k * STEP, 1)
+        turned = jnp.concatenate([here, jnp.zeros((128 - count, 128), f32)], axis=0).T
+        for g in range(own // ROWS):
+            for b in range(blocks):
+                line = (g + REACH) * (blocks + 1) + b
+                begin = g * ROWS + b * 128
+                spread_refs[q][begin : begin + 128, :] = jnp.broadcast_to(
+                    turned[:, line : line + 1], (128, 128)
+                )
+
+
+def plan_windows(row_ref, grid_ref, span_ref, item_ref):
+    blocks = ROWS // 128
+    regions = row_ref.shape[1] // ROWS - 2 * REACH
+    per = ROWS // TILE
+    tiles = regions * per
+    ways = 128 // STEP
+    offsets = 2 * REACH + 1
+    keys = [
+        grid_ref[2, h * (blocks + 1) : h * (blocks + 1) + blocks, :] for h in range(regions + 2 * REACH)
+    ]
+    mine = jnp.concatenate(keys[REACH : REACH + regions], axis=0)
+    top = jnp.where(mine < 0.5 * DEAD, mine, -DEAD)
+    size = 1
+    while size < TILE:
+        top = jnp.maximum(top, pltpu.roll(top, 128 - size, 1))
+        size *= 2
+    parts = 128 // TILE
+    lines = regions * blocks
+    tile = lax.broadcasted_iota(jnp.int32, (lines, tiles), 1)
+    line = lax.broadcasted_iota(jnp.int32, (lines, tiles), 0)
+    first = jnp.zeros((1, tiles), f32)
+    last = jnp.zeros((1, tiles), f32)
+    for p in range(parts):
+        here = tile == line * parts + p
+        lane = slice(p * TILE, p * TILE + 1)
+        first = first + jnp.sum(
+            jnp.where(here, jnp.broadcast_to(mine[:, lane], (lines, tiles)), 0.0), axis=0, keepdims=True
+        )
+        last = last + jnp.sum(
+            jnp.where(here, jnp.broadcast_to(top[:, lane], (lines, tiles)), 0.0), axis=0, keepdims=True
+        )
+    under, over = first - 1.001, last + 1.001
+    begins, ends = [], []
+    for key in keys:
+        begin = jnp.zeros((blocks, tiles), f32)
+        end = jnp.zeros((blocks, tiles), f32)
+        for k in range(ways):
+            low = jnp.broadcast_to(key[:, k * STEP : k * STEP + 1], (blocks, tiles))
+            high = jnp.broadcast_to(key[:, (k + 1) * STEP - 1 : (k + 1) * STEP], (blocks, tiles))
+            begin = begin + jnp.where(high < under, 1.0, 0.0)
+            end = end + jnp.where(low <= over, 1.0, 0.0)
+        begins.append(jnp.sum(begin, axis=0, keepdims=True))
+        ends.append(jnp.sum(end, axis=0, keepdims=True))
+    group = lax.broadcasted_iota(jnp.int32, (1, tiles), 1) // per
+    alive = first < 0.5 * DEAD
+    starts, stops = [], []
+    needs = jnp.zeros((1, tiles), f32)
+    for dh in range(offsets):
+        d = dh - REACH
+        start = jnp.zeros((1, tiles), f32)
+        stop = jnp.zeros((1, tiles), f32)
+        for g in range(regions):
+            h = g + dh
+            base = float(h * (ROWS + 128) // STEP)
+            begin, end = begins[h] + base, ends[h] + base
+            if d:
+                source = 3 + abs(d)
+                owner = (g + REACH if d > 0 else h) * ROWS
+                flag = row_ref[source : source + 1, owner : owner + 128]
+                end = jnp.where(flag[:, :tiles] > 0.5, end, begin)
+            start = jnp.where(group == g, begin, start)
+            stop = jnp.where(group == g, end, stop)
+        stop = jnp.where(alive, jnp.maximum(stop, start), start)
+        needs = jnp.maximum(needs, jnp.floor((stop - start + (ways - 1.0)) * (1.0 / ways)))
+        starts.append(start)
+        stops.append(stop)
+    blank = jnp.full((8 - offsets, tiles), float(EMPTY), f32)
+    for m in range(blocks + 1):
+        lines_m = [
+            jnp.where(start + float(ways * m) < stop, start + float(ways * m), float(EMPTY))
+            for start, stop in zip(starts, stops)
+        ]
+        span_ref[8 * m : 8 * m + 8, :] = jnp.concatenate(lines_m + [blank], axis=0).astype(jnp.int32)
+    row = lax.broadcasted_iota(jnp.int32, (tiles, tiles), 0)
+    col = lax.broadcasted_iota(jnp.int32, (tiles, tiles), 1)
+    many = jnp.broadcast_to(needs, (tiles, tiles)).astype(bf16)
+    done = dot((col <= row).astype(f32).astype(bf16), many, NT)
+    each = dot((col == row).astype(f32).astype(bf16), many, NT)
+    total = jnp.max(done, axis=0, keepdims=True)
+    for k in range(item_ref.shape[1]):
+        slot = lax.broadcasted_iota(jnp.int32, (1, tiles), 1).astype(f32) + float(k * tiles)
+        past = done <= slot
+        at = jnp.sum(jnp.where(past, 1.0, 0.0), axis=0, keepdims=True)
+        began = jnp.sum(jnp.where(past, each, 0.0), axis=0, keepdims=True)
+        spare = slot >= total
+        item_ref[0, k : k + 1, :] = jnp.where(spare, 0.0, at).astype(jnp.int32)
+        item_ref[1, k : k + 1, :] = jnp.where(spare, float(blocks), slot - began).astype(jnp.int32)
+        item_ref[2, k : k + 1, :] = total.astype(jnp.int32)
+
+
+def turn_vectors(v_ref, row_ref, turn_ref):
+    ens, wide = v_ref.shape
+    padded = ROWS + 128
+    row = lax.broadcasted_iota(jnp.int32, (256, 256), 0)
+    eye = (row == lax.broadcasted_iota(jnp.int32, (256, 256), 1)).astype(f32).astype(bf16)
+    for h in range(wide // ROWS):
+        for b in range(ROWS // 256):
+            at = slice(h * ROWS + b * 256, h * ROWS + (b + 1) * 256)
+            stack = jnp.concatenate(two(v_ref[:, at] * row_ref[2:3, at]), axis=0)
+            begin = h * padded + b * 256
+            turn_ref[begin : begin + 256, :] = dot(eye, stack, NT).astype(bf16)
+        turn_ref[h * padded + ROWS : (h + 1) * padded, :] = jnp.zeros((128, 2 * ens), bf16)
+
+
+def apply_cov(
+    span_ref, item_ref, row_ref, table_refs, spread_refs, v_ref, img_ref, turn_ref, sum_ref, s_ref
+):
     ens, wide = v_ref.shape
     own = img_ref.shape[1]
     lead = REACH * ROWS
-    chunk = 2048
-    for c in range(wide // chunk):
-        at = pl.ds(c * chunk, chunk)
-        hi, lo = two(v_ref[:, at] * row_ref[2:3, at])
-        stack_ref[0:ens, at] = hi
-        stack_ref[ens : 2 * ens, at] = lo
-    stack_ref[:, wide : wide + KB] = jnp.zeros((2 * ens, KB), bf16)
     s_ref[...] = jnp.zeros_like(s_ref)
-    img_ref[...] = jnp.zeros_like(img_ref)
-    depth = UNROLL * KB
+    sum_ref[...] = jnp.zeros_like(sum_ref)
+
+    def windows(n):
+        line, lane = lax.shift_right_logical(n, jnp.int32(7)), lax.bitwise_and(n, jnp.int32(127))
+        tile = item_ref[0, line, lane]
+        level = item_ref[1, line, lane] * 8
+        return [tile] + [span_ref[level + dh, tile] for dh in range(2 * REACH + 1)]
 
     def step(k, carry):
-        before = jnp.maximum(k - 1, 0)
-        vhi, vlo = [], []
-        for p in range(UNROLL):
-            block = list_ref[before * UNROLL + p]
-            part = stack_ref[:, pl.ds(pl.multiple_of(block * KB, KB), KB)]
-            vhi.append(part[:ens])
-            vlo.append(part[ens:])
-        lhs = jnp.concatenate(vhi + vlo + vhi, axis=1)
-        shi = s_ref[:depth]
-        rhs = jnp.concatenate([shi, shi, s_ref[depth:]], axis=0)
-        o_at = pl.ds(pl.multiple_of(tile_ref[before] * NB, NB), NB)
-        img_ref[:, o_at] += dot(lhs, rhs)
-        i_at = pl.ds(pl.multiple_of(lead + tile_ref[k] * NB, NB), NB)
-        a_i = row_ref[0:1, i_at]
-        b_i = row_ref[1:2, i_at]
-        for p in range(UNROLL):
-            block = list_ref[k * UNROLL + p]
-            j_at = pl.ds(pl.multiple_of(block * KB, KB), KB)
-            da = along_ref[j_at, :] - a_i
-            db = across_ref[j_at, :] - b_i
-            r2 = da * da + db * db
-            r = r2 * lax.rsqrt(jnp.maximum(r2, 1e-30))
-            u = jnp.maximum(1.0 - r, 0.0)
-            u2 = u * u
-            hi, lo = two((u2 * u2) * (r + 0.25))
-            s_ref[p * KB : (p + 1) * KB] = hi
-            s_ref[depth + p * KB : depth + (p + 1) * KB] = lo
-        return carry
-
-    lax.fori_loop(0, count_ref[0] + 1, step, 0)
-    for c in range(own // chunk):
-        at = slice(c * chunk, (c + 1) * chunk)
-        e_at = slice(lead + c * chunk, lead + (c + 1) * chunk)
+        for p in range(PAIR):
+            tile, *found = carry[p]
+            rhs = jnp.concatenate(
+                [turn_ref[pl.ds(pl.multiple_of(w * STEP, STEP), 128), :] for w in found], axis=0
+            )
+            got = dot(s_ref[p], rhs)
+            at = pl.ds(pl.multiple_of(tile * TILE, TILE), TILE)
+            sum_ref[at, :] += got[:TILE] + got[TILE:]
+        now = [windows(k * PAIR + p) for p in range(PAIR)]
+        for p in range(PAIR):
+            tile, *found = now[p]
+            at = pl.ds(pl.multiple_of(tile * TILE, TILE), TILE)
+            a_i = spread_refs[0][at, :]
+            b_i = spread_refs[1][at, :]
+            for d, w in enumerate(found):
+                da = table_refs[0][pl.ds(w, 1), :] - a_i
+                db = table_refs[1][pl.ds(w, 1), :] - b_i
+                r2 = da * da + db * db
+                r = r2 * lax.rsqrt(jnp.maximum(r2, 1e-30))
+                u = jnp.maximum(1.0 - r, 0.0)
+                u2 = u * u
+                hi, lo = two((u2 * u2) * (r + 0.25))
+                s_ref[p, 0:TILE, d * 128 : (d + 1) * 128] = hi
+                s_ref[p, TILE : 2 * TILE, d * 128 : (d + 1) * 128] = lo
+        return now
+
+    trips = lax.shift_right_logical(item_ref[2, 0, 0] + (PAIR - 1), jnp.int32(PAIR.bit_length() - 1))
+    lax.fori_loop(0, trips + 1, step, [windows(p) for p in range(PAIR)])
+    for c in range(own // 128):
+        at = slice(c * 128, (c + 1) * 128)
+        e_at = slice(lead + c * 128, lead + (c + 1) * 128)
+        turned = sum_ref[at, :].T
         img_ref[:, at] = (
-            img_ref[:, at] * (row_ref[2:3, e_at] * 0.25) + row_ref[3:4, e_at] * v_ref[:, e_at]
+            (turned[:ens] + turned[ens:]) * (row_ref[2:3, e_at] * 0.25) + row_ref[3:4, e_at] * v_ref[:, e_at]
         )
 
 
@@ -222,7 +315,6 @@
 
 
 def first_kernel(
-    bounds_ref,
     c0,
     c1,
     c2,
@@ -230,26 +322,42 @@
     imga_ref,
     imgb_ref,
     gram_ref,
-    list_ref,
-    tile_ref,
-    count_ref,
+    span_out,
+    item_out,
+    span_ref,
+    item_ref,
+    plan_sem,
     row_ref,
+    grid_ref,
     along_ref,
     across_ref,
+    along_i_ref,
+    across_i_ref,
     v_ref,
     img_ref,
-    stack_ref,
+    turn_ref,
+    sum_ref,
     s_ref,
 ):
     ens, own = img_ref.shape
     lead = REACH * ROWS
     chunks = [c0, c1, c2, c3]
-    build_list(bounds_ref, list_ref, tile_ref, count_ref, own // NB)
-    prepare(chunks, row_ref, along_ref, across_ref)
+    tables = (along_ref, across_ref)
+    spreads = (along_i_ref, across_i_ref)
+    lay_grid(chunks, row_ref, grid_ref)
+    plan_windows(row_ref, grid_ref, span_out, item_out)
+    span_copy = pltpu.make_async_copy(span_out, span_ref, plan_sem.at[0])
+    item_copy = pltpu.make_async_copy(item_out, item_ref, plan_sem.at[1])
+    span_copy.start()
+    item_copy.start()
+    lay_tables(grid_ref, tables, spreads)
     for c, ref in enumerate(chunks):
         v_ref[:, c * lead : (c + 1) * lead] = ref[:ens, :]
+    turn_vectors(v_ref, row_ref, turn_ref)
+    span_copy.wait()
+    item_copy.wait()
     apply_cov(
-        list_ref, tile_ref, count_ref, row_ref, along_ref, across_ref, v_ref, img_ref, stack_ref, s_ref
+        span_ref, item_ref, row_ref, tables, spreads, v_ref, img_ref, turn_ref, sum_ref, s_ref
     )
     imga_ref[...] = img_ref[:, :lead]
     imgb_ref[...] = img_ref[:, lead:]
@@ -258,9 +366,8 @@
 
 
 def second_kernel(
-    list_ref,
-    tile_ref,
-    count_ref,
+    span_in,
+    item_in,
     step_ref,
     c0,
     c1,
@@ -271,23 +378,40 @@
     i2,
     i3,
     gram_ref,
+    span_ref,
+    item_ref,
+    plan_sem,
     row_ref,
+    grid_ref,
     along_ref,
     across_ref,
+    along_i_ref,
+    across_i_ref,
     v_ref,
     img_ref,
-    stack_ref,
+    turn_ref,
+    sum_ref,
     s_ref,
 ):
     ens, own = img_ref.shape
     lead = REACH * ROWS
     chunks = [c0, c1, c2, c3]
-    prepare(chunks, row_ref, along_ref, across_ref)
+    tables = (along_ref, across_ref)
+    spreads = (along_i_ref, across_i_ref)
+    span_copy = pltpu.make_async_copy(span_in, span_ref, plan_sem.at[0])
+    item_copy = pltpu.make_async_copy(item_in, item_ref, plan_sem.at[1])
+    span_copy.start()
+    item_copy.start()
+    lay_grid(chunks, row_ref, grid_ref)
+    lay_tables(grid_ref, tables, spreads)
     step_t = step_ref[...].T
     for c, (ref, image) in enumerate(zip(chunks, [i0, i1, i2, i3])):
         v_ref[:, c * lead : (c + 1) * lead] = ref[:ens, :] - combine(step_t, image[...])
+    turn_vectors(v_ref, row_ref, turn_ref)
+    span_copy.wait()
+    item_copy.wait()
     apply_cov(
-        list_ref, tile_ref, count_ref, row_ref, along_ref, across_ref, v_ref, img_ref, stack_ref, s_ref
+        span_ref, item_ref, row_ref, tables, spreads, v_ref, img_ref, turn_ref, sum_ref, s_ref
     )
     r = v_ref[:, lead : lead + own]
     gram_ref[:ens] = gram(r, jnp.concatenate([r, img_ref[...]], axis=0))
@@ -295,51 +419,67 @@
     gram_ref[ens:] = jnp.concatenate([mixed, mixed], axis=1)
 
 
+def plan_shapes(own):
+    tiles = own // TILE
+    most = tiles * (ROWS // 128)
+    return (8 * (ROWS // 128 + 1), tiles), (3, most // 128 + 1, 128)
+
+
 def scratch(ens, own):
-    wide = own + 2 * REACH * ROWS
+    regions = own // ROWS + 2 * REACH
+    wide = regions * ROWS
+    lines = -(-(regions * (ROWS // 128 + 1) + 1) // 8) * 8
+    table = pltpu.VMEM((128 // STEP * lines, 128), f32)
+    spread = pltpu.VMEM((own, 128), f32)
+    spans, items = plan_shapes(own)
     return [
+        pltpu.SMEM(spans, jnp.int32),
+        pltpu.SMEM(items, jnp.int32),
+        pltpu.SemaphoreType.DMA((2,)),
         pltpu.VMEM((8, wide), f32),
-        pltpu.VMEM((wide + KB, NB), f32),
-        pltpu.VMEM((wide + KB, NB), f32),
+        pltpu.VMEM((3, lines, 128), f32),
+        table,
+        table,
+        spread,
+        spread,
         pltpu.VMEM((ens, wide), f32),
         pltpu.VMEM((ens, own), f32),
-        pltpu.VMEM((2 * ens, wide + KB), bf16),
-        pltpu.VMEM((2 * UNROLL * KB, NB), bf16),
+        pltpu.VMEM((regions * (ROWS + 128) + 128, 2 * ens), bf16),
+        pltpu.VMEM((own, 128), f32),
+        pltpu.VMEM((PAIR, 2 * TILE, (2 * REACH + 1) * 128), bf16),
     ]
 
 
-def first_call(bounds, chunks, ens, own):
-    tiles = own // NB
-    trips = tiles * -(-(2 * REACH + 1) * (ROWS // KB) // UNROLL) + 2
+def first_call(chunks, ens, own):
     half = jax.ShapeDtypeStruct((ens, own // 2), f32)
+    spans, items = plan_shapes(own)
     return pl.pallas_call(
         first_kernel,
         out_shape=(
             half,
             half,
             jax.ShapeDtypeStruct((ens, 2 * ens), f32),
-            jax.ShapeDtypeStruct((trips * UNROLL,), jnp.int32),
-            jax.ShapeDtypeStruct((trips,), jnp.int32),
-            jax.ShapeDtypeStruct((1,), jnp.int32),
+            jax.ShapeDtypeStruct(spans, jnp.int32),
+            jax.ShapeDtypeStruct(items, jnp.int32),
         ),
-        in_specs=[smem] + [vmem] * 4,
-        out_specs=(vmem, vmem, vmem, smem, smem, smem),
+        in_specs=[vmem] * 4,
+        out_specs=(vmem,) * 5,
         scratch_shapes=scratch(ens, own),
         compiler_params=params(),
         name="operate_first",
-    )(bounds, *chunks)
-
-
-def second_call(lists, step, chunks, images, ens, own):
+    )(*chunks)
+
+
+def second_call(plan, step, chunks, images, ens, own):
     return pl.pallas_call(
         second_kernel,
         out_shape=jax.ShapeDtypeStruct((2 * ens, 2 * ens), f32),
-        in_specs=[smem] * 3 + [vmem] * 9,
+        in_specs=[vmem] * 11,
         out_specs=vmem,
         scratch_shapes=scratch(ens, own),
         compiler_params=params(),
         name="operate_second",
-    )(*lists, step, *chunks, *images)
+    )(*plan, step, *chunks, *images)
 
 
 def flip(me, size):
@@ -597,37 +737,6 @@
     )(coef, innov, info, back, *cols)
 
 
-def block_bounds(key_ext, flags_ext, regions):
-    wide = regions + 2 * REACH
-    jkeys = key_ext.reshape(wide, ROWS // KB, KB)
-    jmin = jkeys.min(axis=2)
-    jmax = jnp.where(jkeys < 0.5 * DEAD, jkeys, -DEAD).max(axis=2)
-    ikeys = key_ext.reshape(wide, ROWS // NB, NB)[REACH : REACH + regions]
-    imin = ikeys.min(axis=2)
-    imax = jnp.where(ikeys < 0.5 * DEAD, ikeys, -DEAD).max(axis=2)
-    los, his = [], []
-    ids = jnp.arange(ROWS // KB, dtype=jnp.int32)[None, None, :]
-    for dh in range(2 * REACH + 1):
-        lo_j = jmin[dh : dh + regions]
-        hi_j = jmax[dh : dh + regions]
-        d = dh - REACH
-        if d == 0:
-            flag = jnp.ones((regions,), jnp.bool_)
-        elif d > 0:
-            flag = flags_ext[d - 1, REACH : REACH + regions] > 0.5
-        else:
-            flag = flags_ext[-d - 1, REACH + d : REACH + d + regions] > 0.5
-        near = (
-            (hi_j[:, None, :] >= imin[:, :, None] - 1.001)
-            & (lo_j[:, None, :] <= imax[:, :, None] + 1.001)
-            & (imin[:, :, None] < 0.5 * DEAD)
-            & flag[:, None, None]
-        )
-        los.append(jnp.where(near, ids, ROWS // KB).min(axis=2).reshape(-1))
-        his.append(jnp.where(near, ids + 1, 0).max(axis=2).reshape(-1))
-    return jnp.stack([jnp.concatenate(los), jnp.concatenate(his)])
-
-
 def on_device(
     innovation,
     obs_along,
@@ -640,7 +749,6 @@
     col_owner,
 ):
     axes = ("reg", "col")
-    regions = obs_count.shape[0]
     ens, own = innovation.shape
     live = (
         (jnp.arange(ROWS, dtype=jnp.int32)[None, :] < obs_count[:, None])
@@ -658,24 +766,19 @@
     local_col = (col_owner - lax.axis_index(axes) * COLS_DEV) % total_cols
     info = jnp.stack([obs_gain, live, local_col.astype(f32)] + [zero] * 5)
 
-    first, last, rank, own_meta = sort_call(innovation, meta)
+    first, last, rank = sort_call(innovation, meta)
     after = shift(first, -1)
     before = shift(last, 1)
     chunks = [before, first, last, after]
     innov_cols = innov_columns_call(innovation, info)
     innov_came = shift(innov_cols[:, COLS_DEV:], 1)
-    metas = [before[ens:], own_meta, after[ens:]]
-    keys = jnp.concatenate([m[6] for m in metas])
-    flags_ext = jnp.concatenate([m[4:6, ::ROWS] for m in metas], axis=1)
-    bounds = block_bounds(keys, flags_ext, regions)
-
-    imga, imgb, grams, *lists = first_call(bounds, chunks, ens, own)
+    imga, imgb, grams, *plan = first_call(chunks, ens, own)
     img_after = shift(imga, -1)
     img_before = shift(imgb, 1)
     step0, inv0, curv0 = solve_first(sum_all(grams, 0))
     back, img_cols = columns_call(info, rank, imga, imgb)
     img_came = shift(img_cols[:, COLS_DEV:], 1)
-    grams = second_call(lists, step0, chunks, [img_before, imga, imgb, img_after], ens, own)
+    grams = second_call(plan, step0, chunks, [img_before, imga, imgb, img_after], ens, own)
     coef = solve_second(sum_all(grams, 1), step0, inv0, curv0)
     return tuple(
         final_call(coef, innovation, info, back, innov_cols, innov_came, img_cols, img_came)

time: 158 us -> 137 us (0.87)
  Pallas kernels: 125 us -> 112 us
  starting transfers between devices: 17 us -> 11.9 us
  other arithmetic: 2.61 us -> 0.76 us
    pallas_call x1, Pallas kernels: 21.9 us -> 16.1 us  [first_call(): pl.pallas_call(first_kernel, out_shape=(half, half, jax.ShapeDtypeStruct(...]
    ppermute x6, starting transfers between devices: 17 us -> 11.9 us  [shift(): lax.ppermute(block, axis, [((i - distance) % n, i) for i in range(n)])]
    pallas_call x1, Pallas kernels: 20.8 us -> 17.1 us  [second_call(): pl.pallas_call(second_kernel, out_shape=jax.ShapeDtypeStruct((2 * ens, 2...]
    pallas_call x2, Pallas kernels: 38.9 us -> 35.3 us  [sum_all(): pl.pallas_call(functools.partial(reduce_kernel, steps, n_col), out_shape=...]
    slice x8 -> x0, local copies, waits for them, and re-layouts: 2.03 us -> none  [the longest x2 1.08 us: on_device(): flags_ext = jnp.concatenate([m[4:6, ::ROWS] for m in metas], axis=1)]
    unnamed x30, local copies, waits for them, and re-layouts: 4.7 us -> 6.33 us
  transfers between devices with their start and end apart: 6 -> 6, of which waited for: 0 -> 0; matrix products, arithmetic and copies ran while one was open for 5% -> 2% of each run, Pallas kernels for 73% -> 74%
where the time goes in v1:
time: 137 us; the launch traced here: 136 us
  Pallas kernels  112 us (82%)
  starting transfers between devices  11.9 us (9%)
  local copies, waits for them, and re-layouts  10.6 us (8%)
    pallas_call x2, Pallas kernels, sum_all(): pl.pallas_call(functools.partial(reduce_kernel, steps, n_col), out_shape=...  35.3 us
    pallas_call x1, Pallas kernels, second_call(): pl.pallas_call(second_kernel, out_shape=jax.ShapeDtypeStruct((2 * ens, 2...  17.1 us
    pallas_call x1, Pallas kernels, first_call(): pl.pallas_call(first_kernel, out_shape=(half, half, jax.ShapeDtypeStruct(...  16.1 us
    ppermute x6, starting transfers between devices, shift(): lax.ppermute(block, axis, [((i - distance) % n, i) for i in range(n)])  11.9 us
    pallas_call x1, Pallas kernels, columns_call(): pl.pallas_call(columns_kernel, out_shape=(jax.ShapeDtypeStruct((ens, 2 *...  9.01 us
    pallas_call x1, Pallas kernels, solve_second(): pl.pallas_call(solve_second_kernel, out_shape=jax.ShapeDtypeStruct((ens,...  8.24 us
    pallas_call x1, Pallas kernels, innov_columns_call(): pl.pallas_call(innov_columns_kernel, out_shape=jax.ShapeDtypeStruct((ens,...  8.04 us
    pallas_call x1, Pallas kernels, solve_first(): pl.pallas_call(solve_first_kernel, out_shape=(small, small, small), in_sp...  7.2 us
  transfers between devices with their start and end apart: 6, of which 0 were waited for; matrix products, arithmetic and copies ran while one was open for 2% of the time, Pallas kernels for 74%

profile of v1, /device:TPU:0, one launch (start us, length us, event | category | flops | bytes accessed | tf_op | source)
XLA Modules:
  0.0 135.7 jit_solution(17201908173675974470)
XLA Ops:
  0.6 0.0 copy-start.12
  0.6 0.7 convert_bitcast_fusion
  1.4 0.0 copy-done.12
  1.4 0.1 broadcast_bitcast_fusion
  1.5 0.0 copy-start.6
  1.5 0.0 copy-start.7
  1.6 0.7 copy-done.6
  2.2 0.0 copy-done.7
  2.3 0.0 copy-start.8
  2.3 0.0 copy-start.9
  2.3 0.7 copy-done.8
  3.0 0.0 copy-done.9
  3.0 1.5 %stack.39.meta_ref = f32[16,4096]{1,0:T(8,128)} concatenate(f32[1,4096]{1,0:T(1,128)S(1)} %bitcast.37, f32[1,4096]{1,0:T(1,128)S(1)} %bitcast.30, f32[1,4096]{1,0:T(1,128)S(1)} %bitcast.32, f32[1,4096]{1,0:T(1,128)S(1)} %bitcast.38, f32[1,4096]{1,0:T(1,128)S(1)} %bitcast.34, f32[1,4096]{1,0:T(1,128)S(1)} %bitcast.35, f32[1,4096]{1,0:T(1,128)S(1)} %bitcast.31, ...), dimensions={0} | concatenate | bytes 524288 | tf_op jit(solution)/shard_map/stack | solution.py:760
  4.5 6.7 %sort_slots.1 = (f32[72,2048]{1,0:T(8,128)}, f32[72,2048]{1,0:T(8,128)}, f32[8,4096]{1,0:T(8,128)}) custom-call(f32[64,4096]{1,0:T(8,128)} %innov_ref.5, f32[16,4096]{1,0:T(8,128)} %stack.39.meta_ref), custom_call_target="tpu_custom_call" | custom-call | tf_op jit(solution)/shard_map/sort_slots/pallas_call | solution.py:101
  11.2 0.5 collective-permute-start
  11.7 5.9 %collective-permute-start.1 = (f32[72,2048]{1,0:T(8,128)}, f32[72,2048]{1,0:T(8,128)S(1)}, u32[]{:S(2)}, u32[]{:S(2)}) collective-permute-start(f32[72,2048]{1,0:T(8,128)} %get-tuple-element.16.c1), channel_id=1, source_target_pairs={{1,0},{2,1},{3,2},{4,3},{5,4},{6,5},{7,6},{8,7},{9,8},{10,9},{11,1... | collective-permute-start | bytes 1769480 | tf_op jit(solution)/shard_map/ppermute | solution.py:35
  17.6 0.0 copy-start.11
  17.6 0.7 copy-done.11
  18.3 0.0 copy-start.10
  18.3 0.7 copy-done.10
  19.0 0.8 stack.43.info_ref
  19.8 8.0 %innov_columns.1.rc_ref = f32[64,2048]{1,0:T(8,128)} custom-call(f32[64,4096]{1,0:T(8,128)} %innov_ref.5, f32[8,4096]{1,0:T(8,128)} %stack.43.info_ref), custom_call_target="tpu_custom_call" | custom-call | flops 4294967296 | bytes 4194304 | tf_op jit(solution)/shard_map/innov_columns/pallas_call | solution.py:679
  27.9 1.0 slice.26
  28.8 0.1 collective-permute-start.4
  28.9 0.0 collective-permute-done.c0
  28.9 0.0 copy-start
  28.9 0.0 collective-permute-done.1.c3
  28.9 0.8 copy-done
  29.7 0.0 copy-start.1
  29.7 0.8 copy-done.1
  30.6 16.1 %operate_first.1 = (f32[64,2048]{1,0:T(8,128)}, f32[64,2048]{1,0:T(8,128)}, f32[64,128]{1,0:T(8,128)}, s32[72,128]{1,0:T(8,128)}, s32[3,9,128]{2,1,0:T(8,128)}) custom-call(f32[72,2048]{1,0:T(8,128)} %copy-done, f32[72,2048]{1,0:T(8,128)} %get-tuple-element.16.c1, f32[72,2048]{1,0:T(8,128)} %get-tuple-element.15.c2, f32[72,2048]{1,0:T(8,128)} %copy-done.1), custom_call_target="tpu_custom_call" | custom-call | tf_op jit(solution)/shard_map/operate_first/pallas_call | solution.py:456
  46.7 0.1 collective-permute-start.2
  46.8 5.3 %collective-permute-start.3 = (f32[64,2048]{1,0:T(8,128)}, f32[64,2048]{1,0:T(8,128)S(1)}, u32[]{:S(2)}, u32[]{:S(2)}) collective-permute-start(f32[64,2048]{1,0:T(8,128)} %get-tuple-element.22.i1.imga_ref), channel_id=1, source_target_pairs={{1,0},{2,1},{3,2},{4,3},{5,4},{6,5},{7,6},{8,7},{9,8},{10,9},{11,1... | collective-permute-start | bytes 1572872 | tf_op jit(solution)/shard_map/ppermute | solution.py:35
  52.1 9.0 %columns.1 = (f32[64,4096]{1,0:T(8,128)}, f32[64,2048]{1,0:T(8,128)}) custom-call(f32[8,4096]{1,0:T(8,128)} %stack.43.info_ref, f32[8,4096]{1,0:T(8,128)} %get-tuple-element.25.rank_ref, f32[64,2048]{1,0:T(8,128)} %get-tuple-element.22.i1.imga_ref, f32[64,2048]{1,0:T(8,128)} %get-tuple-element.21.i2.imgb_ref), custom_call_target="tpu_custom_call" | custom-call | flops 6442450944 | bytes 4194304 | tf_op jit(solution)/shard_map/columns/pallas_call | solution.py:694
  61.1 1.0 slice.25
  62.1 0.1 collective-permute-start.5
  62.1 15.8 %sum_all.2.gram_ref = f32[64,128]{1,0:T(8,128)} custom-call(f32[64,128]{1,0:T(8,128)} %get-tuple-element.19.x_ref), custom_call_target="tpu_custom_call" | custom-call | tf_op jit(solution)/shard_map/sum_all/pallas_call | solution.py:544
  77.9 7.2 %solve_first.1 = (f32[64,64]{1,0:T(8,128)}, f32[64,64]{1,0:T(8,128)}, f32[64,64]{1,0:T(8,128)}) custom-call(f32[64,128]{1,0:T(8,128)} %sum_all.2.gram_ref), custom_call_target="tpu_custom_call" | custom-call | tf_op jit(solution)/shard_map/solve_first/pallas_call | solution.py:613
  85.1 0.0 collective-permute-done.2.i0
  85.1 0.0 copy-start.2
  85.1 0.0 collective-permute-done.3.i3
  85.2 0.0 copy-start.3
  85.2 0.8 copy-done.2
  85.9 0.2 copy-done.3
  86.1 17.1 %operate_second.1.x_ref = f32[128,128]{1,0:T(8,128)} custom-call(s32[72,128]{1,0:T(8,128)} %get-tuple-element.17.span_in, s32[3,9,128]{2,1,0:T(8,128)} %get-tuple-element.18.item_in, f32[64,64]{1,0:T(8,128)} %get-tuple-element.20.step_ref, f32[72,2048]{1,0:T(8,128)} %copy-done, f32[72,2048]{1,0:T(8,128)} %get-tuple-element.16.c1, ...), custom_call_target="tpu_custom_call" | custom-call | tf_op jit(solution)/shard_map/operate_second/pallas_call | solution.py:474
  103.3 19.5 %sum_all.3.gram_ref = f32[128,128]{1,0:T(8,128)} custom-call(f32[128,128]{1,0:T(8,128)} %operate_second.1.x_ref), custom_call_target="tpu_custom_call" | custom-call | tf_op jit(solution)/shard_map/sum_all/pallas_call | solution.py:544
  122.8 8.2 %solve_second.1.coef_ref = f32[64,128]{1,0:T(8,128)} custom-call(f32[128,128]{1,0:T(8,128)} %sum_all.3.gram_ref, f32[64,64]{1,0:T(8,128)} %get-tuple-element.20.step_ref, f32[64,64]{1,0:T(8,128)} %get-tuple-element.23.inv_ref, f32[64,64]{1,0:T(8,128)} %get-tuple-element.24.curv_ref), custom_call_target="tpu_custom_call" | custom-call | tf_op jit(solution)/shard_map/solve_second/pallas_call | solution.py:624
  131.0 0.0 collective-permute-done.4.rin_ref
  131.0 0.0 copy-start.4
  131.0 0.0 collective-permute-done.5.iin_ref
  131.0 0.0 copy-start.5
  131.0 0.7 copy-done.4
  131.7 0.1 copy-done.5
  131.9 3.9 %final.1 = (f32[64,4096]{1,0:T(8,128)}, f32[64,1024]{1,0:T(8,128)}) custom-call(f32[64,128]{1,0:T(8,128)} %solve_second.1.coef_ref, f32[64,4096]{1,0:T(8,128)} %innov_ref.5, f32[8,4096]{1,0:T(8,128)} %stack.43.info_ref, f32[64,4096]{1,0:T(8,128)} %get-tuple-element.26.back_ref, f32[64,2048]{1,0:T(8,128)} %innov_columns.1.rc_ref, f32[64,1024]{1,0:T(8,128)} %copy-done.4, ...), custom_call_target="tpu_custom_call" | custom-call | tf_op jit(solution)/shard_map/final/pallas_call | solution.py:727
  (10 shorter events, 0.1 us)
Async XLA Ops:
  0.6 0.8 copy-start.12
  1.5 0.7 copy-start.6
  1.5 0.7 copy-start.7
  2.3 0.7 copy-start.8
  2.3 0.7 copy-start.9
  11.2 17.7 %collective-permute-start = (f32[72,2048]{1,0:T(8,128)}, f32[72,2048]{1,0:T(8,128)S(1)}, u32[]{:S(2)}, u32[]{:S(2)}) collective-permute-start(f32[72,2048]{1,0:T(8,128)} %get-tuple-element.15.c2), channel_id=1, source_target_pairs={{31,0},{0,1},{1,2},{2,3},{3,4},{4,5},{5,6},{6,7},{7,8},{8,9},{9,10... | collective-permute-start | bytes 1769480 | tf_op jit(solution)/shard_map/ppermute | solution.py:35
  11.7 17.2 %collective-permute-start.1 = (f32[72,2048]{1,0:T(8,128)}, f32[72,2048]{1,0:T(8,128)S(1)}, u32[]{:S(2)}, u32[]{:S(2)}) collective-permute-start(f32[72,2048]{1,0:T(8,128)} %get-tuple-element.16.c1), channel_id=1, source_target_pairs={{1,0},{2,1},{3,2},{4,3},{5,4},{6,5},{7,6},{8,7},{9,8},{10,9},{11,1... | collective-permute-start | bytes 1769480 | tf_op jit(solution)/shard_map/ppermute | solution.py:35
  17.6 0.7 copy-start.11
  18.3 0.7 copy-start.10
  28.8 102.2 %collective-permute-start.4 = (f32[64,1024]{1,0:T(8,128)S(1)}, f32[64,1024]{1,0:T(8,128)S(1)}, u32[]{:S(2)}, u32[]{:S(2)}) collective-permute-start(f32[64,1024]{1,0:T(8,128)S(1)} %slice.26), channel_id=1, source_target_pairs={{31,0},{0,1},{1,2},{2,3},{3,4},{4,5},{5,6},{6,7},{7,8},{8,9},{9,10... | collective-permute-start | bytes 786440 | tf_op jit(solution)/shard_map/ppermute | solution.py:35
  28.9 0.8 copy-start
  29.7 0.8 copy-start.1
  46.7 38.4 %collective-permute-start.2 = (f32[64,2048]{1,0:T(8,128)}, f32[64,2048]{1,0:T(8,128)S(1)}, u32[]{:S(2)}, u32[]{:S(2)}) collective-permute-start(f32[64,2048]{1,0:T(8,128)} %get-tuple-element.21.i2.imgb_ref), channel_id=1, source_target_pairs={{31,0},{0,1},{1,2},{2,3},{3,4},{4,5},{5,6},{6,7},{7,8},{8,9},{9,10... | collective-permute-start | bytes 1572872 | tf_op jit(solution)/shard_map/ppermute | solution.py:35
  46.8 38.4 %collective-permute-start.3 = (f32[64,2048]{1,0:T(8,128)}, f32[64,2048]{1,0:T(8,128)S(1)}, u32[]{:S(2)}, u32[]{:S(2)}) collective-permute-start(f32[64,2048]{1,0:T(8,128)} %get-tuple-element.22.i1.imga_ref), channel_id=1, source_target_pairs={{1,0},{2,1},{3,2},{4,3},{5,4},{6,5},{7,6},{8,7},{9,8},{10,9},{11,1... | collective-permute-start | bytes 1572872 | tf_op jit(solution)/shard_map/ppermute | solution.py:35
  62.1 69.0 %collective-permute-start.5 = (f32[64,1024]{1,0:T(8,128)S(1)}, f32[64,1024]{1,0:T(8,128)S(1)}, u32[]{:S(2)}, u32[]{:S(2)}) collective-permute-start(f32[64,1024]{1,0:T(8,128)S(1)} %slice.25), channel_id=1, source_target_pairs={{31,0},{0,1},{1,2},{2,3},{3,4},{4,5},{5,6},{6,7},{7,8},{8,9},{9,10... | collective-permute-start | bytes 786440 | tf_op jit(solution)/shard_map/ppermute | solution.py:35
  85.1 0.8 copy-start.2
  85.2 1.0 copy-start.3
  131.0 0.7 copy-start.4
  131.0 0.8 copy-start.5

commit v2 on v1

--- a/solution.py
+++ b/solution.py
@@ -14,6 +14,7 @@
 TILE = 32
 STEP = 16
 PAIR = 4
+PANEL = 8
 EMPTY = ROWS // STEP
 DEAD = 1e9
 FAR = 1e6
@@ -66,8 +67,8 @@
 def sort_kernel(innov_ref, meta_ref, first_ref, last_ref, rank_ref):
     regions = innov_ref.shape[1] // ROWS
     kept = first_ref.shape[0]
-    sub = lax.broadcasted_iota(jnp.int32, (ROWS, 128), 0)
-    lane = lax.broadcasted_iota(jnp.int32, (ROWS, 128), 1)
+    sub = lax.broadcasted_iota(jnp.int32, (128, 128), 0)
+    lane = lax.broadcasted_iota(jnp.int32, (128, 128), 1)
     for g in range(regions):
         cols = pl.ds(g * ROWS, ROWS)
         meta = meta_ref[:, cols]
@@ -76,9 +77,18 @@
         key_col = jnp.broadcast_to(key, (128, ROWS)).T
         ranks = []
         for b in range(ROWS // 128):
-            mine = key[:, b * 128 : (b + 1) * 128]
-            before = (key_col < mine) | ((key_col == mine) & (sub < lane + b * 128))
-            ranks.append(jnp.sum(before.astype(f32), axis=0, keepdims=True))
+            begin, end = b * 128, (b + 1) * 128
+            mine = key[:, begin:end]
+            other = key_col[begin:end]
+            before = (other < mine) | ((other == mine) & (sub < lane))
+            total = jnp.sum(jnp.where(before, 1.0, 0.0), axis=0, keepdims=True)
+            if b:
+                before = jnp.where(key_col[:begin] <= mine, 1.0, 0.0)
+                total = total + jnp.sum(before, axis=0, keepdims=True)
+            if end < ROWS:
+                before = jnp.where(key_col[end:] < mine, 1.0, 0.0)
+                total = total + jnp.sum(before, axis=0, keepdims=True)
+            ranks.append(total)
         rank = jnp.concatenate(ranks, axis=1)
         rank_ref[:, cols] = jnp.broadcast_to(rank, (8, ROWS))
         stack = jnp.concatenate([innov_ref[:, cols] * live, meta], axis=0)
@@ -314,6 +324,26 @@
     )
 
 
+def square(n):
+    return lax.broadcasted_iota(jnp.int32, (n, n), 0), lax.broadcasted_iota(jnp.int32, (n, n), 1)
+
+
+def pack_pair(upper, lower):
+    n = upper.shape[0]
+    row, col = square(n)
+    upper, lower = symmetric(upper), symmetric(lower)
+    spare = jnp.sum(jnp.where(row == col, lower, 0.0), axis=0, keepdims=True)
+    return jnp.where(col >= row, upper, lower), jnp.broadcast_to(spare, (8, n))
+
+
+def unpack_pair(packed, spare):
+    n = packed.shape[0]
+    row, col = square(n)
+    other = packed.T
+    lower = jnp.where(row == col, jnp.broadcast_to(spare, (n, n)), jnp.where(col > row, other, packed))
+    return jnp.where(col >= row, packed, other), lower
+
+
 def first_kernel(
     c0,
     c1,
@@ -362,7 +392,11 @@
     imga_ref[...] = img_ref[:, :lead]
     imgb_ref[...] = img_ref[:, lead:]
     r = v_ref[:, lead : lead + own]
-    gram_ref[...] = gram(r, jnp.concatenate([r, img_ref[...]], axis=0))
+    both = gram(r, jnp.concatenate([r, img_ref[...]], axis=0))
+    packed, spare = pack_pair(both[:, :ens], both[:, ens:])
+    half = ens // 2
+    gram_ref[0:half, :] = jnp.concatenate([packed[:half], packed[half:]], axis=1)
+    gram_ref[half : half + 8, :] = jnp.concatenate([spare, spare], axis=1)
 
 
 def second_kernel(
@@ -414,9 +448,11 @@
         span_ref, item_ref, row_ref, tables, spreads, v_ref, img_ref, turn_ref, sum_ref, s_ref
     )
     r = v_ref[:, lead : lead + own]
-    gram_ref[:ens] = gram(r, jnp.concatenate([r, img_ref[...]], axis=0))
+    both = gram(r, jnp.concatenate([r, img_ref[...]], axis=0))
     mixed = gram(r, jnp.concatenate([i1[...], i2[...]], axis=1))
-    gram_ref[ens:] = jnp.concatenate([mixed, mixed], axis=1)
+    packed, spare = pack_pair(both[:, :ens], both[:, ens:])
+    gram_ref[0:ens, :] = jnp.concatenate([packed, mixed], axis=1)
+    gram_ref[ens : ens + 8, :] = jnp.concatenate([spare, spare], axis=1)
 
 
 def plan_shapes(own):
@@ -458,7 +494,7 @@
         out_shape=(
             half,
             half,
-            jax.ShapeDtypeStruct((ens, 2 * ens), f32),
+            jax.ShapeDtypeStruct((ens // 2 + 8, 2 * ens), f32),
             jax.ShapeDtypeStruct(spans, jnp.int32),
             jax.ShapeDtypeStruct(items, jnp.int32),
         ),
@@ -473,7 +509,7 @@
 def second_call(plan, step, chunks, images, ens, own):
     return pl.pallas_call(
         second_kernel,
-        out_shape=jax.ShapeDtypeStruct((2 * ens, 2 * ens), f32),
+        out_shape=jax.ShapeDtypeStruct((ens + 8, 2 * ens), f32),
         in_specs=[vmem] * 11,
         out_specs=vmem,
         scratch_shapes=scratch(ens, own),
@@ -567,23 +603,41 @@
 
 def eliminate(chains):
     ens, both = chains[0].shape
-    rows = lax.broadcasted_iota(jnp.int32, (ens, both), 0)
-    for k in range(ens):
-        done = []
-        for m in chains:
-            col = jnp.broadcast_to(m[:, k : k + 1], (ens, both))
-            pivot = m[k : k + 1] / col[k : k + 1]
-            done.append(jnp.where(rows == k, pivot, m - col * pivot))
-        chains = done
-    return [m[:, ens:] for m in chains]
+    parts = range(ens // 8)
+    rows = lax.broadcasted_iota(jnp.int32, (8, both), 0)
+    chains = [[m[8 * i : 8 * i + 8] for i in parts] for m in chains]
+
+    def clear(parts_of, col, pivot, at):
+        done = [x - c * pivot for x, c in zip(parts_of, col)]
+        done[at // 8] = jnp.where(rows == at % 8, pivot, done[at // 8])
+        return done
+
+    for k in range(0, ens, PANEL):
+        columns = [
+            [[jnp.broadcast_to(x[:, k + j : k + j + 1], (8, both)) for x in m] for j in range(PANEL)]
+            for m in chains
+        ]
+        for p in range(PANEL):
+            at = k + p
+            one = slice(at % 8, at % 8 + 1)
+            done = []
+            for m, cols in zip(chains, columns):
+                col = cols[p]
+                scale = 1.0 / col[at // 8][one]
+                for j in range(p + 1, PANEL):
+                    cols[j] = clear(cols[j], col, cols[j][at // 8][one] * scale, at)
+                done.append(clear(m, col, m[at // 8][one] * scale, at))
+            chains = done
+    return [jnp.concatenate(m, axis=0)[:, ens:] for m in chains]
 
 
 def solve_first_kernel(gram_ref, step_ref, inv_ref, curv_ref):
-    ens = gram_ref.shape[0]
-    norm = symmetric(gram_ref[:, :ens])
-    curv = symmetric(gram_ref[:, ens:])
-    rows = lax.broadcasted_iota(jnp.int32, (ens, ens), 0)
-    eye = (rows == lax.broadcasted_iota(jnp.int32, (ens, ens), 1)).astype(f32)
+    ens = step_ref.shape[0]
+    half = ens // 2
+    packed = jnp.concatenate([gram_ref[0:half, :ens], gram_ref[0:half, ens:]], axis=0)
+    norm, curv = unpack_pair(packed, gram_ref[half : half + 1, :ens])
+    row, col = square(ens)
+    eye = (row == col).astype(f32)
     step, inv = eliminate(
         [jnp.concatenate([curv, norm], axis=1), jnp.concatenate([norm, eye], axis=1)]
     )
@@ -594,9 +648,8 @@
 
 def solve_second_kernel(gram_ref, step_ref, inv_ref, curv_ref, coef_ref):
     ens = step_ref.shape[0]
-    norm = symmetric(gram_ref[:ens, :ens])
-    cross = gram_ref[:ens, ens:]
-    mixed = gram_ref[ens:, :ens]
+    norm, cross = unpack_pair(gram_ref[0:ens, :ens], gram_ref[ens : ens + 1, :ens])
+    mixed = gram_ref[0:ens, ens:]
     conj = mm(inv_ref[...], norm)
     coupled = mm(mixed, conj)
     quad = mm(conj, mm(curv_ref[...], conj), TN)
@@ -608,7 +661,7 @@
 
 
 def solve_first(grams):
-    ens = grams.shape[0]
+    ens = grams.shape[1] // 2
     small = jax.ShapeDtypeStruct((ens, ens), f32)
     return pl.pallas_call(
         solve_first_kernel,

time: 137 us -> 126 us (0.920)
  Pallas kernels: 112 us -> 101 us
    pallas_call x1, Pallas kernels: 8.24 us -> 4.38 us  [solve_second(): pl.pallas_call(solve_second_kernel, out_shape=jax.ShapeDtypeStruct((ens,...]
    pallas_call x1, Pallas kernels: 7.2 us -> 3.75 us  [solve_first(): pl.pallas_call(solve_first_kernel, out_shape=(small, small, small), in_sp...]
    pallas_call x2, Pallas kernels: 35.3 us -> 32.2 us  [sum_all(): pl.pallas_call(functools.partial(reduce_kernel, steps, n_col), out_shape=...]
  transfers between devices with their start and end apart: 6 -> 6, of which waited for: 0 -> 0; matrix products, arithmetic and copies ran while one was open for 2% -> 2% of each run, Pallas kernels for 74% -> 73%
where the time goes in v2:
time: 126 us; the launch traced here: 125 us
  Pallas kernels  101 us (80%)
  starting transfers between devices  11.9 us (9%)
  local copies, waits for them, and re-layouts  10.6 us (8%)
    pallas_call x2, Pallas kernels, sum_all(): pl.pallas_call(functools.partial(reduce_kernel, steps, n_col), out_shape=...  32.2 us
    pallas_call x1, Pallas kernels, second_call(): pl.pallas_call(second_kernel, out_shape=jax.ShapeDtypeStruct((ens + 8, 2...  17.3 us
    pallas_call x1, Pallas kernels, first_call(): pl.pallas_call(first_kernel, out_shape=(half, half, jax.ShapeDtypeStruct(...  16.5 us
    ppermute x6, starting transfers between devices, shift(): lax.ppermute(block, axis, [((i - distance) % n, i) for i in range(n)])  11.9 us
    pallas_call x1, Pallas kernels, columns_call(): pl.pallas_call(columns_kernel, out_shape=(jax.ShapeDtypeStruct((ens, 2 *...  9 us
    pallas_call x1, Pallas kernels, innov_columns_call(): pl.pallas_call(innov_columns_kernel, out_shape=jax.ShapeDtypeStruct((ens,...  8.04 us
    unnamed x30, local copies, waits for them, and re-layouts  6.33 us
    pallas_call x1, Pallas kernels, sort_call(): pl.pallas_call(sort_kernel, out_shape=(half, half, jax.ShapeDtypeStruct((...  6.24 us
  transfers between devices with their start and end apart: 6, of which 0 were waited for; matrix products, arithmetic and copies ran while one was open for 2% of the time, Pallas kernels for 73%

profile of v2, /device:TPU:0, one launch (start us, length us, event | category | flops | bytes accessed | tf_op | source)
XLA Modules:
  0.0 125.5 jit_solution(16693971062025066528)
XLA Ops:
  0.6 0.0 copy-start.12
  0.6 0.7 convert_bitcast_fusion
  1.4 0.0 copy-done.12
  1.4 0.1 broadcast_bitcast_fusion
  1.5 0.0 copy-start.6
  1.5 0.0 copy-start.7
  1.6 0.7 copy-done.6
  2.2 0.0 copy-done.7
  2.3 0.0 copy-start.8
  2.3 0.0 copy-start.9
  2.3 0.7 copy-done.8
  3.0 0.0 copy-done.9
  3.0 1.5 %stack.39.meta_ref = f32[16,4096]{1,0:T(8,128)} concatenate(f32[1,4096]{1,0:T(1,128)S(1)} %bitcast.37, f32[1,4096]{1,0:T(1,128)S(1)} %bitcast.30, f32[1,4096]{1,0:T(1,128)S(1)} %bitcast.32, f32[1,4096]{1,0:T(1,128)S(1)} %bitcast.38, f32[1,4096]{1,0:T(1,128)S(1)} %bitcast.34, f32[1,4096]{1,0:T(1,128)S(1)} %bitcast.35, f32[1,4096]{1,0:T(1,128)S(1)} %bitcast.31, ...), dimensions={0} | concatenate | bytes 524288 | tf_op jit(solution)/shard_map/stack | solution.py:813
  4.5 6.2 %sort_slots.1 = (f32[72,2048]{1,0:T(8,128)}, f32[72,2048]{1,0:T(8,128)}, f32[8,4096]{1,0:T(8,128)}) custom-call(f32[64,4096]{1,0:T(8,128)} %innov_ref.5, f32[16,4096]{1,0:T(8,128)} %stack.39.meta_ref), custom_call_target="tpu_custom_call" | custom-call | tf_op jit(solution)/shard_map/sort_slots/pallas_call | solution.py:111
  10.7 0.5 collective-permute-start
  11.2 5.9 %collective-permute-start.1 = (f32[72,2048]{1,0:T(8,128)}, f32[72,2048]{1,0:T(8,128)S(1)}, u32[]{:S(2)}, u32[]{:S(2)}) collective-permute-start(f32[72,2048]{1,0:T(8,128)} %get-tuple-element.16.c1), channel_id=1, source_target_pairs={{1,0},{2,1},{3,2},{4,3},{5,4},{6,5},{7,6},{8,7},{9,8},{10,9},{11,1... | collective-permute-start | bytes 1769480 | tf_op jit(solution)/shard_map/ppermute | solution.py:36
  17.1 0.0 copy-start.11
  17.2 0.7 copy-done.11
  17.9 0.0 copy-start.10
  17.9 0.7 copy-done.10
  18.6 0.8 stack.43.info_ref
  19.4 8.0 %innov_columns.1.rc_ref = f32[64,2048]{1,0:T(8,128)} custom-call(f32[64,4096]{1,0:T(8,128)} %innov_ref.5, f32[8,4096]{1,0:T(8,128)} %stack.43.info_ref), custom_call_target="tpu_custom_call" | custom-call | flops 4294967296 | bytes 4194304 | tf_op jit(solution)/shard_map/innov_columns/pallas_call | solution.py:732
  27.4 1.0 slice.26
  28.4 0.1 collective-permute-start.4
  28.5 0.0 collective-permute-done.c0
  28.5 0.0 copy-start
  28.5 0.0 collective-permute-done.1.c3
  28.5 0.8 copy-done
  29.3 0.0 copy-start.1
  29.3 0.8 copy-done.1
  30.1 16.5 %operate_first.1 = (f32[64,2048]{1,0:T(8,128)}, f32[64,2048]{1,0:T(8,128)}, f32[40,128]{1,0:T(8,128)}, s32[72,128]{1,0:T(8,128)}, s32[3,9,128]{2,1,0:T(8,128)}) custom-call(f32[72,2048]{1,0:T(8,128)} %copy-done, f32[72,2048]{1,0:T(8,128)} %get-tuple-element.16.c1, f32[72,2048]{1,0:T(8,128)} %get-tuple-element.15.c2, f32[72,2048]{1,0:T(8,128)} %copy-done.1), custom_call_target="tpu_custom_call" | custom-call | tf_op jit(solution)/shard_map/operate_first/pallas_call | solution.py:492
  46.7 0.1 collective-permute-start.2
  46.7 5.3 %collective-permute-start.3 = (f32[64,2048]{1,0:T(8,128)}, f32[64,2048]{1,0:T(8,128)S(1)}, u32[]{:S(2)}, u32[]{:S(2)}) collective-permute-start(f32[64,2048]{1,0:T(8,128)} %get-tuple-element.22.i1.imga_ref), channel_id=1, source_target_pairs={{1,0},{2,1},{3,2},{4,3},{5,4},{6,5},{7,6},{8,7},{9,8},{10,9},{11,1... | collective-permute-start | bytes 1572872 | tf_op jit(solution)/shard_map/ppermute | solution.py:36
  52.0 9.0 %columns.1 = (f32[64,4096]{1,0:T(8,128)}, f32[64,2048]{1,0:T(8,128)}) custom-call(f32[8,4096]{1,0:T(8,128)} %stack.43.info_ref, f32[8,4096]{1,0:T(8,128)} %get-tuple-element.25.rank_ref, f32[64,2048]{1,0:T(8,128)} %get-tuple-element.22.i1.imga_ref, f32[64,2048]{1,0:T(8,128)} %get-tuple-element.21.i2.imgb_ref), custom_call_target="tpu_custom_call" | custom-call | flops 6442450944 | bytes 4194304 | tf_op jit(solution)/shard_map/columns/pallas_call | solution.py:747
  61.1 1.0 slice.25
  62.0 0.1 collective-permute-start.5
  62.1 16.3 %sum_all.2.gram_ref = f32[40,128]{1,0:T(8,128)} custom-call(f32[40,128]{1,0:T(8,128)} %get-tuple-element.19.x_ref), custom_call_target="tpu_custom_call" | custom-call | tf_op jit(solution)/shard_map/sum_all/pallas_call | solution.py:580
  78.4 3.8 %solve_first.1 = (f32[64,64]{1,0:T(8,128)}, f32[64,64]{1,0:T(8,128)}, f32[64,64]{1,0:T(8,128)}) custom-call(f32[40,128]{1,0:T(8,128)} %sum_all.2.gram_ref), custom_call_target="tpu_custom_call" | custom-call | tf_op jit(solution)/shard_map/solve_first/pallas_call | solution.py:666
  82.2 0.0 collective-permute-done.2.i0
  82.2 0.0 copy-start.2
  82.2 0.0 collective-permute-done.3.i3
  82.2 0.0 copy-start.3
  82.2 0.8 copy-done.2
  83.0 0.2 copy-done.3
  83.2 17.3 %operate_second.1.x_ref = f32[72,128]{1,0:T(8,128)} custom-call(s32[72,128]{1,0:T(8,128)} %get-tuple-element.17.span_in, s32[3,9,128]{2,1,0:T(8,128)} %get-tuple-element.18.item_in, f32[64,64]{1,0:T(8,128)} %get-tuple-element.20.step_ref, f32[72,2048]{1,0:T(8,128)} %copy-done, f32[72,2048]{1,0:T(8,128)} %get-tuple-element.16.c1, ...), custom_call_target="tpu_custom_call" | custom-call | tf_op jit(solution)/shard_map/operate_second/pallas_call | solution.py:510
  100.5 15.8 %sum_all.3.gram_ref = f32[72,128]{1,0:T(8,128)} custom-call(f32[72,128]{1,0:T(8,128)} %operate_second.1.x_ref), custom_call_target="tpu_custom_call" | custom-call | tf_op jit(solution)/shard_map/sum_all/pallas_call | solution.py:580
  116.4 4.4 %solve_second.1.coef_ref = f32[64,128]{1,0:T(8,128)} custom-call(f32[72,128]{1,0:T(8,128)} %sum_all.3.gram_ref, f32[64,64]{1,0:T(8,128)} %get-tuple-element.20.step_ref, f32[64,64]{1,0:T(8,128)} %get-tuple-element.23.inv_ref, f32[64,64]{1,0:T(8,128)} %get-tuple-element.24.curv_ref), custom_call_target="tpu_custom_call" | custom-call | tf_op jit(solution)/shard_map/solve_second/pallas_call | solution.py:677
  120.8 0.0 collective-permute-done.4.rin_ref
  120.8 0.0 copy-start.4
  120.8 0.0 collective-permute-done.5.iin_ref
  120.8 0.0 copy-start.5
  120.8 0.7 copy-done.4
  121.5 0.1 copy-done.5
  121.6 3.9 %final.1 = (f32[64,4096]{1,0:T(8,128)}, f32[64,1024]{1,0:T(8,128)}) custom-call(f32[64,128]{1,0:T(8,128)} %solve_second.1.coef_ref, f32[64,4096]{1,0:T(8,128)} %innov_ref.5, f32[8,4096]{1,0:T(8,128)} %stack.43.info_ref, f32[64,4096]{1,0:T(8,128)} %get-tuple-element.26.back_ref, f32[64,2048]{1,0:T(8,128)} %innov_columns.1.rc_ref, f32[64,1024]{1,0:T(8,128)} %copy-done.4, ...), custom_call_target="tpu_custom_call" | custom-call | tf_op jit(solution)/shard_map/final/pallas_call | solution.py:780
  (10 shorter events, 0.1 us)
Async XLA Ops:
  0.6 0.8 copy-start.12
  1.5 0.7 copy-start.6
  1.5 0.7 copy-start.7
  2.3 0.7 copy-start.8
  2.3 0.7 copy-start.9
  10.7 17.7 %collective-permute-start = (f32[72,2048]{1,0:T(8,128)}, f32[72,2048]{1,0:T(8,128)S(1)}, u32[]{:S(2)}, u32[]{:S(2)}) collective-permute-start(f32[72,2048]{1,0:T(8,128)} %get-tuple-element.15.c2), channel_id=1, source_target_pairs={{31,0},{0,1},{1,2},{2,3},{3,4},{4,5},{5,6},{6,7},{7,8},{8,9},{9,10... | collective-permute-start | bytes 1769480 | tf_op jit(solution)/shard_map/ppermute | solution.py:36
  11.2 17.2 %collective-permute-start.1 = (f32[72,2048]{1,0:T(8,128)}, f32[72,2048]{1,0:T(8,128)S(1)}, u32[]{:S(2)}, u32[]{:S(2)}) collective-permute-start(f32[72,2048]{1,0:T(8,128)} %get-tuple-element.16.c1), channel_id=1, source_target_pairs={{1,0},{2,1},{3,2},{4,3},{5,4},{6,5},{7,6},{8,7},{9,8},{10,9},{11,1... | collective-permute-start | bytes 1769480 | tf_op jit(solution)/shard_map/ppermute | solution.py:36
  17.1 0.7 copy-start.11
  17.9 0.7 copy-start.10
  28.4 92.4 %collective-permute-start.4 = (f32[64,1024]{1,0:T(8,128)S(1)}, f32[64,1024]{1,0:T(8,128)S(1)}, u32[]{:S(2)}, u32[]{:S(2)}) collective-permute-start(f32[64,1024]{1,0:T(8,128)S(1)} %slice.26), channel_id=1, source_target_pairs={{31,0},{0,1},{1,2},{2,3},{3,4},{4,5},{5,6},{6,7},{7,8},{8,9},{9,10... | collective-permute-start | bytes 786440 | tf_op jit(solution)/shard_map/ppermute | solution.py:36
  28.5 0.8 copy-start
  29.3 0.8 copy-start.1
  46.7 35.5 %collective-permute-start.2 = (f32[64,2048]{1,0:T(8,128)}, f32[64,2048]{1,0:T(8,128)S(1)}, u32[]{:S(2)}, u32[]{:S(2)}) collective-permute-start(f32[64,2048]{1,0:T(8,128)} %get-tuple-element.21.i2.imgb_ref), channel_id=1, source_target_pairs={{31,0},{0,1},{1,2},{2,3},{3,4},{4,5},{5,6},{6,7},{7,8},{8,9},{9,10... | collective-permute-start | bytes 1572872 | tf_op jit(solution)/shard_map/ppermute | solution.py:36
  46.7 35.5 %collective-permute-start.3 = (f32[64,2048]{1,0:T(8,128)}, f32[64,2048]{1,0:T(8,128)S(1)}, u32[]{:S(2)}, u32[]{:S(2)}) collective-permute-start(f32[64,2048]{1,0:T(8,128)} %get-tuple-element.22.i1.imga_ref), channel_id=1, source_target_pairs={{1,0},{2,1},{3,2},{4,3},{5,4},{6,5},{7,6},{8,7},{9,8},{10,9},{11,1... | collective-permute-start | bytes 1572872 | tf_op jit(solution)/shard_map/ppermute | solution.py:36
  62.0 58.7 %collective-permute-start.5 = (f32[64,1024]{1,0:T(8,128)S(1)}, f32[64,1024]{1,0:T(8,128)S(1)}, u32[]{:S(2)}, u32[]{:S(2)}) collective-permute-start(f32[64,1024]{1,0:T(8,128)S(1)} %slice.25), channel_id=1, source_target_pairs={{31,0},{0,1},{1,2},{2,3},{3,4},{4,5},{5,6},{6,7},{7,8},{8,9},{9,10... | collective-permute-start | bytes 786440 | tf_op jit(solution)/shard_map/ppermute | solution.py:36
  82.2 0.8 copy-start.2
  82.2 1.0 copy-start.3
  120.8 0.7 copy-start.4
  120.8 0.8 copy-start.5

commit v3 on v2

--- a/solution.py
+++ b/solution.py
@@ -10,7 +10,6 @@
 ROWS = 1024
 REACH = 2
 COLS_DEV = 1024
-META = 16
 TILE = 32
 STEP = 16
 PAIR = 4
@@ -28,12 +27,7 @@
 TN = (((0,), (0,)), ((), ()))
 vmem = pl.BlockSpec(memory_space=pltpu.VMEM)
 smem = pl.BlockSpec(memory_space=pltpu.SMEM)
-
-
-def shift(block, distance):
-    axis = ("reg", "col")
-    n = lax.axis_size(axis)
-    return lax.ppermute(block, axis, [((i - distance) % n, i) for i in range(n)])
+anywhere = pl.BlockSpec(memory_space=pl.ANY)
 
 
 def dot(a, b, dims=NN):
@@ -64,58 +58,133 @@
     return pltpu.CompilerParams(vmem_limit_bytes=VMEM_LIMIT)
 
 
-def sort_kernel(innov_ref, meta_ref, first_ref, last_ref, rank_ref):
+def ring(total, n_col):
+    me = lax.axis_index("reg") * n_col + lax.axis_index("col")
+    left, right = (me + total - 1) % total, (me + 1) % total
+    return me, (left // n_col, left % n_col), (right // n_col, right % n_col)
+
+
+def send_to(src, dst, sems, k, device):
+    return pltpu.make_async_remote_copy(
+        src_ref=src,
+        dst_ref=dst,
+        send_sem=sems[0].at[k],
+        recv_sem=sems[1].at[k],
+        device_id=device,
+        device_id_type=pl.DeviceIdType.MESH,
+    )
+
+
+def greet(devices):
+    barrier = pltpu.get_barrier_semaphore()
+    for device in devices:
+        pl.semaphore_signal(barrier, inc=1, device_id=device, device_id_type=pl.DeviceIdType.MESH)
+
+
+def live_row(count_ref, g):
+    slot = lax.broadcasted_iota(jnp.int32, (1, ROWS), 1)
+    return (slot < count_ref[g]).astype(f32)
+
+
+def sort_kernel(
+    total,
+    n_col,
+    count_ref,
+    pair_ref,
+    innov_ref,
+    along_ref,
+    across_ref,
+    scale_ref,
+    error_ref,
+    first_ref,
+    last_ref,
+    before_ref,
+    after_ref,
+    rank_ref,
+    send_sem,
+    recv_sem,
+):
     regions = innov_ref.shape[1] // ROWS
-    kept = first_ref.shape[0]
     sub = lax.broadcasted_iota(jnp.int32, (128, 128), 0)
     lane = lax.broadcasted_iota(jnp.int32, (128, 128), 1)
-    for g in range(regions):
-        cols = pl.ds(g * ROWS, ROWS)
-        meta = meta_ref[:, cols]
-        key = meta[6:7]
-        live = (key < 0.5 * DEAD).astype(f32)
+    _, left, right = ring(total, n_col)
+    greet([left, right])
+
+    def sort_region(out_ref, shift_by, r, carry):
+        g = shift_by + r
+        cols = pl.ds(pl.multiple_of(g * ROWS, ROWS), ROWS)
+        live = live_row(count_ref, g)
+        across = across_ref[:, cols]
+        key = jnp.where(live > 0.5, across, DEAD)
+        flags = [jnp.full((1, ROWS), pair_ref[g, d], jnp.int32).astype(f32) for d in range(REACH)]
+        meta = [along_ref[:, cols], across, scale_ref[:, cols] * live, error_ref[:, cols]]
+        stack = jnp.concatenate(
+            [innov_ref[:, cols] * live] + meta + flags + [key, jnp.zeros((1, ROWS), f32)], axis=0
+        )
         key_col = jnp.broadcast_to(key, (128, ROWS)).T
         ranks = []
         for b in range(ROWS // 128):
             begin, end = b * 128, (b + 1) * 128
             mine = key[:, begin:end]
             other = key_col[begin:end]
-            before = (other < mine) | ((other == mine) & (sub < lane))
-            total = jnp.sum(jnp.where(before, 1.0, 0.0), axis=0, keepdims=True)
+            ahead = (other < mine) | ((other == mine) & (sub < lane))
+            rank = jnp.sum(jnp.where(ahead, 1.0, 0.0), axis=0, keepdims=True)
             if b:
-                before = jnp.where(key_col[:begin] <= mine, 1.0, 0.0)
-                total = total + jnp.sum(before, axis=0, keepdims=True)
+                ahead = jnp.where(key_col[:begin] <= mine, 1.0, 0.0)
+                rank = rank + jnp.sum(ahead, axis=0, keepdims=True)
             if end < ROWS:
-                before = jnp.where(key_col[end:] < mine, 1.0, 0.0)
-                total = total + jnp.sum(before, axis=0, keepdims=True)
-            ranks.append(total)
+                ahead = jnp.where(key_col[end:] < mine, 1.0, 0.0)
+                rank = rank + jnp.sum(ahead, axis=0, keepdims=True)
+            ranks.append(rank)
         rank = jnp.concatenate(ranks, axis=1)
         rank_ref[:, cols] = jnp.broadcast_to(rank, (8, ROWS))
-        stack = jnp.concatenate([innov_ref[:, cols] * live, meta], axis=0)
         lhs = jnp.concatenate(three(stack), axis=0)
         n = stack.shape[0]
         rank_i = rank.astype(jnp.int32)
-        out_ref = first_ref if g < regions // 2 else last_ref
         for c in range(ROWS // 256):
             slot = lax.broadcasted_iota(jnp.int32, (256, ROWS), 0) + c * 256
             place = (slot == rank_i).astype(f32).astype(bf16)
             got = dot(lhs, place, NT)
-            start = (g % (regions // 2)) * ROWS + c * 256
-            got = (got[:n] + got[n : 2 * n] + got[2 * n :])[:kept]
-            out_ref[:, start : start + 256] = got
-
-
-def sort_call(innov, meta):
+            at = pl.ds(pl.multiple_of(r * ROWS + c * 256, 256), 256)
+            out_ref[:, at] = got[:n] + got[n : 2 * n] + got[2 * n :]
+        return carry
+
+    half = regions // 2
+    lax.fori_loop(0, half, functools.partial(sort_region, first_ref, 0), 0)
+    pl.semaphore_wait(pltpu.get_barrier_semaphore(), 2)
+    sems = (send_sem, recv_sem)
+    back = send_to(first_ref, after_ref, sems, 0, left)
+    back.start()
+    lax.fori_loop(0, half, functools.partial(sort_region, last_ref, half), 0)
+    ahead = send_to(last_ref, before_ref, sems, 1, right)
+    ahead.start()
+    back.wait()
+    ahead.wait()
+
+
+def sizes():
+    n_col = lax.axis_size("col")
+    return lax.axis_size("reg") * n_col, n_col
+
+
+def comm_params(which):
+    return pltpu.CompilerParams(
+        collective_id=which, has_side_effects=True, vmem_limit_bytes=VMEM_LIMIT
+    )
+
+
+def sort_call(count, pair, innov, *rows):
     ens, n = innov.shape
     half = jax.ShapeDtypeStruct((ens + 8, n // 2), f32)
     return pl.pallas_call(
-        sort_kernel,
-        out_shape=(half, half, jax.ShapeDtypeStruct((8, n), f32)),
-        in_specs=[vmem, vmem],
-        out_specs=(vmem,) * 3,
-        compiler_params=params(),
+        functools.partial(sort_kernel, *sizes()),
+        out_shape=(half,) * 4 + (jax.ShapeDtypeStruct((8, n), f32),),
+        in_specs=[smem] * 2 + [vmem] * 5,
+        out_specs=(vmem, vmem, anywhere, anywhere, vmem),
+        scratch_shapes=[pltpu.SemaphoreType.DMA((2,)), pltpu.SemaphoreType.DMA((2,))],
+        compiler_params=comm_params(0),
         name="sort_slots",
-    )(innov, meta)
+    )(count, pair, innov, *rows)
 
 
 def lay_grid(chunks, row_ref, grid_ref):
@@ -530,67 +599,234 @@
     return steps
 
 
-def reduce_kernel(steps, n_col, x_ref, out_ref, send, recv, send_sem, recv_sem):
-    me = lax.axis_index("reg") * n_col + lax.axis_index("col")
-    partners = []
-    for sizes in steps:
-        others = [me + flip(me, size) for size in sizes]
-        if len(sizes) == 2:
-            others.append(others[0] + flip(me, sizes[1]))
-        partners.append([(other // n_col, other % n_col) for other in others])
-    barrier = pltpu.get_barrier_semaphore()
-    for group in partners:
-        for other in group:
-            pl.semaphore_signal(
-                barrier, inc=1, device_id=other, device_id_type=pl.DeviceIdType.MESH
-            )
-    pl.semaphore_wait(barrier, sum(len(group) for group in partners))
+def partners_of(steps, n_col, me):
+    found = []
+    for amounts in steps:
+        others = [me + flip(me, size) for size in amounts]
+        if len(amounts) == 2:
+            others.append(others[0] + flip(me, amounts[1]))
+        found.append([(other // n_col, other % n_col) for other in others])
+    return found
+
+
+def sum_all(partners, x_ref, send, recv, sems, work):
     total = x_ref[...]
     slot = 0
     for k, group in enumerate(partners):
         if k:
             send[k] = total
-        copies = []
-        for p, other in enumerate(group):
-            copies.append(
-                pltpu.make_async_remote_copy(
-                    src_ref=send.at[k] if k else x_ref,
-                    dst_ref=recv.at[slot + p],
-                    send_sem=send_sem.at[slot + p],
-                    recv_sem=recv_sem.at[slot + p],
-                    device_id=other,
-                    device_id_type=pl.DeviceIdType.MESH,
-                )
-            )
+        source = send.at[k] if k else x_ref
+        copies = [
+            send_to(source, recv.at[slot + p], sems, slot + p, other) for p, other in enumerate(group)
+        ]
         for copy in copies:
             copy.start()
+        if k < len(work):
+            work[k]()
         for copy in copies:
             copy.wait()
         total = total + recv[slot]
         if len(group) == 3:
             total = total + (recv[slot + 1] + recv[slot + 2])
         slot += len(group)
-    out_ref[...] = total
-
-
-def sum_all(x, which):
-    n_col = lax.axis_size("col")
-    steps = exchange_steps(lax.axis_size("reg") * n_col)
-    slots = sum(2 ** len(sizes) - 1 for sizes in steps)
+    for piece in work[len(partners) :]:
+        piece()
+    return total
+
+
+def local_column(owner, me, total):
+    local = owner - me * COLS_DEV
+    return jnp.where(local < 0, local + total * COLS_DEV, local)
+
+
+def add_columns(scaled_ref, owner_ref, me, total, base, target_ref):
+    own = owner_ref.shape[1]
+
+    def one(c, carry):
+        got = jnp.zeros((scaled_ref.shape[0], 256), f32)
+        for g in range(own // ROWS):
+            at = slice(g * ROWS, (g + 1) * ROWS)
+            slot = lax.broadcasted_iota(jnp.int32, (256, ROWS), 0) + (base + c * 256)
+            owner = local_column(owner_ref[:, at], me, total)
+            hot = (slot == owner).astype(f32).astype(bf16)
+            got = got + dot(scaled_ref[:, at], hot, NT)
+        ens = target_ref.shape[0]
+        target_ref[:, pl.ds(pl.multiple_of(c * 256, 256), 256)] = got[:ens] + got[ens:]
+        return carry
+
+    lax.fori_loop(0, COLS_DEV // 256, one, 0)
+
+
+def join_first_kernel(
+    steps,
+    total,
+    n_col,
+    x_ref,
+    imga_ref,
+    imgb_ref,
+    rank_ref,
+    gain_ref,
+    owner_ref,
+    out_ref,
+    before_ref,
+    after_ref,
+    back_ref,
+    cols_ref,
+    came_ref,
+    scaled_ref,
+    edge_ref,
+    send,
+    recv,
+    send_sem,
+    recv_sem,
+    bulk_send_sem,
+    bulk_recv_sem,
+):
+    ens, half = imga_ref.shape
+    me, left, right = ring(total, n_col)
+    partners = partners_of(steps, n_col, me)
+    everyone = [other for group in partners for other in group] + [left, right]
+    greet(everyone)
+    pl.semaphore_wait(pltpu.get_barrier_semaphore(), len(everyone))
+    bulk = (bulk_send_sem, bulk_recv_sem)
+    copies = [send_to(imga_ref, after_ref, bulk, 0, left), send_to(imgb_ref, before_ref, bulk, 1, right)]
+    edge = send_to(edge_ref, came_ref, bulk, 2, right)
+
+    def unsort():
+        for copy in copies:
+            copy.start()
+        for k, img_ref in enumerate((imga_ref, imgb_ref)):
+
+            def one(r, carry, k=k, img_ref=img_ref):
+                at = pl.ds(pl.multiple_of(k * half + r * ROWS, ROWS), ROWS)
+                rank = rank_ref[0:1, at].astype(jnp.int32)
+                mine = img_ref[:, pl.ds(pl.multiple_of(r * ROWS, ROWS), ROWS)]
+                lhs = jnp.concatenate(two(mine), axis=0)
+                got = jnp.zeros((2 * ens, ROWS), f32)
+                for c in range(ROWS // 256):
+                    slot = lax.broadcasted_iota(jnp.int32, (256, ROWS), 0) + c * 256
+                    place = (slot == rank).astype(f32).astype(bf16)
+                    got = got + dot(lhs[:, c * 256 : (c + 1) * 256], place)
+                image = got[:ens] + got[ens:]
+                back_ref[:, at] = image
+                scaled_ref[:, at] = jnp.concatenate(two(image * gain_ref[:, at]), axis=0)
+                return carry
+
+            lax.fori_loop(0, half // ROWS, one, 0)
+
+    def outer():
+        add_columns(scaled_ref, owner_ref, me, total, COLS_DEV, edge_ref)
+        edge.start()
+
+    def inner():
+        add_columns(scaled_ref, owner_ref, me, total, 0, cols_ref)
+
+    out_ref[...] = sum_all(partners, x_ref, send, recv, (send_sem, recv_sem), [unsort, outer, inner])
+    for copy in copies + [edge]:
+        copy.wait()
+
+
+def join_second_kernel(
+    steps,
+    total,
+    n_col,
+    count_ref,
+    x_ref,
+    innov_ref,
+    gain_ref,
+    owner_ref,
+    out_ref,
+    cols_ref,
+    came_ref,
+    scaled_ref,
+    edge_ref,
+    send,
+    recv,
+    send_sem,
+    recv_sem,
+    bulk_send_sem,
+    bulk_recv_sem,
+):
+    own = innov_ref.shape[1]
+    me, left, right = ring(total, n_col)
+    partners = partners_of(steps, n_col, me)
+    everyone = [other for group in partners for other in group] + [left, right]
+    greet(everyone)
+    pl.semaphore_wait(pltpu.get_barrier_semaphore(), len(everyone))
+    edge = send_to(edge_ref, came_ref, (bulk_send_sem, bulk_recv_sem), 0, right)
+
+    def scale():
+        def one(g, carry):
+            at = pl.ds(pl.multiple_of(g * ROWS, ROWS), ROWS)
+            factor = gain_ref[:, at] * live_row(count_ref, g)
+            scaled_ref[:, at] = jnp.concatenate(two(innov_ref[:, at] * factor), axis=0)
+            return carry
+
+        lax.fori_loop(0, own // ROWS, one, 0)
+
+    def outer():
+        add_columns(scaled_ref, owner_ref, me, total, COLS_DEV, edge_ref)
+        edge.start()
+
+    def inner():
+        add_columns(scaled_ref, owner_ref, me, total, 0, cols_ref)
+
+    out_ref[...] = sum_all(partners, x_ref, send, recv, (send_sem, recv_sem), [scale, outer, inner])
+    edge.wait()
+
+
+def join_scratch(steps, shape, ens, own, bulk):
+    slots = sum(2 ** len(amounts) - 1 for amounts in steps)
+    return [
+        pltpu.VMEM((2 * ens, own), bf16),
+        pltpu.VMEM((ens, COLS_DEV), f32),
+        pltpu.VMEM((len(steps),) + shape, f32),
+        pltpu.VMEM((slots,) + shape, f32),
+        pltpu.SemaphoreType.DMA((slots,)),
+        pltpu.SemaphoreType.DMA((slots,)),
+        pltpu.SemaphoreType.DMA((bulk,)),
+        pltpu.SemaphoreType.DMA((bulk,)),
+    ]
+
+
+def join_first(x, imga, imgb, rank, gain, owner):
+    ens, half = imga.shape
+    total, n_col = sizes()
+    steps = exchange_steps(total)
+    halo = jax.ShapeDtypeStruct((ens, half), f32)
+    cols = jax.ShapeDtypeStruct((ens, COLS_DEV), f32)
     return pl.pallas_call(
-        functools.partial(reduce_kernel, steps, n_col),
-        out_shape=jax.ShapeDtypeStruct(x.shape, f32),
-        in_specs=[vmem],
-        out_specs=vmem,
-        scratch_shapes=[
-            pltpu.VMEM((len(steps),) + x.shape, f32),
-            pltpu.VMEM((slots,) + x.shape, f32),
-            pltpu.SemaphoreType.DMA((slots,)),
-            pltpu.SemaphoreType.DMA((slots,)),
-        ],
-        compiler_params=pltpu.CompilerParams(collective_id=which, has_side_effects=True),
-        name="sum_all",
-    )(x)
+        functools.partial(join_first_kernel, steps, total, n_col),
+        out_shape=(
+            jax.ShapeDtypeStruct(x.shape, f32),
+            halo,
+            halo,
+            jax.ShapeDtypeStruct((ens, 2 * half), f32),
+            cols,
+            cols,
+        ),
+        in_specs=[vmem] * 6,
+        out_specs=(vmem, anywhere, anywhere, vmem, vmem, anywhere),
+        scratch_shapes=join_scratch(steps, x.shape, ens, 2 * half, 3),
+        compiler_params=comm_params(1),
+        name="join_first",
+    )(x, imga, imgb, rank, gain, owner)
+
+
+def join_second(count, x, innov, gain, owner):
+    ens, own = innov.shape
+    total, n_col = sizes()
+    steps = exchange_steps(total)
+    cols = jax.ShapeDtypeStruct((ens, COLS_DEV), f32)
+    return pl.pallas_call(
+        functools.partial(join_second_kernel, steps, total, n_col),
+        out_shape=(jax.ShapeDtypeStruct(x.shape, f32), cols, cols),
+        in_specs=[smem] + [vmem] * 4,
+        out_specs=(vmem, vmem, anywhere),
+        scratch_shapes=join_scratch(steps, x.shape, ens, own, 1),
+        compiler_params=comm_params(2),
+        name="join_second",
+    )(count, x, innov, gain, owner)
 
 
 def symmetric(matrix):
@@ -683,99 +919,20 @@
     )(grams, step0, inv0, curv0)
 
 
-def add_columns(stack, owner, cols_ref):
-    ens = cols_ref.shape[0]
-    for c in range(2 * COLS_DEV // 256):
-        slot = lax.broadcasted_iota(jnp.int32, (256, ROWS), 0) + c * 256
-        hot = (slot == owner).astype(f32).astype(bf16)
-        got = dot(stack, hot, NT)
-        part = slice(c * 256, (c + 1) * 256)
-        cols_ref[:, part] += got[:ens] + got[ens:]
-
-
-def innov_columns_kernel(innov_ref, info_ref, cols_ref):
-    cols_ref[...] = jnp.zeros_like(cols_ref)
-
-    def one(g, carry):
-        at = pl.ds(pl.multiple_of(g * ROWS, ROWS), ROWS)
-        scale = info_ref[0:1, at] * info_ref[1:2, at]
-        owner = info_ref[2:3, at].astype(jnp.int32)
-        add_columns(jnp.concatenate(two(innov_ref[:, at] * scale), axis=0), owner, cols_ref)
-        return carry
-
-    lax.fori_loop(0, innov_ref.shape[1] // ROWS, one, 0)
-
-
-def columns_kernel(info_ref, rank_ref, imga_ref, imgb_ref, back_ref, cols_ref):
-    ens, own = back_ref.shape
-    half = own // 2
-    cols_ref[...] = jnp.zeros_like(cols_ref)
-    for g in range(own // ROWS):
-        at = slice(g * ROWS, (g + 1) * ROWS)
-        rank = rank_ref[0:1, at].astype(jnp.int32)
-        img_ref = imga_ref if g * ROWS < half else imgb_ref
-        begin = (g * ROWS) % half
-        lhs = jnp.concatenate(two(img_ref[:, begin : begin + ROWS]), axis=0)
-        total = jnp.zeros((2 * ens, ROWS), f32)
-        for c in range(ROWS // 256):
-            slot = lax.broadcasted_iota(jnp.int32, (256, ROWS), 0) + c * 256
-            place = (slot == rank).astype(f32).astype(bf16)
-            total = total + dot(lhs[:, c * 256 : (c + 1) * 256], place)
-        image = total[:ens] + total[ens:]
-        back_ref[:, at] = image
-        owner = info_ref[2:3, at].astype(jnp.int32)
-        add_columns(jnp.concatenate(two(image * info_ref[0:1, at]), axis=0), owner, cols_ref)
-
-
-def innov_columns_call(innov, info):
-    ens, own = innov.shape
-    return pl.pallas_call(
-        innov_columns_kernel,
-        out_shape=jax.ShapeDtypeStruct((ens, 2 * COLS_DEV), f32),
-        in_specs=[vmem] * 2,
-        out_specs=vmem,
-        compiler_params=params(),
-        cost_estimate=pl.CostEstimate(
-            flops=2 * 256 * own * 2048, bytes_accessed=4 << 20, transcendentals=0
-        ),
-        name="innov_columns",
-    )(innov, info)
-
-
-def columns_call(info, rank, imga, imgb):
-    ens, half = imga.shape
-    return pl.pallas_call(
-        columns_kernel,
-        out_shape=(
-            jax.ShapeDtypeStruct((ens, 2 * half), f32),
-            jax.ShapeDtypeStruct((ens, 2 * COLS_DEV), f32),
-        ),
-        in_specs=[vmem] * 4,
-        out_specs=(vmem, vmem),
-        compiler_params=params(),
-        cost_estimate=pl.CostEstimate(
-            flops=2 * 256 * 2 * half * 3072, bytes_accessed=4 << 20, transcendentals=0
-        ),
-        name="columns",
-    )(info, rank, imga, imgb)
-
-
-def final_kernel(coef_ref, innov_ref, info_ref, back_ref, rc_ref, rin_ref, ic_ref, iin_ref, w_ref, inc_ref):
+def final_kernel(count_ref, coef_ref, innov_ref, back_ref, rc_ref, rin_ref, ic_ref, iin_ref, w_ref, inc_ref):
     coef = coef_ref[...]
     ens = coef.shape[0]
-    own = innov_ref.shape[1]
-    chunk = 1024
     first, second = coef[:, :ens], coef[:, ens:]
-    for c in range(own // chunk):
-        at = pl.ds(c * chunk, chunk)
-        live = info_ref[1:2, at]
+    for g in range(innov_ref.shape[1] // ROWS):
+        at = pl.ds(g * ROWS, ROWS)
+        live = live_row(count_ref, g)
         w_ref[:, at] = combine(first, innov_ref[:, at] * live) + combine(second, back_ref[:, at])
-    inc_ref[...] = combine(first, rc_ref[:, :COLS_DEV] + rin_ref[...]) + combine(
-        second, ic_ref[:, :COLS_DEV] + iin_ref[...]
+    inc_ref[...] = combine(first, rc_ref[...] + rin_ref[...]) + combine(
+        second, ic_ref[...] + iin_ref[...]
     )
 
 
-def final_call(coef, innov, info, back, *cols):
+def final_call(count, coef, innov, back, *cols):
     ens, own = innov.shape
     return pl.pallas_call(
         final_kernel,
@@ -783,11 +940,11 @@
             jax.ShapeDtypeStruct((ens, own), f32),
             jax.ShapeDtypeStruct((ens, COLS_DEV), f32),
         ),
-        in_specs=[vmem] * 8,
+        in_specs=[smem] + [vmem] * 7,
         out_specs=(vmem, vmem),
         compiler_params=params(),
         name="final",
-    )(coef, innov, info, back, *cols)
+    )(count, coef, innov, back, *cols)
 
 
 def on_device(
@@ -801,41 +958,18 @@
     obs_count,
     col_owner,
 ):
-    axes = ("reg", "col")
     ens, own = innovation.shape
-    live = (
-        (jnp.arange(ROWS, dtype=jnp.int32)[None, :] < obs_count[:, None])
-        .astype(f32)
-        .reshape(own)
-    )
-    flags = jnp.repeat(pair_live.astype(f32).T, ROWS, axis=1)
-    zero = jnp.zeros((own,), f32)
-    meta = jnp.stack(
-        [obs_along, obs_across, obs_scale * live, obs_error, flags[0], flags[1]]
-        + [jnp.where(live > 0.5, obs_across, DEAD)]
-        + [zero] * (META - 7)
-    )
-    total_cols = COLS_DEV * lax.axis_size(axes)
-    local_col = (col_owner - lax.axis_index(axes) * COLS_DEV) % total_cols
-    info = jnp.stack([obs_gain, live, local_col.astype(f32)] + [zero] * 5)
-
-    first, last, rank = sort_call(innovation, meta)
-    after = shift(first, -1)
-    before = shift(last, 1)
+    rows = [x.reshape(1, own) for x in (obs_along, obs_across, obs_scale, obs_error)]
+    gain, owner = obs_gain.reshape(1, own), col_owner.reshape(1, own)
+    first, last, before, after, rank = sort_call(obs_count, pair_live, innovation, *rows)
     chunks = [before, first, last, after]
-    innov_cols = innov_columns_call(innovation, info)
-    innov_came = shift(innov_cols[:, COLS_DEV:], 1)
     imga, imgb, grams, *plan = first_call(chunks, ens, own)
-    img_after = shift(imga, -1)
-    img_before = shift(imgb, 1)
-    step0, inv0, curv0 = solve_first(sum_all(grams, 0))
-    back, img_cols = columns_call(info, rank, imga, imgb)
-    img_came = shift(img_cols[:, COLS_DEV:], 1)
+    grams, img_before, img_after, back, ic, iin = join_first(grams, imga, imgb, rank, gain, owner)
+    step0, inv0, curv0 = solve_first(grams)
     grams = second_call(plan, step0, chunks, [img_before, imga, imgb, img_after], ens, own)
-    coef = solve_second(sum_all(grams, 1), step0, inv0, curv0)
-    return tuple(
-        final_call(coef, innovation, info, back, innov_cols, innov_came, img_cols, img_came)
-    )
+    grams, rc, rin = join_second(obs_count, grams, innovation, gain, owner)
+    coef = solve_second(grams, step0, inv0, curv0)
+    return tuple(final_call(obs_count, coef, innovation, back, rc, rin, ic, iin))
 
 
 def solution(mesh):

time: 126 us -> 118 us (0.937)
  Pallas kernels: 101 us -> 115 us
  starting transfers between devices: 11.9 us -> 0 us
  local copies, waits for them, and re-layouts: 10.6 us -> 1.33 us
    pallas_call x5 -> x3, Pallas kernels: 55.5 us -> 71.8 us  [the longest x1 32 us: join_first(): pl.pallas_call(functools.partial(join_first_kernel, steps, total, n_col),...]
    ppermute x6 -> x0, starting transfers between devices: 11.9 us -> none  [shift(): lax.ppermute(block, axis, [((i - distance) % n, i) for i in range(n)])]
    unnamed x30 -> x3, local copies, waits for them, and re-layouts: 6.33 us -> 1.33 us
    another operation x5 -> x0, local copies, waits for them, and re-layouts: 2.31 us -> none  [the longest x2 1.51 us: on_device(): jnp.stack([obs_along, obs_across, obs_scale * live, obs_error, flags[0],...]
    slice x3 -> x0, local copies, waits for them, and re-layouts: 1.94 us -> none  [the longest x1 0.97 us: on_device(): innov_came = shift(innov_cols[:, COLS_DEV:], 1)]
    pallas_call x1, Pallas kernels: 16.5 us -> 15 us  [first_call(): pl.pallas_call(first_kernel, out_shape=(half, half, jax.ShapeDtypeStruct(...]
    pallas_call x1, Pallas kernels: 17.3 us -> 16 us  [second_call(): pl.pallas_call(second_kernel, out_shape=jax.ShapeDtypeStruct((ens + 8, 2...]
  transfers between devices with their start and end apart: 6 -> 0, of which waited for: 0 -> 0; matrix products, arithmetic and copies ran while one was open for 2% -> 0% of each run, Pallas kernels for 73% -> 0%
where the time goes in v3:
time: 118 us; the launch traced here: 117 us
  Pallas kernels  115 us (97%)
  local copies, waits for them, and re-layouts  1.33 us (1%)
    pallas_call x1, Pallas kernels, join_first(): pl.pallas_call(functools.partial(join_first_kernel, steps, total, n_col),...  32 us
    pallas_call x1, Pallas kernels, sort_call(): pl.pallas_call(functools.partial(sort_kernel, *sizes()), out_shape=(half,...  21.9 us
    pallas_call x1, Pallas kernels, join_second(): pl.pallas_call(functools.partial(join_second_kernel, steps, total, n_col)...  17.9 us
    pallas_call x1, Pallas kernels, second_call(): pl.pallas_call(second_kernel, out_shape=jax.ShapeDtypeStruct((ens + 8, 2...  16 us
    pallas_call x1, Pallas kernels, first_call(): pl.pallas_call(first_kernel, out_shape=(half, half, jax.ShapeDtypeStruct(...  15 us
    pallas_call x1, Pallas kernels, solve_second(): pl.pallas_call(solve_second_kernel, out_shape=jax.ShapeDtypeStruct((ens,...  4.37 us
    pallas_call x1, Pallas kernels, solve_first(): pl.pallas_call(solve_first_kernel, out_shape=(small, small, small), in_sp...  3.76 us
    pallas_call x1, Pallas kernels, final_call(): pl.pallas_call(final_kernel, out_shape=(jax.ShapeDtypeStruct((ens, own),...  3.69 us

profile of v3, /device:TPU:0, one launch (start us, length us, event | category | flops | bytes accessed | tf_op | source)
XLA Modules:
  0.0 116.7 jit_solution(8473976971353961123)
XLA Ops:
  0.6 0.0 copy-start
  0.6 0.7 copy-done
  1.3 0.7 copy.11.pair_ref
  2.0 21.9 %sort_slots.1 = (f32[72,2048]{1,0:T(8,128)}, f32[72,2048]{1,0:T(8,128)}, f32[72,2048]{1,0:T(8,128)}, f32[72,2048]{1,0:T(8,128)}, f32[8,4096]{1,0:T(8,128)}) custom-call(s32[4]{0:T(128)} %count_ref.5, s32[4,2]{1,0:T(4,128)} %copy.11.pair_ref, f32[64,4096]{1,0:T(8,128)} %innov_ref.5, f32[1,4096]{1,0:T(1,128)} %bitcast.10, f32[1,4096]{1,0:T(1,128)} %bitcast.11, ...), custom_call_target="tpu_custom_call" | custom-call | tf_op jit(solution)/shard_map/sort_slots/pallas_call | solution.py:179
  23.9 15.0 %operate_first.1 = (f32[64,2048]{1,0:T(8,128)}, f32[64,2048]{1,0:T(8,128)}, f32[40,128]{1,0:T(8,128)}, s32[72,128]{1,0:T(8,128)}, s32[3,9,128]{2,1,0:T(8,128)}) custom-call(f32[72,2048]{1,0:T(8,128)} %get-tuple-element.24.c0, f32[72,2048]{1,0:T(8,128)} %get-tuple-element.25.c1, f32[72,2048]{1,0:T(8,128)} %get-tuple-element.26.c2, ...), custom_call_target="tpu_custom_call" | custom-call | tf_op jit(solution)/shard_map/operate_first/pallas_call | solution.py:561
  38.9 32.0 %join_first.1 = (f32[40,128]{1,0:T(8,128)}, f32[64,2048]{1,0:T(8,128)}, f32[64,2048]{1,0:T(8,128)}, f32[64,4096]{1,0:T(8,128)}, f32[64,1024]{1,0:T(8,128)}, /*index=5*/f32[64,1024]{1,0:T(8,128)}) custom-call(f32[40,128]{1,0:T(8,128)} %get-tuple-element.30.x_ref, f32[64,2048]{1,0:T(8,128)} %get-tuple-element.31.imga_ref.i1, ...), custom_call_target="tpu_custom_call" | custom-call | tf_op jit(solution)/shard_map/join_first/pallas_call | solution.py:798
  70.9 3.8 %solve_first.1 = (f32[64,64]{1,0:T(8,128)}, f32[64,64]{1,0:T(8,128)}, f32[64,64]{1,0:T(8,128)}) custom-call(f32[40,128]{1,0:T(8,128)} %get-tuple-element.34.gram_ref), custom_call_target="tpu_custom_call" | custom-call | tf_op jit(solution)/shard_map/solve_first/pallas_call | solution.py:902
  74.7 16.0 %operate_second.1.x_ref = f32[72,128]{1,0:T(8,128)} custom-call(s32[72,128]{1,0:T(8,128)} %get-tuple-element.28.span_in, s32[3,9,128]{2,1,0:T(8,128)} %get-tuple-element.29.item_in, f32[64,64]{1,0:T(8,128)} %get-tuple-element.35.step_ref, f32[72,2048]{1,0:T(8,128)} %get-tuple-element.24.c0, f32[72,2048]{1,0:T(8,128)} %get-tuple-element.25.c1, ...), custom_call_target="tpu_custom_call" | custom-call | tf_op jit(solution)/shard_map/operate_second/pallas_call | solution.py:579
  90.7 17.9 %join_second.1 = (f32[72,128]{1,0:T(8,128)}, f32[64,1024]{1,0:T(8,128)}, f32[64,1024]{1,0:T(8,128)}) custom-call(s32[4]{0:T(128)} %count_ref.5, f32[72,128]{1,0:T(8,128)} %operate_second.1.x_ref, f32[64,4096]{1,0:T(8,128)} %innov_ref.5, f32[1,4096]{1,0:T(1,128)} %bitcast.7, s32[1,4096]{1,0:T(1,128)} %bitcast.9), custom_call_target="tpu_custom_call" | custom-call | tf_op jit(solution)/shard_map/join_second/pallas_call | solution.py:821
  108.6 4.4 %solve_second.1.coef_ref = f32[64,128]{1,0:T(8,128)} custom-call(f32[72,128]{1,0:T(8,128)} %get-tuple-element.38.gram_ref, f32[64,64]{1,0:T(8,128)} %get-tuple-element.35.step_ref, f32[64,64]{1,0:T(8,128)} %get-tuple-element.39.inv_ref, f32[64,64]{1,0:T(8,128)} %get-tuple-element.40.curv_ref), custom_call_target="tpu_custom_call" | custom-call | tf_op jit(solution)/shard_map/solve_second/pallas_call | solution.py:913
  113.0 3.7 %final.1 = (f32[64,4096]{1,0:T(8,128)}, f32[64,1024]{1,0:T(8,128)}) custom-call(s32[4]{0:T(128)} %count_ref.5, f32[64,128]{1,0:T(8,128)} %solve_second.1.coef_ref, f32[64,4096]{1,0:T(8,128)} %innov_ref.5, f32[64,4096]{1,0:T(8,128)} %get-tuple-element.41.back_ref, f32[64,1024]{1,0:T(8,128)} %get-tuple-element.42.rc_ref, ...), custom_call_target="tpu_custom_call" | custom-call | tf_op jit(solution)/shard_map/final/pallas_call | solution.py:937
Async XLA Ops:
  0.6 0.7 copy-start

commit v4 on v3

--- a/solution.py
+++ b/solution.py
@@ -17,7 +17,9 @@
 EMPTY = ROWS // STEP
 DEAD = 1e9
 FAR = 1e6
-VMEM_LIMIT = 60 * 1024 * 1024
+VMEM_LIMIT = 24 * 1024 * 1024
+SORT_LIMIT = 60 * 1024 * 1024
+KEEP = 128
 
 highest = lax.Precision.HIGHEST
 f32 = jnp.float32
@@ -30,6 +32,12 @@
 anywhere = pl.BlockSpec(memory_space=pl.ANY)
 
 
+def shift(block, distance):
+    axis = ("reg", "col")
+    n = lax.axis_size(axis)
+    return lax.ppermute(block, axis, [((i - distance) % n, i) for i in range(n)])
+
+
 def dot(a, b, dims=NN):
     return lax.dot_general(a, b, dims, preferred_element_type=f32)
 
@@ -87,8 +95,6 @@
 
 
 def sort_kernel(
-    total,
-    n_col,
     count_ref,
     pair_ref,
     innov_ref,
@@ -98,17 +104,11 @@
     error_ref,
     first_ref,
     last_ref,
-    before_ref,
-    after_ref,
     rank_ref,
-    send_sem,
-    recv_sem,
 ):
     regions = innov_ref.shape[1] // ROWS
     sub = lax.broadcasted_iota(jnp.int32, (128, 128), 0)
     lane = lax.broadcasted_iota(jnp.int32, (128, 128), 1)
-    _, left, right = ring(total, n_col)
-    greet([left, right])
 
     def sort_region(out_ref, shift_by, r, carry):
         g = shift_by + r
@@ -116,7 +116,7 @@
         live = live_row(count_ref, g)
         across = across_ref[:, cols]
         key = jnp.where(live > 0.5, across, DEAD)
-        flags = [jnp.full((1, ROWS), pair_ref[g, d], jnp.int32).astype(f32) for d in range(REACH)]
+        flags = [jnp.full((1, ROWS), pair_ref[d, g], jnp.int32).astype(f32) for d in range(REACH)]
         meta = [along_ref[:, cols], across, scale_ref[:, cols] * live, error_ref[:, cols]]
         stack = jnp.concatenate(
             [innov_ref[:, cols] * live] + meta + flags + [key, jnp.zeros((1, ROWS), f32)], axis=0
@@ -151,15 +151,7 @@
 
     half = regions // 2
     lax.fori_loop(0, half, functools.partial(sort_region, first_ref, 0), 0)
-    pl.semaphore_wait(pltpu.get_barrier_semaphore(), 2)
-    sems = (send_sem, recv_sem)
-    back = send_to(first_ref, after_ref, sems, 0, left)
-    back.start()
     lax.fori_loop(0, half, functools.partial(sort_region, last_ref, half), 0)
-    ahead = send_to(last_ref, before_ref, sems, 1, right)
-    ahead.start()
-    back.wait()
-    ahead.wait()
 
 
 def sizes():
@@ -177,17 +169,16 @@
     ens, n = innov.shape
     half = jax.ShapeDtypeStruct((ens + 8, n // 2), f32)
     return pl.pallas_call(
-        functools.partial(sort_kernel, *sizes()),
-        out_shape=(half,) * 4 + (jax.ShapeDtypeStruct((8, n), f32),),
+        sort_kernel,
+        out_shape=(half, half, jax.ShapeDtypeStruct((8, n), f32)),
         in_specs=[smem] * 2 + [vmem] * 5,
-        out_specs=(vmem, vmem, anywhere, anywhere, vmem),
-        scratch_shapes=[pltpu.SemaphoreType.DMA((2,)), pltpu.SemaphoreType.DMA((2,))],
-        compiler_params=comm_params(0),
+        out_specs=(vmem,) * 3,
+        compiler_params=pltpu.CompilerParams(vmem_limit_bytes=SORT_LIMIT),
         name="sort_slots",
     )(count, pair, innov, *rows)
 
 
-def lay_grid(chunks, row_ref, grid_ref):
+def lay_grid(chunks, offsets, row_ref, grid_ref):
     width = chunks[0].shape[1]
     per = width // ROWS
     blocks = ROWS // 128
@@ -197,7 +188,7 @@
         for r in range(per):
             h = c * per + r
             at = slice(h * ROWS, (h + 1) * ROWS)
-            row_ref[0:1, at] = row_ref[0:1, at] + float(h)
+            row_ref[0:1, at] = row_ref[0:1, at] + float(offsets[h])
             for q, source in enumerate((0, 1, 6)):
                 for b in range(blocks):
                     line = h * (blocks + 1) + b
@@ -205,10 +196,8 @@
                     grid_ref[q, line : line + 1, :] = row_ref[source : source + 1, begin : begin + 128]
 
 
-def lay_tables(grid_ref, table_refs, spread_refs):
-    own = spread_refs[0].shape[0]
-    blocks = ROWS // 128
-    count = (own // ROWS + 2 * REACH) * (blocks + 1)
+def lay_tables(grid_ref, regions, table_refs):
+    count = regions * (ROWS // 128 + 1)
     ways = 128 // STEP
     lane = lax.broadcasted_iota(jnp.int32, (count, 128), 1)
     for q in range(2):
@@ -218,27 +207,55 @@
         for k in range(1, ways):
             joined = jnp.where(lane < k * STEP, later, here)
             table_refs[q][pl.ds(k, count, stride=ways), :] = pltpu.roll(joined, 128 - k * STEP, 1)
-        turned = jnp.concatenate([here, jnp.zeros((128 - count, 128), f32)], axis=0).T
-        for g in range(own // ROWS):
+
+
+def spread_rows(grid_ref, spread_refs):
+    blocks = ROWS // 128
+    regions = spread_refs[0].shape[0] // ROWS
+    count = regions * (blocks + 1)
+    for q in range(2):
+        turned = jnp.concatenate(
+            [grid_ref[q, :count, :], jnp.zeros((128 - count, 128), f32)], axis=0
+        ).T
+        for g in range(regions):
             for b in range(blocks):
-                line = (g + REACH) * (blocks + 1) + b
+                line = g * (blocks + 1) + b
                 begin = g * ROWS + b * 128
                 spread_refs[q][begin : begin + 128, :] = jnp.broadcast_to(
                     turned[:, line : line + 1], (128, 128)
                 )
 
 
-def plan_windows(row_ref, grid_ref, span_ref, item_ref):
+def own_pairs(regions):
+    near = range(-REACH, REACH + 1)
+    return [[(g + d, d) for d in near if 0 <= g + d < regions] for g in range(regions)]
+
+
+def halo_pairs(regions):
+    found = []
+    for g in range(regions):
+        mine = [(g + d + REACH, d) for d in range(-REACH, 0) if g + d < 0]
+        mine += [(g + d - regions + REACH, d) for d in range(1, REACH + 1) if g + d >= regions]
+        found.append(mine)
+    return found
+
+
+def widest(pairs):
+    return max(len(mine) for mine in pairs)
+
+
+def plan_windows(pairs, row_ref, grid_ref, row_i_ref, grid_i_ref, span_ref, item_ref):
     blocks = ROWS // 128
-    regions = row_ref.shape[1] // ROWS - 2 * REACH
+    regions = len(pairs)
     per = ROWS // TILE
     tiles = regions * per
     ways = 128 // STEP
-    offsets = 2 * REACH + 1
-    keys = [
-        grid_ref[2, h * (blocks + 1) : h * (blocks + 1) + blocks, :] for h in range(regions + 2 * REACH)
-    ]
-    mine = jnp.concatenate(keys[REACH : REACH + regions], axis=0)
+    slots = widest(pairs)
+
+    def keys_of(ref, count):
+        return [ref[2, h * (blocks + 1) : h * (blocks + 1) + blocks, :] for h in range(count)]
+
+    mine = jnp.concatenate(keys_of(grid_i_ref, regions), axis=0)
     top = jnp.where(mine < 0.5 * DEAD, mine, -DEAD)
     size = 1
     while size < TILE:
@@ -261,7 +278,7 @@
         )
     under, over = first - 1.001, last + 1.001
     begins, ends = [], []
-    for key in keys:
+    for key in keys_of(grid_ref, row_ref.shape[1] // ROWS):
         begin = jnp.zeros((blocks, tiles), f32)
         end = jnp.zeros((blocks, tiles), f32)
         for k in range(ways):
@@ -275,18 +292,19 @@
     alive = first < 0.5 * DEAD
     starts, stops = [], []
     needs = jnp.zeros((1, tiles), f32)
-    for dh in range(offsets):
-        d = dh - REACH
+    for slot in range(slots):
         start = jnp.zeros((1, tiles), f32)
         stop = jnp.zeros((1, tiles), f32)
-        for g in range(regions):
-            h = g + dh
-            base = float(h * (ROWS + 128) // STEP)
-            begin, end = begins[h] + base, ends[h] + base
+        for g, mine in enumerate(pairs):
+            if slot >= len(mine):
+                continue
+            j, d = mine[slot]
+            base = float(j * (ROWS + 128) // STEP)
+            begin, end = begins[j] + base, ends[j] + base
             if d:
                 source = 3 + abs(d)
-                owner = (g + REACH if d > 0 else h) * ROWS
-                flag = row_ref[source : source + 1, owner : owner + 128]
+                owner, holder = (g, row_i_ref) if d > 0 else (j, row_ref)
+                flag = holder[source : source + 1, owner * ROWS : owner * ROWS + 128]
                 end = jnp.where(flag[:, :tiles] > 0.5, end, begin)
             start = jnp.where(group == g, begin, start)
             stop = jnp.where(group == g, end, stop)
@@ -294,7 +312,7 @@
         needs = jnp.maximum(needs, jnp.floor((stop - start + (ways - 1.0)) * (1.0 / ways)))
         starts.append(start)
         stops.append(stop)
-    blank = jnp.full((8 - offsets, tiles), float(EMPTY), f32)
+    blank = jnp.full((8 - slots, tiles), float(EMPTY), f32)
     for m in range(blocks + 1):
         lines_m = [
             jnp.where(start + float(ways * m) < stop, start + float(ways * m), float(EMPTY))
@@ -332,56 +350,85 @@
         turn_ref[h * padded + ROWS : (h + 1) * padded, :] = jnp.zeros((128, 2 * ens), bf16)
 
 
-def apply_cov(
-    span_ref, item_ref, row_ref, table_refs, spread_refs, v_ref, img_ref, turn_ref, sum_ref, s_ref
-):
-    ens, wide = v_ref.shape
-    own = img_ref.shape[1]
-    lead = REACH * ROWS
-    s_ref[...] = jnp.zeros_like(s_ref)
-    sum_ref[...] = jnp.zeros_like(sum_ref)
-
-    def windows(n):
-        line, lane = lax.shift_right_logical(n, jnp.int32(7)), lax.bitwise_and(n, jnp.int32(127))
-        tile = item_ref[0, line, lane]
-        level = item_ref[1, line, lane] * 8
-        return [tile] + [span_ref[level + dh, tile] for dh in range(2 * REACH + 1)]
+def windows(work, n, slots):
+    line, lane = lax.shift_right_logical(n, jnp.int32(7)), lax.bitwise_and(n, jnp.int32(127))
+    tile = work["item"][0, line, lane]
+    level = work["item"][1, line, lane] * 8
+    return [tile] + [work["span"][level + slot, tile] for slot in range(slots)]
+
+
+def gather(work, cov, where_to):
+    tile, *found = where_to
+    turn_ref = work["turn"]
+    rhs = jnp.concatenate(
+        [turn_ref[pl.ds(pl.multiple_of(w * STEP, STEP), 128), :] for w in found], axis=0
+    )
+    got = dot(cov, rhs)
+    at = pl.ds(pl.multiple_of(tile * TILE, TILE), TILE)
+    work["sum"][at, :] += got[:TILE] + got[TILE:]
+
+
+def count_trips(work):
+    return lax.shift_right_logical(
+        work["item"][2, 0, 0] + (PAIR - 1), jnp.int32(PAIR.bit_length() - 1)
+    )
+
+
+def apply_cov(work, s_ref, keep, begin):
+    slots = s_ref.shape[2] // 128
+    s_ref[keep : keep + PAIR] = jnp.zeros((PAIR,) + s_ref.shape[1:], bf16)
+
+    def place(k):
+        return jnp.where(k < keep // PAIR, k * PAIR, keep)
 
     def step(k, carry):
+        before = jnp.where(k == begin, keep, place(k - 1))
         for p in range(PAIR):
-            tile, *found = carry[p]
-            rhs = jnp.concatenate(
-                [turn_ref[pl.ds(pl.multiple_of(w * STEP, STEP), 128), :] for w in found], axis=0
-            )
-            got = dot(s_ref[p], rhs)
-            at = pl.ds(pl.multiple_of(tile * TILE, TILE), TILE)
-            sum_ref[at, :] += got[:TILE] + got[TILE:]
-        now = [windows(k * PAIR + p) for p in range(PAIR)]
+            gather(work, s_ref[before + p], carry[p])
+        now = [windows(work, k * PAIR + p, slots) for p in range(PAIR)]
+        after = place(k)
         for p in range(PAIR):
             tile, *found = now[p]
             at = pl.ds(pl.multiple_of(tile * TILE, TILE), TILE)
-            a_i = spread_refs[0][at, :]
-            b_i = spread_refs[1][at, :]
+            a_i = work["along_i"][at, :]
+            b_i = work["across_i"][at, :]
             for d, w in enumerate(found):
-                da = table_refs[0][pl.ds(w, 1), :] - a_i
-                db = table_refs[1][pl.ds(w, 1), :] - b_i
+                da = work["along"][pl.ds(w, 1), :] - a_i
+                db = work["across"][pl.ds(w, 1), :] - b_i
                 r2 = da * da + db * db
                 r = r2 * lax.rsqrt(jnp.maximum(r2, 1e-30))
                 u = jnp.maximum(1.0 - r, 0.0)
                 u2 = u * u
                 hi, lo = two((u2 * u2) * (r + 0.25))
-                s_ref[p, 0:TILE, d * 128 : (d + 1) * 128] = hi
-                s_ref[p, TILE : 2 * TILE, d * 128 : (d + 1) * 128] = lo
+                s_ref[after + p, 0:TILE, d * 128 : (d + 1) * 128] = hi
+                s_ref[after + p, TILE : 2 * TILE, d * 128 : (d + 1) * 128] = lo
         return now
 
-    trips = lax.shift_right_logical(item_ref[2, 0, 0] + (PAIR - 1), jnp.int32(PAIR.bit_length() - 1))
-    lax.fori_loop(0, trips + 1, step, [windows(p) for p in range(PAIR)])
+    trips = count_trips(work)
+    end = jnp.where(trips > begin, trips + 1, begin)
+    lax.fori_loop(begin, end, step, [windows(work, p, slots) for p in range(PAIR)])
+
+
+def apply_kept(work, kept_ref, ring_ref):
+    slots = kept_ref.shape[2] // 128
+    most = KEEP // PAIR
+
+    def step(k, carry):
+        for p in range(PAIR):
+            gather(work, kept_ref[k * PAIR + p], windows(work, k * PAIR + p, slots))
+        return carry
+
+    lax.fori_loop(0, jnp.minimum(count_trips(work), most), step, 0)
+    apply_cov(work, ring_ref, 0, most)
+
+
+def finish(sum_ref, base_ref, row_ref, v_ref, img_ref):
+    ens, own = img_ref.shape
     for c in range(own // 128):
         at = slice(c * 128, (c + 1) * 128)
-        e_at = slice(lead + c * 128, lead + (c + 1) * 128)
-        turned = sum_ref[at, :].T
+        turned = (sum_ref[at, :] + base_ref[at, :]).T
         img_ref[:, at] = (
-            (turned[:ens] + turned[ens:]) * (row_ref[2:3, e_at] * 0.25) + row_ref[3:4, e_at] * v_ref[:, e_at]
+            (turned[:ens] + turned[ens:]) * (row_ref[2:3, at] * 0.25) + row_ref[3:4, at] * v_ref[:, at]
         )
 
 
@@ -413,54 +460,102 @@
     return jnp.where(col >= row, packed, other), lower
 
 
-def first_kernel(
-    c0,
-    c1,
-    c2,
-    c3,
+def start_plan(span_in, item_in, work):
+    copies = [
+        pltpu.make_async_copy(span_in, work["span"], work["plan_sem"].at[0]),
+        pltpu.make_async_copy(item_in, work["item"], work["plan_sem"].at[1]),
+    ]
+    for copy in copies:
+        copy.start()
+    return copies
+
+
+def multiply(copies, work, kept_ref=None):
+    turn_vectors(work["v"], work["row"], work["turn"])
+    work["sum"][...] = jnp.zeros_like(work["sum"])
+    for copy in copies:
+        copy.wait()
+    if kept_ref is None:
+        apply_cov(work, work["s"], KEEP, 0)
+    else:
+        apply_kept(work, kept_ref, work["ring"])
+
+
+def lay_own(first_ref, last_ref, work):
+    regions = first_ref.shape[1] * 2 // ROWS
+    lay_grid([first_ref, last_ref], range(regions), work["row"], work["grid"])
+    spread_rows(work["grid"], (work["along_i"], work["across_i"]))
+    lay_tables(work["grid"], regions, (work["along"], work["across"]))
+
+
+def lay_halo(before_ref, after_ref, first_ref, last_ref, work):
+    regions = first_ref.shape[1] * 2 // ROWS
+    offsets = list(range(-REACH, 0)) + list(range(regions, regions + REACH))
+    lay_grid([first_ref, last_ref], range(regions), work["row_i"], work["grid_i"])
+    lay_grid([before_ref, after_ref], offsets, work["row"], work["grid"])
+    lay_tables(work["grid"], 2 * REACH, (work["along"], work["across"]))
+
+
+def take_rows(chunks, row_ref):
+    width = chunks[0].shape[1]
+    for c, ref in enumerate(chunks):
+        row_ref[:, c * width : (c + 1) * width] = ref[ref.shape[0] - 8 :, :]
+
+
+def first_own_kernel(
+    names, first_ref, last_ref, sum_out, span_out, item_out, along_out, across_out, along_i_out, across_i_out, s_out, *refs
+):
+    work = dict(zip(names, refs))
+    work.update(along=along_out, across=across_out, along_i=along_i_out, across_i=across_i_out)
+    work.update(sum=sum_out, s=s_out)
+    ens = work["v"].shape[0]
+    lead = first_ref.shape[1]
+    lay_own(first_ref, last_ref, work)
+    pairs = own_pairs(2 * lead // ROWS)
+    plan_windows(pairs, work["row"], work["grid"], work["row"], work["grid"], span_out, item_out)
+    copies = start_plan(span_out, item_out, work)
+    work["v"][:, :lead] = first_ref[:ens, :]
+    work["v"][:, lead:] = last_ref[:ens, :]
+    multiply(copies, work)
+
+
+def first_halo_kernel(
+    names,
+    before_ref,
+    after_ref,
+    first_ref,
+    last_ref,
+    base_ref,
+    along_i_ref,
+    across_i_ref,
     imga_ref,
     imgb_ref,
     gram_ref,
     span_out,
     item_out,
-    span_ref,
-    item_ref,
-    plan_sem,
-    row_ref,
-    grid_ref,
-    along_ref,
-    across_ref,
-    along_i_ref,
-    across_i_ref,
-    v_ref,
-    img_ref,
-    turn_ref,
-    sum_ref,
-    s_ref,
+    along_out,
+    across_out,
+    s_out,
+    *refs,
 ):
-    ens, own = img_ref.shape
-    lead = REACH * ROWS
-    chunks = [c0, c1, c2, c3]
-    tables = (along_ref, across_ref)
-    spreads = (along_i_ref, across_i_ref)
-    lay_grid(chunks, row_ref, grid_ref)
-    plan_windows(row_ref, grid_ref, span_out, item_out)
-    span_copy = pltpu.make_async_copy(span_out, span_ref, plan_sem.at[0])
-    item_copy = pltpu.make_async_copy(item_out, item_ref, plan_sem.at[1])
-    span_copy.start()
-    item_copy.start()
-    lay_tables(grid_ref, tables, spreads)
-    for c, ref in enumerate(chunks):
-        v_ref[:, c * lead : (c + 1) * lead] = ref[:ens, :]
-    turn_vectors(v_ref, row_ref, turn_ref)
-    span_copy.wait()
-    item_copy.wait()
-    apply_cov(
-        span_ref, item_ref, row_ref, tables, spreads, v_ref, img_ref, turn_ref, sum_ref, s_ref
-    )
+    work = dict(zip(names, refs))
+    work.update(along=along_out, across=across_out, along_i=along_i_ref, across_i=across_i_ref, s=s_out)
+    ens = work["v"].shape[0]
+    lead = first_ref.shape[1]
+    lay_halo(before_ref, after_ref, first_ref, last_ref, work)
+    pairs = halo_pairs(2 * lead // ROWS)
+    plan_windows(pairs, work["row"], work["grid"], work["row_i"], work["grid_i"], span_out, item_out)
+    copies = start_plan(span_out, item_out, work)
+    work["v"][:, :lead] = before_ref[:ens, :]
+    work["v"][:, lead:] = after_ref[:ens, :]
+    multiply(copies, work)
+    work["v"][:, :lead] = first_ref[:ens, :]
+    work["v"][:, lead:] = last_ref[:ens, :]
+    img_ref = work["img"]
+    finish(work["sum"], base_ref, work["row_i"], work["v"], img_ref)
     imga_ref[...] = img_ref[:, :lead]
     imgb_ref[...] = img_ref[:, lead:]
-    r = v_ref[:, lead : lead + own]
+    r = work["v"][...]
     both = gram(r, jnp.concatenate([r, img_ref[...]], axis=0))
     packed, spare = pack_pair(both[:, :ens], both[:, ens:])
     half = ens // 2
@@ -468,57 +563,80 @@
     gram_ref[half : half + 8, :] = jnp.concatenate([spare, spare], axis=1)
 
 
-def second_kernel(
+def second_own_kernel(
+    names,
     span_in,
     item_in,
-    step_ref,
-    c0,
-    c1,
-    c2,
-    c3,
-    i0,
-    i1,
-    i2,
-    i3,
     gram_ref,
-    span_ref,
-    item_ref,
-    plan_sem,
-    row_ref,
-    grid_ref,
+    first_ref,
+    last_ref,
+    imga_ref,
+    imgb_ref,
     along_ref,
     across_ref,
     along_i_ref,
     across_i_ref,
-    v_ref,
-    img_ref,
-    turn_ref,
-    sum_ref,
-    s_ref,
+    kept_ref,
+    sum_out,
+    rest_out,
+    step_out,
+    inv_out,
+    curv_out,
+    *refs,
 ):
-    ens, own = img_ref.shape
-    lead = REACH * ROWS
-    chunks = [c0, c1, c2, c3]
-    tables = (along_ref, across_ref)
-    spreads = (along_i_ref, across_i_ref)
-    span_copy = pltpu.make_async_copy(span_in, span_ref, plan_sem.at[0])
-    item_copy = pltpu.make_async_copy(item_in, item_ref, plan_sem.at[1])
-    span_copy.start()
-    item_copy.start()
-    lay_grid(chunks, row_ref, grid_ref)
-    lay_tables(grid_ref, tables, spreads)
+    work = dict(zip(names, refs))
+    work.update(along=along_ref, across=across_ref, along_i=along_i_ref, across_i=across_i_ref)
+    work.update(sum=sum_out, v=rest_out)
+    ens = step_out.shape[0]
+    lead = first_ref.shape[1]
+    copies = start_plan(span_in, item_in, work)
+    take_rows([first_ref, last_ref], work["row"])
+    solve_first(gram_ref, step_out, inv_out, curv_out)
+    step_t = step_out[...].T
+    rest_out[:, :lead] = first_ref[:ens, :] - combine(step_t, imga_ref[...])
+    rest_out[:, lead:] = last_ref[:ens, :] - combine(step_t, imgb_ref[...])
+    multiply(copies, work, kept_ref)
+
+
+def second_halo_kernel(
+    names,
+    span_in,
+    item_in,
+    step_ref,
+    before_ref,
+    after_ref,
+    img_before_ref,
+    img_after_ref,
+    first_ref,
+    last_ref,
+    rest_ref,
+    imga_ref,
+    imgb_ref,
+    base_ref,
+    along_ref,
+    across_ref,
+    along_i_ref,
+    across_i_ref,
+    kept_ref,
+    gram_ref,
+    *refs,
+):
+    work = dict(zip(names, refs))
+    work.update(along=along_ref, across=across_ref, along_i=along_i_ref, across_i=across_i_ref)
+    ens = step_ref.shape[0]
+    lead = before_ref.shape[1]
+    copies = start_plan(span_in, item_in, work)
+    take_rows([first_ref, last_ref], work["row_i"])
+    take_rows([before_ref, after_ref], work["row"])
     step_t = step_ref[...].T
-    for c, (ref, image) in enumerate(zip(chunks, [i0, i1, i2, i3])):
-        v_ref[:, c * lead : (c + 1) * lead] = ref[:ens, :] - combine(step_t, image[...])
-    turn_vectors(v_ref, row_ref, turn_ref)
-    span_copy.wait()
-    item_copy.wait()
-    apply_cov(
-        span_ref, item_ref, row_ref, tables, spreads, v_ref, img_ref, turn_ref, sum_ref, s_ref
-    )
-    r = v_ref[:, lead : lead + own]
+    work["v"][:, :lead] = before_ref[:ens, :] - combine(step_t, img_before_ref[...])
+    work["v"][:, lead:] = after_ref[:ens, :] - combine(step_t, img_after_ref[...])
+    multiply(copies, work, kept_ref)
+    img_ref = work["img"]
+    finish(work["sum"], base_ref, work["row_i"], rest_ref, img_ref)
+    r = rest_ref[...]
     both = gram(r, jnp.concatenate([r, img_ref[...]], axis=0))
-    mixed = gram(r, jnp.concatenate([i1[...], i2[...]], axis=1))
+    mixed = gram(r, jnp.concatenate([imga_ref[...], imgb_ref[...]], axis=1))
     packed, spare = pack_pair(both[:, :ens], both[:, ens:])
     gram_ref[0:ens, :] = jnp.concatenate([packed, mixed], axis=1)
     gram_ref[ens : ens + 8, :] = jnp.concatenate([spare, spare], axis=1)
@@ -530,61 +648,89 @@
     return (8 * (ROWS // 128 + 1), tiles), (3, most // 128 + 1, 128)
 
 
-def scratch(ens, own):
-    regions = own // ROWS + 2 * REACH
-    wide = regions * ROWS
-    lines = -(-(regions * (ROWS // 128 + 1) + 1) // 8) * 8
-    table = pltpu.VMEM((128 // STEP * lines, 128), f32)
-    spread = pltpu.VMEM((own, 128), f32)
+def plan_out(own):
+    return tuple(jax.ShapeDtypeStruct(shape, jnp.int32) for shape in plan_shapes(own))
+
+
+def table_shapes(own, halo):
+    near = 2 * REACH if halo else own // ROWS
+    slots = widest((halo_pairs if halo else own_pairs)(own // ROWS))
+    table = jax.ShapeDtypeStruct((128 // STEP * near * (ROWS // 128 + 1), 128), f32)
+    kept = jax.ShapeDtypeStruct((KEEP + PAIR, 2 * TILE, slots * 128), bf16)
+    return (table, table), (kept,)
+
+
+def scratch(ens, own, halo, again):
+    regions = own // ROWS
+    near = 2 * REACH if halo else regions
+    slots = widest((halo_pairs if halo else own_pairs)(regions))
+
+    def grid(count):
+        return pltpu.VMEM((3, -(-(count * (ROWS // 128 + 1) + 1) // 8) * 8, 128), f32)
+
     spans, items = plan_shapes(own)
-    return [
-        pltpu.SMEM(spans, jnp.int32),
-        pltpu.SMEM(items, jnp.int32),
-        pltpu.SemaphoreType.DMA((2,)),
-        pltpu.VMEM((8, wide), f32),
-        pltpu.VMEM((3, lines, 128), f32),
-        table,
-        table,
-        spread,
-        spread,
-        pltpu.VMEM((ens, wide), f32),
-        pltpu.VMEM((ens, own), f32),
-        pltpu.VMEM((regions * (ROWS + 128) + 128, 2 * ens), bf16),
-        pltpu.VMEM((own, 128), f32),
-        pltpu.VMEM((PAIR, 2 * TILE, (2 * REACH + 1) * 128), bf16),
-    ]
-
-
-def first_call(chunks, ens, own):
+    shapes = {
+        "span": pltpu.SMEM(spans, jnp.int32),
+        "item": pltpu.SMEM(items, jnp.int32),
+        "plan_sem": pltpu.SemaphoreType.DMA((2,)),
+        "row": pltpu.VMEM((8, near * ROWS), f32),
+        "turn": pltpu.VMEM((near * (ROWS + 128), 2 * ens), bf16),
+    }
+    if not again:
+        shapes["grid"] = grid(near)
+    if again:
+        shapes["ring"] = pltpu.VMEM((PAIR, 2 * TILE, slots * 128), bf16)
+    if halo:
+        shapes["row_i"] = pltpu.VMEM((8, own), f32)
+        shapes["grid_i"] = grid(regions)
+        shapes["img"] = pltpu.VMEM((ens, own), f32)
+        shapes["sum"] = pltpu.VMEM((own, 128), f32)
+    if halo or not again:
+        shapes["v"] = pltpu.VMEM((ens, near * ROWS), f32)
+    return tuple(shapes), list(shapes.values())
+
+
+def operate(kernel, name, kind, args, outs, ens, own):
+    names, shapes = scratch(ens, own, *kind)
+    return pl.pallas_call(
+        functools.partial(kernel, names),
+        out_shape=outs,
+        in_specs=[vmem] * len(args),
+        out_specs=(vmem,) * len(outs),
+        scratch_shapes=shapes,
+        compiler_params=params(),
+        cost_estimate=pl.CostEstimate(flops=10**10, bytes_accessed=4 << 20, transcendentals=0),
+        name=name,
+    )(*args)
+
+
+def first_own_call(first, last, ens, own):
+    tables, kept = table_shapes(own, False)
+    spread = jax.ShapeDtypeStruct((own, 128), f32)
+    outs = (spread,) + plan_out(own) + tables + (spread, spread) + kept
+    return operate(first_own_kernel, "first_own", (False, False), (first, last), outs, ens, own)
+
+
+def first_halo_call(chunks, base, spreads, ens, own):
+    tables, kept = table_shapes(own, True)
     half = jax.ShapeDtypeStruct((ens, own // 2), f32)
-    spans, items = plan_shapes(own)
-    return pl.pallas_call(
-        first_kernel,
-        out_shape=(
-            half,
-            half,
-            jax.ShapeDtypeStruct((ens // 2 + 8, 2 * ens), f32),
-            jax.ShapeDtypeStruct(spans, jnp.int32),
-            jax.ShapeDtypeStruct(items, jnp.int32),
-        ),
-        in_specs=[vmem] * 4,
-        out_specs=(vmem,) * 5,
-        scratch_shapes=scratch(ens, own),
-        compiler_params=params(),
-        name="operate_first",
-    )(*chunks)
-
-
-def second_call(plan, step, chunks, images, ens, own):
-    return pl.pallas_call(
-        second_kernel,
-        out_shape=jax.ShapeDtypeStruct((ens + 8, 2 * ens), f32),
-        in_specs=[vmem] * 11,
-        out_specs=vmem,
-        scratch_shapes=scratch(ens, own),
-        compiler_params=params(),
-        name="operate_second",
-    )(*plan, step, *chunks, *images)
+    outs = (half, half, jax.ShapeDtypeStruct((ens // 2 + 8, 2 * ens), f32))
+    outs += plan_out(own) + tables + kept
+    args = (*chunks, base, *spreads)
+    return operate(first_halo_kernel, "first_halo", (True, False), args, outs, ens, own)
+
+
+def second_own_call(plan, grams, first, last, imga, imgb, laid, ens, own):
+    small = jax.ShapeDtypeStruct((ens, ens), f32)
+    outs = (jax.ShapeDtypeStruct((own, 2 * ens), f32), jax.ShapeDtypeStruct((ens, own), f32))
+    args = (*plan, grams, first, last, imga, imgb, *laid)
+    return operate(second_own_kernel, "second_own", (False, True), args, outs + (small,) * 3, ens, own)
+
+
+def second_halo_call(plan, step, before, after, images, first, last, rest, mine, base, laid, ens, own):
+    args = (*plan, step, before, after, *images, first, last, rest, *mine, base, *laid)
+    outs = (jax.ShapeDtypeStruct((ens + 8, 2 * ens), f32),)
+    return operate(second_halo_kernel, "second_halo", (True, True), args, outs, ens, own)[0]
 
 
 def flip(me, size):
@@ -668,33 +814,23 @@
     gain_ref,
     owner_ref,
     out_ref,
-    before_ref,
-    after_ref,
     back_ref,
     cols_ref,
-    came_ref,
+    edge_ref,
     scaled_ref,
-    edge_ref,
     send,
     recv,
     send_sem,
     recv_sem,
-    bulk_send_sem,
-    bulk_recv_sem,
 ):
     ens, half = imga_ref.shape
-    me, left, right = ring(total, n_col)
+    me = lax.axis_index("reg") * n_col + lax.axis_index("col")
     partners = partners_of(steps, n_col, me)
-    everyone = [other for group in partners for other in group] + [left, right]
+    everyone = [other for group in partners for other in group]
     greet(everyone)
     pl.semaphore_wait(pltpu.get_barrier_semaphore(), len(everyone))
-    bulk = (bulk_send_sem, bulk_recv_sem)
-    copies = [send_to(imga_ref, after_ref, bulk, 0, left), send_to(imgb_ref, before_ref, bulk, 1, right)]
-    edge = send_to(edge_ref, came_ref, bulk, 2, right)
 
     def unsort():
-        for copy in copies:
-            copy.start()
         for k, img_ref in enumerate((imga_ref, imgb_ref)):
 
             def one(r, carry, k=k, img_ref=img_ref):
@@ -716,14 +852,11 @@
 
     def outer():
         add_columns(scaled_ref, owner_ref, me, total, COLS_DEV, edge_ref)
-        edge.start()
 
     def inner():
         add_columns(scaled_ref, owner_ref, me, total, 0, cols_ref)
 
     out_ref[...] = sum_all(partners, x_ref, send, recv, (send_sem, recv_sem), [unsort, outer, inner])
-    for copy in copies + [edge]:
-        copy.wait()
 
 
 def join_second_kernel(
@@ -739,11 +872,11 @@
     cols_ref,
     came_ref,
     scaled_ref,
-    edge_ref,
     send,
     recv,
     send_sem,
     recv_sem,
+    edge_ref,
     bulk_send_sem,
     bulk_recv_sem,
 ):
@@ -766,26 +899,23 @@
 
     def outer():
         add_columns(scaled_ref, owner_ref, me, total, COLS_DEV, edge_ref)
+
+    def inner():
         edge.start()
-
-    def inner():
         add_columns(scaled_ref, owner_ref, me, total, 0, cols_ref)
 
     out_ref[...] = sum_all(partners, x_ref, send, recv, (send_sem, recv_sem), [scale, outer, inner])
     edge.wait()
 
 
-def join_scratch(steps, shape, ens, own, bulk):
+def join_scratch(steps, shape, ens, own):
     slots = sum(2 ** len(amounts) - 1 for amounts in steps)
     return [
         pltpu.VMEM((2 * ens, own), bf16),
-        pltpu.VMEM((ens, COLS_DEV), f32),
         pltpu.VMEM((len(steps),) + shape, f32),
         pltpu.VMEM((slots,) + shape, f32),
         pltpu.SemaphoreType.DMA((slots,)),
         pltpu.SemaphoreType.DMA((slots,)),
-        pltpu.SemaphoreType.DMA((bulk,)),
-        pltpu.SemaphoreType.DMA((bulk,)),
     ]
 
 
@@ -793,21 +923,18 @@
     ens, half = imga.shape
     total, n_col = sizes()
     steps = exchange_steps(total)
-    halo = jax.ShapeDtypeStruct((ens, half), f32)
     cols = jax.ShapeDtypeStruct((ens, COLS_DEV), f32)
     return pl.pallas_call(
         functools.partial(join_first_kernel, steps, total, n_col),
         out_shape=(
             jax.ShapeDtypeStruct(x.shape, f32),
-            halo,
-            halo,
             jax.ShapeDtypeStruct((ens, 2 * half), f32),
             cols,
             cols,
         ),
         in_specs=[vmem] * 6,
-        out_specs=(vmem, anywhere, anywhere, vmem, vmem, anywhere),
-        scratch_shapes=join_scratch(steps, x.shape, ens, 2 * half, 3),
+        out_specs=(vmem,) * 4,
+        scratch_shapes=join_scratch(steps, x.shape, ens, 2 * half),
         compiler_params=comm_params(1),
         name="join_first",
     )(x, imga, imgb, rank, gain, owner)
@@ -823,7 +950,12 @@
         out_shape=(jax.ShapeDtypeStruct(x.shape, f32), cols, cols),
         in_specs=[smem] + [vmem] * 4,
         out_specs=(vmem, vmem, anywhere),
-        scratch_shapes=join_scratch(steps, x.shape, ens, own, 1),
+        scratch_shapes=join_scratch(steps, x.shape, ens, own)
+        + [
+            pltpu.VMEM((ens, COLS_DEV), f32),
+            pltpu.SemaphoreType.DMA((1,)),
+            pltpu.SemaphoreType.DMA((1,)),
+        ],
         compiler_params=comm_params(2),
         name="join_second",
     )(count, x, innov, gain, owner)
@@ -867,7 +999,7 @@
     return [jnp.concatenate(m, axis=0)[:, ens:] for m in chains]
 
 
-def solve_first_kernel(gram_ref, step_ref, inv_ref, curv_ref):
+def solve_first(gram_ref, step_ref, inv_ref, curv_ref):
     ens = step_ref.shape[0]
     half = ens // 2
     packed = jnp.concatenate([gram_ref[0:half, :ens], gram_ref[0:half, ens:]], axis=0)
@@ -882,7 +1014,7 @@
     curv_ref[...] = curv
 
 
-def solve_second_kernel(gram_ref, step_ref, inv_ref, curv_ref, coef_ref):
+def solve_second(gram_ref, step_ref, inv_ref, curv_ref):
     ens = step_ref.shape[0]
     norm, cross = unpack_pair(gram_ref[0:ens, :ens], gram_ref[ens : ens + 1, :ens])
     mixed = gram_ref[0:ens, ens:]
@@ -893,36 +1025,13 @@
     (step,) = eliminate([jnp.concatenate([curv, norm], axis=1)])
     step0 = step_ref[...]
     keep = step0 + step + mm(conj, step)
-    coef_ref[...] = jnp.concatenate([keep.T, -mm(step0, step).T], axis=1)
-
-
-def solve_first(grams):
-    ens = grams.shape[1] // 2
-    small = jax.ShapeDtypeStruct((ens, ens), f32)
-    return pl.pallas_call(
-        solve_first_kernel,
-        out_shape=(small, small, small),
-        in_specs=[vmem],
-        out_specs=(vmem, vmem, vmem),
-        name="solve_first",
-    )(grams)
-
-
-def solve_second(grams, step0, inv0, curv0):
-    ens = step0.shape[0]
-    return pl.pallas_call(
-        solve_second_kernel,
-        out_shape=jax.ShapeDtypeStruct((ens, 2 * ens), f32),
-        in_specs=[vmem] * 4,
-        out_specs=vmem,
-        name="solve_second",
-    )(grams, step0, inv0, curv0)
-
-
-def final_kernel(count_ref, coef_ref, innov_ref, back_ref, rc_ref, rin_ref, ic_ref, iin_ref, w_ref, inc_ref):
-    coef = coef_ref[...]
-    ens = coef.shape[0]
-    first, second = coef[:, :ens], coef[:, ens:]
+    return keep.T, -mm(step0, step).T
+
+
+def final_kernel(
+    count_ref, gram_ref, step_ref, inv_ref, curv_ref, innov_ref, back_ref, rc_ref, rin_ref, ic_ref, iin_ref, w_ref, inc_ref
+):
+    first, second = solve_second(gram_ref, step_ref, inv_ref, curv_ref)
     for g in range(innov_ref.shape[1] // ROWS):
         at = pl.ds(g * ROWS, ROWS)
         live = live_row(count_ref, g)
@@ -932,7 +1041,7 @@
     )
 
 
-def final_call(count, coef, innov, back, *cols):
+def final_call(count, solved, innov, back, *cols):
     ens, own = innov.shape
     return pl.pallas_call(
         final_kernel,
@@ -940,11 +1049,11 @@
             jax.ShapeDtypeStruct((ens, own), f32),
             jax.ShapeDtypeStruct((ens, COLS_DEV), f32),
         ),
-        in_specs=[smem] + [vmem] * 7,
+        in_specs=[smem] + [vmem] * 10,
         out_specs=(vmem, vmem),
         compiler_params=params(),
         name="final",
-    )(count, coef, innov, back, *cols)
+    )(count, *solved, innov, back, *cols)
 
 
 def on_device(
@@ -961,15 +1070,26 @@
     ens, own = innovation.shape
     rows = [x.reshape(1, own) for x in (obs_along, obs_across, obs_scale, obs_error)]
     gain, owner = obs_gain.reshape(1, own), col_owner.reshape(1, own)
-    first, last, before, after, rank = sort_call(obs_count, pair_live, innovation, *rows)
-    chunks = [before, first, last, after]
-    imga, imgb, grams, *plan = first_call(chunks, ens, own)
-    grams, img_before, img_after, back, ic, iin = join_first(grams, imga, imgb, rank, gain, owner)
-    step0, inv0, curv0 = solve_first(grams)
-    grams = second_call(plan, step0, chunks, [img_before, imga, imgb, img_after], ens, own)
+    first, last, rank = sort_call(obs_count, pair_live.T, innovation, *rows)
+    after, before = shift(first, -1), shift(last, 1)
+    base, *rest = first_own_call(first, last, ens, own)
+    plan_own, laid_own = rest[:2], rest[2:]
+    spreads = laid_own[2:4]
+    chunks = [before, after, first, last]
+    imga, imgb, grams, *rest = first_halo_call(chunks, base, spreads, ens, own)
+    plan_halo, laid_halo = rest[:2], rest[2:4] + spreads + rest[4:]
+    grams, back, ic, edge = join_first(grams, imga, imgb, rank, gain, owner)
+    senda, sendb, grams = lax.optimization_barrier((imga, imgb, grams))
+    img_after, img_before = shift(senda, -1), shift(sendb, 1)
+    iin = shift(edge, 1)
+    base, rest, step0, inv0, curv0 = second_own_call(plan_own, grams, first, last, imga, imgb, laid_own, ens, own)
+    images = [img_before, img_after]
+    grams = second_halo_call(
+        plan_halo, step0, before, after, images, first, last, rest, [imga, imgb], base, laid_halo, ens, own
+    )
     grams, rc, rin = join_second(obs_count, grams, innovation, gain, owner)
-    coef = solve_second(grams, step0, inv0, curv0)
-    return tuple(final_call(obs_count, coef, innovation, back, rc, rin, ic, iin))
+    solved = (grams, step0, inv0, curv0)
+    return tuple(final_call(obs_count, solved, innovation, back, rc, rin, ic, iin))
 
 
 def solution(mesh):

time: 118 us -> 101 us (0.86)
  Pallas kernels: 115 us -> 82.5 us
  starting transfers between devices: 0 us -> 11.9 us
  waiting for transfers between devices: 0 us -> 2.67 us
    pallas_call x5, Pallas kernels: 61.1 us -> 39 us  [the longest x4 31.6 us: operate(): pl.pallas_call(functools.partial(kernel, names), out_shape=outs, in_specs...]
    pallas_call x1, Pallas kernels: 32 us -> 18.6 us  [join_first(): pl.pallas_call(functools.partial(join_first_kernel, steps, total, n_col),...]
    ppermute x0 -> x5, starting transfers between devices: none -> 11.9 us  [shift(): lax.ppermute(block, axis, [((i - distance) % n, i) for i in range(n)])]
    ppermute x0 -> x5, waiting for transfers between devices: none -> 2.67 us  [shift(): lax.ppermute(block, axis, [((i - distance) % n, i) for i in range(n)])]
    pallas_call x1, Pallas kernels: 17.9 us -> 19.6 us  [join_second(): pl.pallas_call(functools.partial(join_second_kernel, steps, total, n_col)...]
    pallas_call x1, Pallas kernels: 3.69 us -> 5.33 us  [final_call(): pl.pallas_call(final_kernel, out_shape=(jax.ShapeDtypeStruct((ens, own),...]
  transfers between devices with their start and end apart: 0 -> 5, of which waited for: 0 -> 1; matrix products, arithmetic and copies ran while one was open for 0% -> 0% of each run, Pallas kernels for 0% -> 42%
where the time goes in v4:
time: 101 us; the launch traced here: 100 us
  Pallas kernels  82.5 us (82%)
  starting transfers between devices  11.9 us (12%)
  waiting for transfers between devices  2.67 us (3%)
  local copies, waits for them, and re-layouts  2.19 us (2%)
    pallas_call x4, Pallas kernels, operate(): pl.pallas_call(functools.partial(kernel, names), out_shape=outs, in_specs...  31.6 us
    pallas_call x1, Pallas kernels, join_second(): pl.pallas_call(functools.partial(join_second_kernel, steps, total, n_col)...  19.6 us
    pallas_call x1, Pallas kernels, join_first(): pl.pallas_call(functools.partial(join_first_kernel, steps, total, n_col),...  18.6 us
    ppermute x5, starting transfers between devices, shift(): lax.ppermute(block, axis, [((i - distance) % n, i) for i in range(n)])  11.9 us
    pallas_call x1, Pallas kernels, sort_call(): pl.pallas_call(sort_kernel, out_shape=(half, half, jax.ShapeDtypeStruct((...  7.46 us
    pallas_call x1, Pallas kernels, final_call(): pl.pallas_call(final_kernel, out_shape=(jax.ShapeDtypeStruct((ens, own),...  5.33 us
    ppermute x5, waiting for transfers between devices, shift(): lax.ppermute(block, axis, [((i - distance) % n, i) for i in range(n)])  2.67 us
    unnamed x14, local copies, waits for them, and re-layouts  2.19 us
  transfers between devices with their start and end apart: 5, of which 1 were waited for; matrix products, arithmetic and copies ran while one was open for 0% of the time, Pallas kernels for 42%

profile of v4, /device:TPU:0, one launch (start us, length us, event | category | flops | bytes accessed | tf_op | source)
XLA Modules:
  0.0 100.0 jit_solution(15457209705757206733)
XLA Ops:
  0.6 7.5 %sort_slots.1 = (f32[72,2048]{1,0:T(8,128)}, f32[72,2048]{1,0:T(8,128)}, f32[8,4096]{1,0:T(8,128)}) custom-call(s32[4]{0:T(128)} %count_ref.5, s32[2,4]{1,0:T(2,128)} %bitcast.15, f32[64,4096]{1,0:T(8,128)} %innov_ref.5, f32[1,4096]{1,0:T(1,128)} %bitcast.11, f32[1,4096]{1,0:T(1,128)} %bitcast.12, f32[1,4096]{1,0:T(1,128)} %bitcast.13, f32[1,4096]{1,0:T(1,128)} %bitcast.14), custom_call_target="tpu_custom_call" | custom-call | tf_op jit(solution)/shard_map/sort_slots/pallas_call | solution.py:171
  8.1 0.5 collective-permute-start
  8.6 5.9 %collective-permute-start.1 = (f32[72,2048]{1,0:T(8,128)}, f32[72,2048]{1,0:T(8,128)S(1)}, u32[]{:S(2)}, u32[]{:S(2)}) collective-permute-start(f32[72,2048]{1,0:T(8,128)} %get-tuple-element.37.first_ref), channel_id=1, source_target_pairs={{1,0},{2,1},{3,2},{4,3},{5,4},{6,5},{7,6},{8,7},{9,8},{10,9},{11,1... | collective-permute-start | bytes 1769480 | tf_op jit(solution)/shard_map/ppermute | solution.py:38
  14.5 0.0 copy-start.5
  14.5 1.1 %copy-done.5 = f32[72,2048]{1,0:T(8,128)S(1)} copy-done((f32[72,2048]{1,0:T(8,128)S(1)}, f32[72,2048]{1,0:T(8,128)}, u32[]{:S(2)}) %copy-start.5) | copy-done | bytes 589848
  15.6 0.0 copy-start.6
  15.6 1.1 %copy-done.6 = f32[72,2048]{1,0:T(8,128)S(1)} copy-done((f32[72,2048]{1,0:T(8,128)S(1)}, f32[72,2048]{1,0:T(8,128)}, u32[]{:S(2)}) %copy-start.6) | copy-done | bytes 589848
  16.7 8.5 %first_own.1 = (f32[4096,128]{1,0:T(8,128)S(1)}, s32[72,128]{1,0:T(8,128)S(1)}, s32[3,9,128]{2,1,0:T(8,128)S(1)}, f32[288,128]{1,0:T(8,128)S(1)}, f32[288,128]{1...) custom-call(f32[72,2048]{1,0:T(8,128)S(1)} %copy-done.5, ...), custom_call_target="tpu_custom_call" | custom-call | flops 10000000000 | bytes 4194304 | tf_op jit(solution)/shard_map/first_own/pallas_call | solution.py:695
  25.2 0.0 collective-permute-done.before_ref
  25.2 0.0 collective-permute-done.1.after_ref
  25.2 0.0 copy-start.1
  25.2 0.0 copy-start.2
  25.2 0.0 copy-start.3
  25.3 8.7 %first_halo.1 = (f32[64,2048]{1,0:T(8,128)S(1)}, f32[64,2048]{1,0:T(8,128)S(1)}, f32[40,128]{1,0:T(8,128)S(1)}, s32[72,128]{1,0:T(8,128)S(1)}, s32[3,9,128]{2,1,...) custom-call(f32[72,2048]{1,0:T(8,128)S(1)} %collective-permute-done.before_ref, ...), custom_call_target="tpu_custom_call" | custom-call | flops 10000000000 | bytes 4194304 | tf_op jit(solution)/shard_map/first_halo/pallas_call | solution.py:695
  34.0 0.0 copy-done.1
  34.0 0.0 copy-done.2
  34.0 0.0 copy-done.3
  34.0 18.6 %join_first.1 = (f32[40,128]{1,0:T(8,128)S(1)}, f32[64,4096]{1,0:T(8,128)S(1)}, f32[64,1024]{1,0:T(8,128)S(1)}, f32[64,1024]{1,0:T(8,128)S(1)}) custom-call(f32[40,128]{1,0:T(8,128)S(1)} %get-tuple-element.47.x_ref, f32[64,2048]{1,0:T(8,128)S(1)} %get-tuple-element.56.imga_ref, f32[64,2048]{1,0:T(8,128)S(1)} %get-tuple-element.55.imgb_ref, ...), custom_call_target="tpu_custom_call" | custom-call | tf_op jit(solution)/shard_map/join_first/pallas_call | solution.py:927
  52.6 0.1 collective-permute-start.4
  52.6 1.8 %collective-permute-start.2 = (f32[64,2048]{1,0:T(8,128)S(1)}, f32[64,2048]{1,0:T(8,128)S(1)}, u32[]{:S(2)}, u32[]{:S(2)}) collective-permute-start(f32[64,2048]{1,0:T(8,128)S(1)} %get-tuple-element.55.imgb_ref), channel_id=1, source_target_pairs={{31,0},{0,1},{1,2},{2,3},{3,4},{4,5},{5,6},{6,7},{7,8},{8,9},{9,10... | collective-permute-start | bytes 1572872 | tf_op jit(solution)/shard_map/ppermute | solution.py:38
  54.4 3.6 %collective-permute-start.3 = (f32[64,2048]{1,0:T(8,128)S(1)}, f32[64,2048]{1,0:T(8,128)S(1)}, u32[]{:S(2)}, u32[]{:S(2)}) collective-permute-start(f32[64,2048]{1,0:T(8,128)S(1)} %get-tuple-element.56.imga_ref), channel_id=1, source_target_pairs={{1,0},{2,1},{3,2},{4,3},{5,4},{6,5},{7,6},{8,7},{9,8},{10,9},{11,1... | collective-permute-start | bytes 1572872 | tf_op jit(solution)/shard_map/ppermute | solution.py:38
  58.0 7.0 %second_own.1 = (f32[4096,128]{1,0:T(8,128)S(1)}, f32[64,4096]{1,0:T(8,128)S(1)}, f32[64,64]{1,0:T(8,128)S(1)}, f32[64,64]{1,0:T(8,128)S(1)}, f32[64,64]{1,0:T(8,128)S(1)}) custom-call(s32[72,128]{1,0:T(8,128)S(1)} %get-tuple-element.43.span_in, s32[3,9,128]{2,1,0:T(8,128)S(1)} %get-tuple-element.44.item_in, f32[40,128]{1,0:T(8,128)S(1)} %get-tuple-element.50.gram_ref, ...), custom_call_target="tpu_custom_call" | custom-call | flops 10000000000 | bytes 4194304 | tf_op jit(solution)/shard_map/second_own/pallas_call | solution.py:695
  65.1 2.7 %collective-permute-done.2.img_before_ref = f32[64,2048]{1,0:T(8,128)S(1)} collective-permute-done((f32[64,2048]{1,0:T(8,128)S(1)}, f32[64,2048]{1,0:T(8,128)S(1)}, u32[]{:S(2)}, u32[]{:S(2)}) %collective-permute-start.2) | collective-permute-done | bytes 524320 | tf_op jit(solution)/shard_map/ppermute | solution.py:38
  67.7 0.0 collective-permute-done.3.img_after_ref
  67.7 0.0 copy-start
  67.7 0.0 copy-start.4
  67.7 7.3 %second_halo.1.x_ref = f32[72,128]{1,0:T(8,128)S(1)} custom-call(s32[72,128]{1,0:T(8,128)S(1)} %get-tuple-element.41.span_in, s32[3,9,128]{2,1,0:T(8,128)S(1)} %get-tuple-element.42.item_in, f32[64,64]{1,0:T(8,128)S(1)} %get-tuple-element.54.step_ref, f32[72,2048]{1,0:T(8,128)S(1)} %collective-permute-done.before_ref, ...), custom_call_target="tpu_custom_call" | custom-call | flops 10000000000 | bytes 4194304 | tf_op jit(solution)/shard_map/second_halo/pallas_call | solution.py:695
  75.0 0.0 copy-done
  75.0 0.0 copy-done.4
  75.0 19.6 %join_second.1 = (f32[72,128]{1,0:T(8,128)S(1)}, f32[64,1024]{1,0:T(8,128)S(1)}, f32[64,1024]{1,0:T(8,128)S(1)}) custom-call(s32[4]{0:T(128)S(1)} %copy-done.4, f32[72,128]{1,0:T(8,128)S(1)} %second_halo.1.x_ref, f32[64,4096]{1,0:T(8,128)S(1)} %copy-done, f32[1,4096]{1,0:T(1,128)S(1)} %bitcast.8, s32[1,4096]{1,0:T(1,128)S(1)} %bitcast.10), custom_call_target="tpu_custom_call" | custom-call | tf_op jit(solution)/shard_map/join_second/pallas_call | solution.py:948
  94.7 0.0 collective-permute-done.4.iin_ref
  94.7 5.3 %final.1 = (f32[64,4096]{1,0:T(8,128)}, f32[64,1024]{1,0:T(8,128)}) custom-call(s32[4]{0:T(128)S(1)} %copy-done.4, f32[72,128]{1,0:T(8,128)S(1)} %get-tuple-element.62.gram_ref, f32[64,64]{1,0:T(8,128)S(1)} %get-tuple-element.54.step_ref, f32[64,64]{1,0:T(8,128)S(1)} %get-tuple-element.63.inv_ref, f32[64,64]{1,0:T(8,128)S(1)} %get-tuple-element.64.curv_ref, ...), custom_call_target="tpu_custom_call" | custom-call | tf_op jit(solution)/shard_map/final/pallas_call | solution.py:1046
Async XLA Ops:
  8.1 17.1 %collective-permute-start = (f32[72,2048]{1,0:T(8,128)}, f32[72,2048]{1,0:T(8,128)S(1)}, u32[]{:S(2)}, u32[]{:S(2)}) collective-permute-start(f32[72,2048]{1,0:T(8,128)} %get-tuple-element.36.last_ref), channel_id=1, source_target_pairs={{31,0},{0,1},{1,2},{2,3},{3,4},{4,5},{5,6},{6,7},{7,8},{8,9},{9,10... | collective-permute-start | bytes 1769480 | tf_op jit(solution)/shard_map/ppermute | solution.py:38
  8.6 16.6 %collective-permute-start.1 = (f32[72,2048]{1,0:T(8,128)}, f32[72,2048]{1,0:T(8,128)S(1)}, u32[]{:S(2)}, u32[]{:S(2)}) collective-permute-start(f32[72,2048]{1,0:T(8,128)} %get-tuple-element.37.first_ref), channel_id=1, source_target_pairs={{1,0},{2,1},{3,2},{4,3},{5,4},{6,5},{7,6},{8,7},{9,8},{10,9},{11,1... | collective-permute-start | bytes 1769480 | tf_op jit(solution)/shard_map/ppermute | solution.py:38
  14.5 1.1 %copy-start.5 = (f32[72,2048]{1,0:T(8,128)S(1)}, f32[72,2048]{1,0:T(8,128)}, u32[]{:S(2)}) copy-start(f32[72,2048]{1,0:T(8,128)} %get-tuple-element.37.first_ref) | copy-start | bytes 1769476
  15.6 1.1 %copy-start.6 = (f32[72,2048]{1,0:T(8,128)S(1)}, f32[72,2048]{1,0:T(8,128)}, u32[]{:S(2)}) copy-start(f32[72,2048]{1,0:T(8,128)} %get-tuple-element.36.last_ref) | copy-start | bytes 1769476
  25.2 8.8 %copy-start.1 = (f32[8,4096]{1,0:T(8,128)S(1)}, f32[8,4096]{1,0:T(8,128)}, u32[]{:S(2)}) copy-start(f32[8,4096]{1,0:T(8,128)} %get-tuple-element.48.rank_ref) | copy-start | bytes 393220
  25.2 8.8 %copy-start.2 = (f32[4096]{0:T(1024)S(1)}, f32[4096]{0:T(1024)}, u32[]{:S(2)}) copy-start(f32[4096]{0:T(1024)} %param.14) | copy-start | bytes 49156
  25.2 8.8 %copy-start.3 = (s32[4096]{0:T(1024)S(1)}, s32[4096]{0:T(1024)}, u32[]{:S(2)}) copy-start(s32[4096]{0:T(1024)} %param.17) | copy-start | bytes 49156
  52.6 42.1 %collective-permute-start.4 = (f32[64,1024]{1,0:T(8,128)S(1)}, f32[64,1024]{1,0:T(8,128)S(1)}, u32[]{:S(2)}, u32[]{:S(2)}) collective-permute-start(f32[64,1024]{1,0:T(8,128)S(1)} %get-tuple-element.69), channel_id=1, source_target_pairs={{31,0},{0,1},{1,2},{2,3},{3,4},{4,5},{5,6},{6,7},{7,8},{8,9},{9,10... | collective-permute-start | bytes 786440 | tf_op jit(solution)/shard_map/ppermute | solution.py:38
  52.6 15.1 %collective-permute-start.2 = (f32[64,2048]{1,0:T(8,128)S(1)}, f32[64,2048]{1,0:T(8,128)S(1)}, u32[]{:S(2)}, u32[]{:S(2)}) collective-permute-start(f32[64,2048]{1,0:T(8,128)S(1)} %get-tuple-element.55.imgb_ref), channel_id=1, source_target_pairs={{31,0},{0,1},{1,2},{2,3},{3,4},{4,5},{5,6},{6,7},{7,8},{8,9},{9,10... | collective-permute-start | bytes 1572872 | tf_op jit(solution)/shard_map/ppermute | solution.py:38
  54.4 13.3 %collective-permute-start.3 = (f32[64,2048]{1,0:T(8,128)S(1)}, f32[64,2048]{1,0:T(8,128)S(1)}, u32[]{:S(2)}, u32[]{:S(2)}) collective-permute-start(f32[64,2048]{1,0:T(8,128)S(1)} %get-tuple-element.56.imga_ref), channel_id=1, source_target_pairs={{1,0},{2,1},{3,2},{4,3},{5,4},{6,5},{7,6},{8,7},{9,8},{10,9},{11,1... | collective-permute-start | bytes 1572872 | tf_op jit(solution)/shard_map/ppermute | solution.py:38
  67.7 7.3 %copy-start = (f32[64,4096]{1,0:T(8,128)S(1)}, f32[64,4096]{1,0:T(8,128)}, u32[]{:S(2)}) copy-start(f32[64,4096]{1,0:T(8,128)} %innov_ref.5) | copy-start | bytes 3145732
  67.7 7.3 %copy-start.4 = (s32[4]{0:T(128)S(1)}, s32[4]{0:T(128)}, u32[]{:S(2)}) copy-start(s32[4]{0:T(128)} %count_ref.5) | copy-start | bytes 52

commit v5 on v4

--- a/solution.py
+++ b/solution.py
@@ -12,13 +12,11 @@
 COLS_DEV = 1024
 TILE = 32
 STEP = 16
-PAIR = 4
 PANEL = 8
 EMPTY = ROWS // STEP
 DEAD = 1e9
 FAR = 1e6
 VMEM_LIMIT = 24 * 1024 * 1024
-SORT_LIMIT = 60 * 1024 * 1024
 KEEP = 128
 
 highest = lax.Precision.HIGHEST
@@ -97,30 +95,50 @@
 def sort_kernel(
     count_ref,
     pair_ref,
+    innov_in,
+    along_in,
+    across_in,
+    scale_in,
+    error_in,
+    first_ref,
+    last_ref,
+    ranka_ref,
+    rankb_ref,
     innov_ref,
     along_ref,
     across_ref,
     scale_ref,
     error_ref,
-    first_ref,
-    last_ref,
-    rank_ref,
+    sem,
 ):
-    regions = innov_ref.shape[1] // ROWS
+    width = first_ref.shape[1]
+    per = width // ROWS
+    moves = [
+        (across_in, across_ref),
+        (along_in, along_ref),
+        (scale_in, scale_ref),
+        (error_in, error_ref),
+        (innov_in.at[:, :width], innov_ref.at[:, :width]),
+        (innov_in.at[:, width:], innov_ref.at[:, width:]),
+    ]
+    fetches = [pltpu.make_async_copy(src, dst, sem.at[k]) for k, (src, dst) in enumerate(moves)]
+    for fetch in fetches:
+        fetch.start()
+    for fetch in fetches[:4]:
+        fetch.wait()
     sub = lax.broadcasted_iota(jnp.int32, (128, 128), 0)
     lane = lax.broadcasted_iota(jnp.int32, (128, 128), 1)
 
-    def sort_region(out_ref, shift_by, r, carry):
-        g = shift_by + r
-        cols = pl.ds(pl.multiple_of(g * ROWS, ROWS), ROWS)
+    def sort_region(g):
+        out_ref, rank_ref = ((first_ref, ranka_ref), (last_ref, rankb_ref))[g // per]
+        r = g % per
+        cols = pl.ds(g * ROWS, ROWS)
+        here = pl.ds(r * ROWS, ROWS)
         live = live_row(count_ref, g)
         across = across_ref[:, cols]
         key = jnp.where(live > 0.5, across, DEAD)
         flags = [jnp.full((1, ROWS), pair_ref[d, g], jnp.int32).astype(f32) for d in range(REACH)]
         meta = [along_ref[:, cols], across, scale_ref[:, cols] * live, error_ref[:, cols]]
-        stack = jnp.concatenate(
-            [innov_ref[:, cols] * live] + meta + flags + [key, jnp.zeros((1, ROWS), f32)], axis=0
-        )
         key_col = jnp.broadcast_to(key, (128, ROWS)).T
         ranks = []
         for b in range(ROWS // 128):
@@ -137,7 +155,12 @@
                 rank = rank + jnp.sum(ahead, axis=0, keepdims=True)
             ranks.append(rank)
         rank = jnp.concatenate(ranks, axis=1)
-        rank_ref[:, cols] = jnp.broadcast_to(rank, (8, ROWS))
+        rank_ref[:, here] = jnp.broadcast_to(rank, (8, ROWS))
+        if r == 0:
+            fetches[4 + g // per].wait()
+        stack = jnp.concatenate(
+            [innov_ref[:, cols] * live] + meta + flags + [key, jnp.zeros((1, ROWS), f32)], axis=0
+        )
         lhs = jnp.concatenate(three(stack), axis=0)
         n = stack.shape[0]
         rank_i = rank.astype(jnp.int32)
@@ -145,13 +168,11 @@
             slot = lax.broadcasted_iota(jnp.int32, (256, ROWS), 0) + c * 256
             place = (slot == rank_i).astype(f32).astype(bf16)
             got = dot(lhs, place, NT)
-            at = pl.ds(pl.multiple_of(r * ROWS + c * 256, 256), 256)
+            at = pl.ds(r * ROWS + c * 256, 256)
             out_ref[:, at] = got[:n] + got[n : 2 * n] + got[2 * n :]
-        return carry
-
-    half = regions // 2
-    lax.fori_loop(0, half, functools.partial(sort_region, first_ref, 0), 0)
-    lax.fori_loop(0, half, functools.partial(sort_region, last_ref, half), 0)
+
+    for g in range(2 * per):
+        sort_region(g)
 
 
 def sizes():
@@ -168,14 +189,18 @@
 def sort_call(count, pair, innov, *rows):
     ens, n = innov.shape
     half = jax.ShapeDtypeStruct((ens + 8, n // 2), f32)
+    rank = jax.ShapeDtypeStruct((8, n // 2), f32)
     return pl.pallas_call(
         sort_kernel,
-        out_shape=(half, half, jax.ShapeDtypeStruct((8, n), f32)),
-        in_specs=[smem] * 2 + [vmem] * 5,
-        out_specs=(vmem,) * 3,
-        compiler_params=pltpu.CompilerParams(vmem_limit_bytes=SORT_LIMIT),
+        out_shape=(half, half, rank, rank),
+        in_specs=[smem] * 2 + [pl.BlockSpec(memory_space=pltpu.HBM)] * 5,
+        out_specs=(vmem,) * 4,
+        scratch_shapes=[pltpu.VMEM((ens, n), f32)]
+        + [pltpu.VMEM((1, n), f32)] * 4
+        + [pltpu.SemaphoreType.DMA((6,))],
+        compiler_params=params(),
         name="sort_slots",
-    )(count, pair, innov, *rows)
+    )(count, pair, *[pltpu.with_memory_space_constraint(x, pltpu.HBM) for x in (innov, *rows)])
 
 
 def lay_grid(chunks, offsets, row_ref, grid_ref):
@@ -368,26 +393,31 @@
     work["sum"][at, :] += got[:TILE] + got[TILE:]
 
 
-def count_trips(work):
+def unroll_of(slots):
+    return 8 if slots <= REACH else 4
+
+
+def count_trips(work, unroll):
     return lax.shift_right_logical(
-        work["item"][2, 0, 0] + (PAIR - 1), jnp.int32(PAIR.bit_length() - 1)
+        work["item"][2, 0, 0] + (unroll - 1), jnp.int32(unroll.bit_length() - 1)
     )
 
 
 def apply_cov(work, s_ref, keep, begin):
     slots = s_ref.shape[2] // 128
-    s_ref[keep : keep + PAIR] = jnp.zeros((PAIR,) + s_ref.shape[1:], bf16)
+    unroll = unroll_of(slots)
+    s_ref[keep : keep + unroll] = jnp.zeros((unroll,) + s_ref.shape[1:], bf16)
 
     def place(k):
-        return jnp.where(k < keep // PAIR, k * PAIR, keep)
+        return jnp.where(k < keep // unroll, k * unroll, keep)
 
     def step(k, carry):
         before = jnp.where(k == begin, keep, place(k - 1))
-        for p in range(PAIR):
+        for p in range(unroll):
             gather(work, s_ref[before + p], carry[p])
-        now = [windows(work, k * PAIR + p, slots) for p in range(PAIR)]
+        now = [windows(work, k * unroll + p, slots) for p in range(unroll)]
         after = place(k)
-        for p in range(PAIR):
+        for p in range(unroll):
             tile, *found = now[p]
             at = pl.ds(pl.multiple_of(tile * TILE, TILE), TILE)
             a_i = work["along_i"][at, :]
@@ -404,21 +434,22 @@
                 s_ref[after + p, TILE : 2 * TILE, d * 128 : (d + 1) * 128] = lo
         return now
 
-    trips = count_trips(work)
+    trips = count_trips(work, unroll)
     end = jnp.where(trips > begin, trips + 1, begin)
-    lax.fori_loop(begin, end, step, [windows(work, p, slots) for p in range(PAIR)])
+    lax.fori_loop(begin, end, step, [windows(work, p, slots) for p in range(unroll)])
 
 
 def apply_kept(work, kept_ref, ring_ref):
     slots = kept_ref.shape[2] // 128
-    most = KEEP // PAIR
+    unroll = unroll_of(slots)
+    most = KEEP // unroll
 
     def step(k, carry):
-        for p in range(PAIR):
-            gather(work, kept_ref[k * PAIR + p], windows(work, k * PAIR + p, slots))
+        for p in range(unroll):
+            gather(work, kept_ref[k * unroll + p], windows(work, k * unroll + p, slots))
         return carry
 
-    lax.fori_loop(0, jnp.minimum(count_trips(work), most), step, 0)
+    lax.fori_loop(0, jnp.minimum(count_trips(work, unroll), most), step, 0)
     apply_cov(work, ring_ref, 0, most)
 
 
@@ -656,7 +687,7 @@
     near = 2 * REACH if halo else own // ROWS
     slots = widest((halo_pairs if halo else own_pairs)(own // ROWS))
     table = jax.ShapeDtypeStruct((128 // STEP * near * (ROWS // 128 + 1), 128), f32)
-    kept = jax.ShapeDtypeStruct((KEEP + PAIR, 2 * TILE, slots * 128), bf16)
+    kept = jax.ShapeDtypeStruct((KEEP + unroll_of(slots), 2 * TILE, slots * 128), bf16)
     return (table, table), (kept,)
 
 
@@ -679,7 +710,7 @@
     if not again:
         shapes["grid"] = grid(near)
     if again:
-        shapes["ring"] = pltpu.VMEM((PAIR, 2 * TILE, slots * 128), bf16)
+        shapes["ring"] = pltpu.VMEM((unroll_of(slots), 2 * TILE, slots * 128), bf16)
     if halo:
         shapes["row_i"] = pltpu.VMEM((8, own), f32)
         shapes["grid_i"] = grid(regions)
@@ -810,14 +841,14 @@
     x_ref,
     imga_ref,
     imgb_ref,
-    rank_ref,
+    ranka_ref,
+    rankb_ref,
     gain_ref,
     owner_ref,
     out_ref,
     back_ref,
-    cols_ref,
+    scaled_ref,
     edge_ref,
-    scaled_ref,
     send,
     recv,
     send_sem,
@@ -831,13 +862,13 @@
     pl.semaphore_wait(pltpu.get_barrier_semaphore(), len(everyone))
 
     def unsort():
-        for k, img_ref in enumerate((imga_ref, imgb_ref)):
-
-            def one(r, carry, k=k, img_ref=img_ref):
+        for k, (img_ref, rank_ref) in enumerate(((imga_ref, ranka_ref), (imgb_ref, rankb_ref))):
+
+            def one(r, carry, k=k, img_ref=img_ref, rank_ref=rank_ref):
                 at = pl.ds(pl.multiple_of(k * half + r * ROWS, ROWS), ROWS)
-                rank = rank_ref[0:1, at].astype(jnp.int32)
-                mine = img_ref[:, pl.ds(pl.multiple_of(r * ROWS, ROWS), ROWS)]
-                lhs = jnp.concatenate(two(mine), axis=0)
+                here = pl.ds(pl.multiple_of(r * ROWS, ROWS), ROWS)
+                rank = rank_ref[0:1, here].astype(jnp.int32)
+                lhs = jnp.concatenate(two(img_ref[:, here]), axis=0)
                 got = jnp.zeros((2 * ens, ROWS), f32)
                 for c in range(ROWS // 256):
                     slot = lax.broadcasted_iota(jnp.int32, (256, ROWS), 0) + c * 256
@@ -853,10 +884,12 @@
     def outer():
         add_columns(scaled_ref, owner_ref, me, total, COLS_DEV, edge_ref)
 
-    def inner():
-        add_columns(scaled_ref, owner_ref, me, total, 0, cols_ref)
-
-    out_ref[...] = sum_all(partners, x_ref, send, recv, (send_sem, recv_sem), [unsort, outer, inner])
+    out_ref[...] = sum_all(partners, x_ref, send, recv, (send_sem, recv_sem), [unsort, outer])
+
+
+def inner_columns_kernel(total, n_col, scaled_ref, owner_ref, cols_ref):
+    me = lax.axis_index("reg") * n_col + lax.axis_index("col")
+    add_columns(scaled_ref, owner_ref, me, total, 0, cols_ref)
 
 
 def join_second_kernel(
@@ -908,10 +941,9 @@
     edge.wait()
 
 
-def join_scratch(steps, shape, ens, own):
+def join_scratch(steps, shape):
     slots = sum(2 ** len(amounts) - 1 for amounts in steps)
     return [
-        pltpu.VMEM((2 * ens, own), bf16),
         pltpu.VMEM((len(steps),) + shape, f32),
         pltpu.VMEM((slots,) + shape, f32),
         pltpu.SemaphoreType.DMA((slots,)),
@@ -919,7 +951,19 @@
     ]
 
 
-def join_first(x, imga, imgb, rank, gain, owner):
+def inner_columns(scaled, owner):
+    return pl.pallas_call(
+        functools.partial(inner_columns_kernel, *sizes()),
+        out_shape=jax.ShapeDtypeStruct((scaled.shape[0] // 2, COLS_DEV), f32),
+        in_specs=[vmem] * 2,
+        out_specs=vmem,
+        compiler_params=params(),
+        cost_estimate=pl.CostEstimate(flops=4 * 10**9, bytes_accessed=1 << 20, transcendentals=0),
+        name="inner_columns",
+    )(scaled, owner)
+
+
+def join_first(x, imga, imgb, ranka, rankb, gain, owner):
     ens, half = imga.shape
     total, n_col = sizes()
     steps = exchange_steps(total)
@@ -929,15 +973,15 @@
         out_shape=(
             jax.ShapeDtypeStruct(x.shape, f32),
             jax.ShapeDtypeStruct((ens, 2 * half), f32),
-            cols,
+            jax.ShapeDtypeStruct((2 * ens, 2 * half), bf16),
             cols,
         ),
-        in_specs=[vmem] * 6,
+        in_specs=[vmem] * 7,
         out_specs=(vmem,) * 4,
-        scratch_shapes=join_scratch(steps, x.shape, ens, 2 * half),
+        scratch_shapes=join_scratch(steps, x.shape),
         compiler_params=comm_params(1),
         name="join_first",
-    )(x, imga, imgb, rank, gain, owner)
+    )(x, imga, imgb, ranka, rankb, gain, owner)
 
 
 def join_second(count, x, innov, gain, owner):
@@ -950,7 +994,8 @@
         out_shape=(jax.ShapeDtypeStruct(x.shape, f32), cols, cols),
         in_specs=[smem] + [vmem] * 4,
         out_specs=(vmem, vmem, anywhere),
-        scratch_shapes=join_scratch(steps, x.shape, ens, own)
+        scratch_shapes=[pltpu.VMEM((2 * ens, own), bf16)]
+        + join_scratch(steps, x.shape)
         + [
             pltpu.VMEM((ens, COLS_DEV), f32),
             pltpu.SemaphoreType.DMA((1,)),
@@ -1070,7 +1115,7 @@
     ens, own = innovation.shape
     rows = [x.reshape(1, own) for x in (obs_along, obs_across, obs_scale, obs_error)]
     gain, owner = obs_gain.reshape(1, own), col_owner.reshape(1, own)
-    first, last, rank = sort_call(obs_count, pair_live.T, innovation, *rows)
+    first, last, rank_a, rank_b = sort_call(obs_count, pair_live.T, innovation, *rows)
     after, before = shift(first, -1), shift(last, 1)
     base, *rest = first_own_call(first, last, ens, own)
     plan_own, laid_own = rest[:2], rest[2:]
@@ -1078,10 +1123,11 @@
     chunks = [before, after, first, last]
     imga, imgb, grams, *rest = first_halo_call(chunks, base, spreads, ens, own)
     plan_halo, laid_halo = rest[:2], rest[2:4] + spreads + rest[4:]
-    grams, back, ic, edge = join_first(grams, imga, imgb, rank, gain, owner)
+    grams, back, scaled, edge = join_first(grams, imga, imgb, rank_a, rank_b, gain, owner)
     senda, sendb, grams = lax.optimization_barrier((imga, imgb, grams))
     img_after, img_before = shift(senda, -1), shift(sendb, 1)
     iin = shift(edge, 1)
+    ic = inner_columns(scaled, owner)
     base, rest, step0, inv0, curv0 = second_own_call(plan_own, grams, first, last, imga, imgb, laid_own, ens, own)
     images = [img_before, img_after]
     grams = second_halo_call(

time: 101 us -> 94.4 us (0.935)
  Pallas kernels: 82.5 us -> 79.1 us
  waiting for transfers between devices: 2.67 us -> 0.01 us
    pallas_call x4, Pallas kernels: 31.6 us -> 27.8 us  [operate(): pl.pallas_call(functools.partial(kernel, names), out_shape=outs, in_specs...]
    ppermute x5, waiting for transfers between devices: 2.67 us -> 0.01 us  [shift(): lax.ppermute(block, axis, [((i - distance) % n, i) for i in range(n)])]
    pallas_call x1 -> x2, Pallas kernels: 7.46 us -> 9.08 us  [the longest x1 5.8 us: sort_call(): pl.pallas_call(sort_kernel, out_shape=(half, half, rank, rank), in_specs=...]
    pallas_call x1, Pallas kernels: 18.6 us -> 17 us  [join_first(): pl.pallas_call(functools.partial(join_first_kernel, steps, total, n_col),...]
    unnamed x14 -> x12, local copies, waits for them, and re-layouts: 2.19 us -> 1.35 us
  transfers between devices with their start and end apart: 5 -> 5, of which waited for: 1 -> 0; matrix products, arithmetic and copies ran while one was open for 0% -> 0% of each run, Pallas kernels for 42% -> 47%
where the time goes in v5:
time: 94.4 us; the launch traced here: 93.3 us
  Pallas kernels  79.1 us (84%)
  starting transfers between devices  12 us (13%)
  local copies, waits for them, and re-layouts  1.35 us (1%)
    pallas_call x4, Pallas kernels, operate(): pl.pallas_call(functools.partial(kernel, names), out_shape=outs, in_specs...  27.8 us
    pallas_call x1, Pallas kernels, join_second(): pl.pallas_call(functools.partial(join_second_kernel, steps, total, n_col)...  19.9 us
    pallas_call x1, Pallas kernels, join_first(): pl.pallas_call(functools.partial(join_first_kernel, steps, total, n_col),...  17 us
    ppermute x5, starting transfers between devices, shift(): lax.ppermute(block, axis, [((i - distance) % n, i) for i in range(n)])  12 us
    pallas_call x1, Pallas kernels, sort_call(): pl.pallas_call(sort_kernel, out_shape=(half, half, rank, rank), in_specs=...  5.8 us
    pallas_call x1, Pallas kernels, final_call(): pl.pallas_call(final_kernel, out_shape=(jax.ShapeDtypeStruct((ens, own),...  5.33 us
    pallas_call x1, Pallas kernels, inner_columns(): pl.pallas_call(functools.partial(inner_columns_kernel, *sizes()), out_sha...  3.28 us
  transfers between devices with their start and end apart: 5, of which 0 were waited for; matrix products, arithmetic and copies ran while one was open for 0% of the time, Pallas kernels for 47%

profile of v5, /device:TPU:0, one launch (start us, length us, event | category | flops | bytes accessed | tf_op | source)
XLA Modules:
  0.0 93.3 jit_solution(8366490775967412015)
XLA Ops:
  0.6 0.0 copy-start.3
  0.6 0.6 copy-done.3
  1.3 0.0 copy-start.5
  1.3 0.7 copy-done.5
  2.0 5.8 %sort_slots.1 = (f32[72,2048]{1,0:T(8,128)S(1)}, f32[72,2048]{1,0:T(8,128)S(1)}, f32[8,2048]{1,0:T(8,128)S(1)}, f32[8,2048]{1,0:T(8,128)S(1)}) custom-call(s32[4]{0:T(128)S(1)} %copy-done.3, s32[2,4]{1,0:T(2,128)S(1)} %bitcast.12, f32[64,4096]{1,0:T(8,128)} %innov_ref.3, f32[1,4096]{1,0:T(1,128)} %bitcast.13, f32[1,4096]{1,0:T(1,128)} %bitcast.14, ...), custom_call_target="tpu_custom_call" | custom-call | tf_op jit(solution)/shard_map/sort_slots/pallas_call | solution.py:193
  7.8 0.5 collective-permute-start
  8.3 6.0 %collective-permute-start.1 = (f32[72,2048]{1,0:T(8,128)S(1)}, f32[72,2048]{1,0:T(8,128)S(1)}, u32[]{:S(2)}, u32[]{:S(2)}) collective-permute-start(f32[72,2048]{1,0:T(8,128)S(1)} %get-tuple-element.38.first_ref), channel_id=1, source_target_pairs={{1,0},{2,1},{3,2},{4,3},{5,4},{6,5},{7,6},{8,7},{9,8},{10,9},{11,1... | collective-permute-start | bytes 1769480 | tf_op jit(solution)/shard_map/ppermute | solution.py:36
  14.3 8.2 %first_own.1 = (f32[4096,128]{1,0:T(8,128)S(1)}, s32[72,128]{1,0:T(8,128)S(1)}, s32[3,9,128]{2,1,0:T(8,128)S(1)}, f32[288,128]{1,0:T(8,128)S(1)}, f32[288,128]{1...) custom-call(f32[72,2048]{1,0:T(8,128)S(1)} %get-tuple-element.38.first_ref, ...), custom_call_target="tpu_custom_call" | custom-call | flops 10000000000 | bytes 4194304 | tf_op jit(solution)/shard_map/first_own/pallas_call | solution.py:726
  22.5 0.0 collective-permute-done.before_ref
  22.6 0.0 collective-permute-done.1.after_ref
  22.6 0.0 copy-start.1
  22.6 0.0 copy-start.2
  22.6 7.0 %first_halo.1 = (f32[64,2048]{1,0:T(8,128)S(1)}, f32[64,2048]{1,0:T(8,128)S(1)}, f32[40,128]{1,0:T(8,128)S(1)}, s32[72,128]{1,0:T(8,128)S(1)}, s32[3,9,128]{2,1,...) custom-call(f32[72,2048]{1,0:T(8,128)S(1)} %collective-permute-done.before_ref, ...), custom_call_target="tpu_custom_call" | custom-call | flops 10000000000 | bytes 4194304 | tf_op jit(solution)/shard_map/first_halo/pallas_call | solution.py:726
  29.6 0.0 copy-done.1
  29.6 0.0 copy-done.2
  29.7 17.0 %join_first.1 = (f32[40,128]{1,0:T(8,128)S(1)}, f32[64,4096]{1,0:T(8,128)S(1)}, bf16[128,4096]{1,0:T(8,128)(2,1)S(1)}, f32[64,1024]{1,0:T(8,128)S(1)}) custom-call(f32[40,128]{1,0:T(8,128)S(1)} %get-tuple-element.48.x_ref, f32[64,2048]{1,0:T(8,128)S(1)} %get-tuple-element.58.imga_ref, f32[64,2048]{1,0:T(8,128)S(1)} %get-tuple-element.57.imgb_ref, ...), custom_call_target="tpu_custom_call" | custom-call | tf_op jit(solution)/shard_map/join_first/pallas_call | solution.py:971
  46.7 0.1 collective-permute-start.4
  46.7 1.5 %collective-permute-start.2 = (f32[64,2048]{1,0:T(8,128)S(1)}, f32[64,2048]{1,0:T(8,128)S(1)}, u32[]{:S(2)}, u32[]{:S(2)}) collective-permute-start(f32[64,2048]{1,0:T(8,128)S(1)} %get-tuple-element.57.imgb_ref), channel_id=1, source_target_pairs={{31,0},{0,1},{1,2},{2,3},{3,4},{4,5},{5,6},{6,7},{7,8},{8,9},{9,10... | collective-permute-start | bytes 1572872 | tf_op jit(solution)/shard_map/ppermute | solution.py:36
  48.2 3.9 %collective-permute-start.3 = (f32[64,2048]{1,0:T(8,128)S(1)}, f32[64,2048]{1,0:T(8,128)S(1)}, u32[]{:S(2)}, u32[]{:S(2)}) collective-permute-start(f32[64,2048]{1,0:T(8,128)S(1)} %get-tuple-element.58.imga_ref), channel_id=1, source_target_pairs={{1,0},{2,1},{3,2},{4,3},{5,4},{6,5},{7,6},{8,7},{9,8},{10,9},{11,1... | collective-permute-start | bytes 1572872 | tf_op jit(solution)/shard_map/ppermute | solution.py:36
  52.1 6.8 %second_own.1 = (f32[4096,128]{1,0:T(8,128)S(1)}, f32[64,4096]{1,0:T(8,128)S(1)}, f32[64,64]{1,0:T(8,128)S(1)}, f32[64,64]{1,0:T(8,128)S(1)}, f32[64,64]{1,0:T(8,128)S(1)}) custom-call(s32[72,128]{1,0:T(8,128)S(1)} %get-tuple-element.44.span_in, s32[3,9,128]{2,1,0:T(8,128)S(1)} %get-tuple-element.45.item_in, f32[40,128]{1,0:T(8,128)S(1)} %get-tuple-element.52.gram_ref, ...), custom_call_target="tpu_custom_call" | custom-call | flops 10000000000 | bytes 4194304 | tf_op jit(solution)/shard_map/second_own/pallas_call | solution.py:726
  58.9 3.3 %inner_columns.1.ic_ref = f32[64,1024]{1,0:T(8,128)S(1)} custom-call(bf16[128,4096]{1,0:T(8,128)(2,1)S(1)} %get-tuple-element.70.scaled_ref, s32[1,4096]{1,0:T(1,128)S(1)} %bitcast.10), custom_call_target="tpu_custom_call" | custom-call | flops 4000000000 | bytes 1048576 | tf_op jit(solution)/shard_map/inner_columns/pallas_call | solution.py:955
  62.2 0.0 collective-permute-done.2.img_before_ref
  62.2 0.0 collective-permute-done.3.img_after_ref
  62.3 0.0 copy-start
  62.3 0.0 copy-start.4
  62.3 5.7 %second_halo.1.x_ref = f32[72,128]{1,0:T(8,128)S(1)} custom-call(s32[72,128]{1,0:T(8,128)S(1)} %get-tuple-element.42.span_in, s32[3,9,128]{2,1,0:T(8,128)S(1)} %get-tuple-element.43.item_in, f32[64,64]{1,0:T(8,128)S(1)} %get-tuple-element.56.step_ref, f32[72,2048]{1,0:T(8,128)S(1)} %collective-permute-done.before_ref, ...), custom_call_target="tpu_custom_call" | custom-call | flops 10000000000 | bytes 4194304 | tf_op jit(solution)/shard_map/second_halo/pallas_call | solution.py:726
  68.0 0.0 copy-done
  68.0 0.0 copy-done.4
  68.0 19.9 %join_second.1 = (f32[72,128]{1,0:T(8,128)S(1)}, f32[64,1024]{1,0:T(8,128)S(1)}, f32[64,1024]{1,0:T(8,128)S(1)}) custom-call(s32[4]{0:T(128)S(1)} %copy-done.4, f32[72,128]{1,0:T(8,128)S(1)} %second_halo.1.x_ref, f32[64,4096]{1,0:T(8,128)S(1)} %copy-done, f32[1,4096]{1,0:T(1,128)S(1)} %bitcast.8, s32[1,4096]{1,0:T(1,128)S(1)} %bitcast.11), custom_call_target="tpu_custom_call" | custom-call | tf_op jit(solution)/shard_map/join_second/pallas_call | solution.py:992
  87.9 0.0 collective-permute-done.4.iin_ref
  88.0 5.3 %final.1 = (f32[64,4096]{1,0:T(8,128)}, f32[64,1024]{1,0:T(8,128)}) custom-call(s32[4]{0:T(128)S(1)} %copy-done.4, f32[72,128]{1,0:T(8,128)S(1)} %get-tuple-element.64.gram_ref, f32[64,64]{1,0:T(8,128)S(1)} %get-tuple-element.56.step_ref, f32[64,64]{1,0:T(8,128)S(1)} %get-tuple-element.65.inv_ref, f32[64,64]{1,0:T(8,128)S(1)} %get-tuple-element.66.curv_ref, ...), custom_call_target="tpu_custom_call" | custom-call | tf_op jit(solution)/shard_map/final/pallas_call | solution.py:1091
Async XLA Ops:
  0.6 0.7 copy-start.3
  1.3 0.7 copy-start.5
  7.8 14.8 %collective-permute-start = (f32[72,2048]{1,0:T(8,128)S(1)}, f32[72,2048]{1,0:T(8,128)S(1)}, u32[]{:S(2)}, u32[]{:S(2)}) collective-permute-start(f32[72,2048]{1,0:T(8,128)S(1)} %get-tuple-element.37.last_ref), channel_id=1, source_target_pairs={{31,0},{0,1},{1,2},{2,3},{3,4},{4,5},{5,6},{6,7},{7,8},{8,9},{9,10... | collective-permute-start | bytes 1769480 | tf_op jit(solution)/shard_map/ppermute | solution.py:36
  8.3 14.2 %collective-permute-start.1 = (f32[72,2048]{1,0:T(8,128)S(1)}, f32[72,2048]{1,0:T(8,128)S(1)}, u32[]{:S(2)}, u32[]{:S(2)}) collective-permute-start(f32[72,2048]{1,0:T(8,128)S(1)} %get-tuple-element.38.first_ref), channel_id=1, source_target_pairs={{1,0},{2,1},{3,2},{4,3},{5,4},{6,5},{7,6},{8,7},{9,8},{10,9},{11,1... | collective-permute-start | bytes 1769480 | tf_op jit(solution)/shard_map/ppermute | solution.py:36
  22.6 7.1 %copy-start.1 = (f32[4096]{0:T(1024)S(1)}, f32[4096]{0:T(1024)}, u32[]{:S(2)}) copy-start(f32[4096]{0:T(1024)} %param.14) | copy-start | bytes 49156
  22.6 7.1 %copy-start.2 = (s32[4096]{0:T(1024)S(1)}, s32[4096]{0:T(1024)}, u32[]{:S(2)}) copy-start(s32[4096]{0:T(1024)} %param.17) | copy-start | bytes 49156
  46.7 41.3 %collective-permute-start.4 = (f32[64,1024]{1,0:T(8,128)S(1)}, f32[64,1024]{1,0:T(8,128)S(1)}, u32[]{:S(2)}, u32[]{:S(2)}) collective-permute-start(f32[64,1024]{1,0:T(8,128)S(1)} %get-tuple-element.71), channel_id=1, source_target_pairs={{31,0},{0,1},{1,2},{2,3},{3,4},{4,5},{5,6},{6,7},{7,8},{8,9},{9,10... | collective-permute-start | bytes 786440 | tf_op jit(solution)/shard_map/ppermute | solution.py:36
  46.7 15.5 %collective-permute-start.2 = (f32[64,2048]{1,0:T(8,128)S(1)}, f32[64,2048]{1,0:T(8,128)S(1)}, u32[]{:S(2)}, u32[]{:S(2)}) collective-permute-start(f32[64,2048]{1,0:T(8,128)S(1)} %get-tuple-element.57.imgb_ref), channel_id=1, source_target_pairs={{31,0},{0,1},{1,2},{2,3},{3,4},{4,5},{5,6},{6,7},{7,8},{8,9},{9,10... | collective-permute-start | bytes 1572872 | tf_op jit(solution)/shard_map/ppermute | solution.py:36
  48.2 14.0 %collective-permute-start.3 = (f32[64,2048]{1,0:T(8,128)S(1)}, f32[64,2048]{1,0:T(8,128)S(1)}, u32[]{:S(2)}, u32[]{:S(2)}) collective-permute-start(f32[64,2048]{1,0:T(8,128)S(1)} %get-tuple-element.58.imga_ref), channel_id=1, source_target_pairs={{1,0},{2,1},{3,2},{4,3},{5,4},{6,5},{7,6},{8,7},{9,8},{10,9},{11,1... | collective-permute-start | bytes 1572872 | tf_op jit(solution)/shard_map/ppermute | solution.py:36
  62.3 5.7 %copy-start = (f32[64,4096]{1,0:T(8,128)S(1)}, f32[64,4096]{1,0:T(8,128)}, u32[]{:S(2)}) copy-start(f32[64,4096]{1,0:T(8,128)} %innov_ref.3) | copy-start | bytes 3145732
  62.3 5.7 %copy-start.4 = (s32[4]{0:T(128)S(1)}, s32[4]{0:T(128)}, u32[]{:S(2)}) copy-start(s32[4]{0:T(128)} %count_ref.5) | copy-start | bytes 52

commit v6 on v5

--- a/solution.py
+++ b/solution.py
@@ -163,11 +163,8 @@
         )
         lhs = jnp.concatenate(three(stack), axis=0)
         n = stack.shape[0]
-        rank_i = rank.astype(jnp.int32)
         for c in range(ROWS // 256):
-            slot = lax.broadcasted_iota(jnp.int32, (256, ROWS), 0) + c * 256
-            place = (slot == rank_i).astype(f32).astype(bf16)
-            got = dot(lhs, place, NT)
+            got = dot(lhs, one_hot(rank - float(c * 256)), NT)
             at = pl.ds(r * ROWS + c * 256, 256)
             out_ref[:, at] = got[:n] + got[n : 2 * n] + got[2 * n :]
 
@@ -200,7 +197,7 @@
         + [pltpu.SemaphoreType.DMA((6,))],
         compiler_params=params(),
         name="sort_slots",
-    )(count, pair, *[pltpu.with_memory_space_constraint(x, pltpu.HBM) for x in (innov, *rows)])
+    )(*[pltpu.with_memory_space_constraint(x, pltpu.HBM) for x in (count, pair, innov, *rows)])
 
 
 def lay_grid(chunks, offsets, row_ref, grid_ref):
@@ -463,6 +460,12 @@
         )
 
 
+def one_hot(row):
+    slot = lax.broadcasted_iota(jnp.int32, (256, row.shape[1]), 0).astype(f32).astype(bf16)
+    same = slot == jnp.broadcast_to(row, (256, row.shape[1])).astype(bf16)
+    return jnp.where(same, jnp.ones((), bf16), jnp.zeros((), bf16))
+
+
 def gram(a, b):
     ahi, alo = two(a)
     bhi, blo = two(b)
@@ -823,9 +826,8 @@
         got = jnp.zeros((scaled_ref.shape[0], 256), f32)
         for g in range(own // ROWS):
             at = slice(g * ROWS, (g + 1) * ROWS)
-            slot = lax.broadcasted_iota(jnp.int32, (256, ROWS), 0) + (base + c * 256)
             owner = local_column(owner_ref[:, at], me, total)
-            hot = (slot == owner).astype(f32).astype(bf16)
+            hot = one_hot((owner - (base + c * 256)).astype(f32))
             got = got + dot(scaled_ref[:, at], hot, NT)
         ens = target_ref.shape[0]
         target_ref[:, pl.ds(pl.multiple_of(c * 256, 256), 256)] = got[:ens] + got[ens:]
@@ -867,12 +869,11 @@
             def one(r, carry, k=k, img_ref=img_ref, rank_ref=rank_ref):
                 at = pl.ds(pl.multiple_of(k * half + r * ROWS, ROWS), ROWS)
                 here = pl.ds(pl.multiple_of(r * ROWS, ROWS), ROWS)
-                rank = rank_ref[0:1, here].astype(jnp.int32)
+                rank = rank_ref[0:1, here]
                 lhs = jnp.concatenate(two(img_ref[:, here]), axis=0)
                 got = jnp.zeros((2 * ens, ROWS), f32)
                 for c in range(ROWS // 256):
-                    slot = lax.broadcasted_iota(jnp.int32, (256, ROWS), 0) + c * 256
-                    place = (slot == rank).astype(f32).astype(bf16)
+                    place = one_hot(rank - float(c * 256))
                     got = got + dot(lhs[:, c * 256 : (c + 1) * 256], place)
                 image = got[:ens] + got[ens:]
                 back_ref[:, at] = image

time: 94.4 us -> 97.9 us (1.037); the launches traced: 93.3 us -> 99.5 us
  Pallas kernels: 79.1 us -> 86.7 us
  local copies, waits for them, and re-layouts: 1.35 us -> 0.03 us
    pallas_call x4, Pallas kernels: 27.8 us -> 38.9 us  [operate(): pl.pallas_call(functools.partial(kernel, names), out_shape=outs, in_specs...]
    pallas_call x1, Pallas kernels: 17 us -> 15.2 us  [join_first(): pl.pallas_call(functools.partial(join_first_kernel, steps, total, n_col),...]
    pallas_call x1, Pallas kernels: 19.9 us -> 18.2 us  [join_second(): pl.pallas_call(functools.partial(join_second_kernel, steps, total, n_col)...]
    unnamed x12 -> x8, local copies, waits for them, and re-layouts: 1.35 us -> 0.03 us
  transfers between devices with their start and end apart: 5 -> 5, of which waited for: 0 -> 0; matrix products, arithmetic and copies ran while one was open for 0% -> 0% of each run, Pallas kernels for 47% -> 52%
where the time goes in v6:
time: 97.9 us; the launch traced here: 99.5 us
  Pallas kernels  86.7 us (89%)
  starting transfers between devices  12 us (12%)
    pallas_call x4, Pallas kernels, operate(): pl.pallas_call(functools.partial(kernel, names), out_shape=outs, in_specs...  38.9 us
    pallas_call x1, Pallas kernels, join_second(): pl.pallas_call(functools.partial(join_second_kernel, steps, total, n_col)...  18.2 us
    pallas_call x1, Pallas kernels, join_first(): pl.pallas_call(functools.partial(join_first_kernel, steps, total, n_col),...  15.2 us
    ppermute x5, starting transfers between devices, shift(): lax.ppermute(block, axis, [((i - distance) % n, i) for i in range(n)])  12 us
    pallas_call x1, Pallas kernels, sort_call(): pl.pallas_call(sort_kernel, out_shape=(half, half, rank, rank), in_specs=...  5.71 us
    pallas_call x1, Pallas kernels, final_call(): pl.pallas_call(final_kernel, out_shape=(jax.ShapeDtypeStruct((ens, own),...  5.33 us
    pallas_call x1, Pallas kernels, inner_columns(): pl.pallas_call(functools.partial(inner_columns_kernel, *sizes()), out_sha...  3.31 us
  transfers between devices with their start and end apart: 5, of which 0 were waited for; matrix products, arithmetic and copies ran while one was open for 0% of the time, Pallas kernels for 52%

profile of v6, /device:TPU:0, one launch (start us, length us, event | category | flops | bytes accessed | tf_op | source)
XLA Modules:
  0.0 99.5 jit_solution(3692535379700515482)
XLA Ops:
  0.6 5.7 %sort_slots.1 = (f32[72,2048]{1,0:T(8,128)S(1)}, f32[72,2048]{1,0:T(8,128)S(1)}, f32[8,2048]{1,0:T(8,128)S(1)}, f32[8,2048]{1,0:T(8,128)S(1)}) custom-call(s32[4]{0:T(128)} %count_ref.5, s32[2,4]{1,0:T(2,128)} %bitcast.16, f32[64,4096]{1,0:T(8,128)} %innov_ref.3, f32[1,4096]{1,0:T(1,128)} %bitcast.12, f32[1,4096]{1,0:T(1,128)} %bitcast.13, ...), custom_call_target="tpu_custom_call" | custom-call | tf_op jit(solution)/shard_map/sort_slots/pallas_call | solution.py:190
  6.4 0.5 collective-permute-start
  6.9 6.0 %collective-permute-start.1 = (f32[72,2048]{1,0:T(8,128)S(1)}, f32[72,2048]{1,0:T(8,128)S(1)}, u32[]{:S(2)}, u32[]{:S(2)}) collective-permute-start(f32[72,2048]{1,0:T(8,128)S(1)} %get-tuple-element.38.first_ref), channel_id=1, source_target_pairs={{1,0},{2,1},{3,2},{4,3},{5,4},{6,5},{7,6},{8,7},{9,8},{10,9},{11,1... | collective-permute-start | bytes 1769480 | tf_op jit(solution)/shard_map/ppermute | solution.py:36
  12.9 12.3 %first_own.1 = (f32[4096,128]{1,0:T(8,128)S(1)}, s32[72,128]{1,0:T(8,128)S(1)}, s32[3,9,128]{2,1,0:T(8,128)S(1)}, f32[288,128]{1,0:T(8,128)S(1)}, f32[288,128]{1...) custom-call(f32[72,2048]{1,0:T(8,128)S(1)} %get-tuple-element.38.first_ref, ...), custom_call_target="tpu_custom_call" | custom-call | flops 10000000000 | bytes 4194304 | tf_op jit(solution)/shard_map/first_own/pallas_call | solution.py:729
  25.2 0.0 collective-permute-done.before_ref
  25.2 0.0 collective-permute-done.1.after_ref
  25.2 0.0 copy-start.1
  25.2 0.0 copy-start.2
  25.2 9.1 %first_halo.1 = (f32[64,2048]{1,0:T(8,128)S(1)}, f32[64,2048]{1,0:T(8,128)S(1)}, f32[40,128]{1,0:T(8,128)S(1)}, s32[72,128]{1,0:T(8,128)S(1)}, s32[3,9,128]{2,1,...) custom-call(f32[72,2048]{1,0:T(8,128)S(1)} %collective-permute-done.before_ref, ...), custom_call_target="tpu_custom_call" | custom-call | flops 10000000000 | bytes 4194304 | tf_op jit(solution)/shard_map/first_halo/pallas_call | solution.py:729
  34.4 0.0 copy-done.1
  34.4 0.0 copy-done.2
  34.4 15.2 %join_first.1 = (f32[40,128]{1,0:T(8,128)S(1)}, f32[64,4096]{1,0:T(8,128)S(1)}, bf16[128,4096]{1,0:T(8,128)(2,1)S(1)}, f32[64,1024]{1,0:T(8,128)S(1)}) custom-call(f32[40,128]{1,0:T(8,128)S(1)} %get-tuple-element.48.x_ref, f32[64,2048]{1,0:T(8,128)S(1)} %get-tuple-element.58.imga_ref, f32[64,2048]{1,0:T(8,128)S(1)} %get-tuple-element.57.imgb_ref, ...), custom_call_target="tpu_custom_call" | custom-call | tf_op jit(solution)/shard_map/join_first/pallas_call | solution.py:972
  49.6 0.1 collective-permute-start.4
  49.7 0.7 collective-permute-start.2
  50.4 4.7 %collective-permute-start.3 = (f32[64,2048]{1,0:T(8,128)S(1)}, f32[64,2048]{1,0:T(8,128)S(1)}, u32[]{:S(2)}, u32[]{:S(2)}) collective-permute-start(f32[64,2048]{1,0:T(8,128)S(1)} %get-tuple-element.58.imga_ref), channel_id=1, source_target_pairs={{1,0},{2,1},{3,2},{4,3},{5,4},{6,5},{7,6},{8,7},{9,8},{10,9},{11,1... | collective-permute-start | bytes 1572872 | tf_op jit(solution)/shard_map/ppermute | solution.py:36
  55.1 10.1 %second_own.1 = (f32[4096,128]{1,0:T(8,128)S(1)}, f32[64,4096]{1,0:T(8,128)S(1)}, f32[64,64]{1,0:T(8,128)S(1)}, f32[64,64]{1,0:T(8,128)S(1)}, f32[64,64]{1,0:T(8,128)S(1)}) custom-call(s32[72,128]{1,0:T(8,128)S(1)} %get-tuple-element.44.span_in, s32[3,9,128]{2,1,0:T(8,128)S(1)} %get-tuple-element.45.item_in, f32[40,128]{1,0:T(8,128)S(1)} %get-tuple-element.52.gram_ref, ...), custom_call_target="tpu_custom_call" | custom-call | flops 10000000000 | bytes 4194304 | tf_op jit(solution)/shard_map/second_own/pallas_call | solution.py:729
  65.2 3.3 %inner_columns.1.ic_ref = f32[64,1024]{1,0:T(8,128)S(1)} custom-call(bf16[128,4096]{1,0:T(8,128)(2,1)S(1)} %get-tuple-element.70.scaled_ref, s32[1,4096]{1,0:T(1,128)S(1)} %bitcast.10), custom_call_target="tpu_custom_call" | custom-call | flops 4000000000 | bytes 1048576 | tf_op jit(solution)/shard_map/inner_columns/pallas_call | solution.py:956
  68.5 0.0 collective-permute-done.2.img_before_ref
  68.6 0.0 collective-permute-done.3.img_after_ref
  68.6 0.0 copy-start
  68.6 0.0 copy-start.3
  68.6 7.4 %second_halo.1.x_ref = f32[72,128]{1,0:T(8,128)S(1)} custom-call(s32[72,128]{1,0:T(8,128)S(1)} %get-tuple-element.42.span_in, s32[3,9,128]{2,1,0:T(8,128)S(1)} %get-tuple-element.43.item_in, f32[64,64]{1,0:T(8,128)S(1)} %get-tuple-element.56.step_ref, f32[72,2048]{1,0:T(8,128)S(1)} %collective-permute-done.before_ref, ...), custom_call_target="tpu_custom_call" | custom-call | flops 10000000000 | bytes 4194304 | tf_op jit(solution)/shard_map/second_halo/pallas_call | solution.py:729
  76.0 0.0 copy-done
  76.0 0.0 copy-done.3
  76.0 18.2 %join_second.1 = (f32[72,128]{1,0:T(8,128)S(1)}, f32[64,1024]{1,0:T(8,128)S(1)}, f32[64,1024]{1,0:T(8,128)S(1)}) custom-call(s32[4]{0:T(128)S(1)} %copy-done.3, f32[72,128]{1,0:T(8,128)S(1)} %second_halo.1.x_ref, f32[64,4096]{1,0:T(8,128)S(1)} %copy-done, f32[1,4096]{1,0:T(1,128)S(1)} %bitcast.8, s32[1,4096]{1,0:T(1,128)S(1)} %bitcast.11), custom_call_target="tpu_custom_call" | custom-call | tf_op jit(solution)/shard_map/join_second/pallas_call | solution.py:993
  94.2 0.0 collective-permute-done.4.iin_ref
  94.2 5.3 %final.1 = (f32[64,4096]{1,0:T(8,128)}, f32[64,1024]{1,0:T(8,128)}) custom-call(s32[4]{0:T(128)S(1)} %copy-done.3, f32[72,128]{1,0:T(8,128)S(1)} %get-tuple-element.64.gram_ref, f32[64,64]{1,0:T(8,128)S(1)} %get-tuple-element.56.step_ref, f32[64,64]{1,0:T(8,128)S(1)} %get-tuple-element.65.inv_ref, f32[64,64]{1,0:T(8,128)S(1)} %get-tuple-element.66.curv_ref, ...), custom_call_target="tpu_custom_call" | custom-call | tf_op jit(solution)/shard_map/final/pallas_call | solution.py:1092
Async XLA Ops:
  6.4 18.9 %collective-permute-start = (f32[72,2048]{1,0:T(8,128)S(1)}, f32[72,2048]{1,0:T(8,128)S(1)}, u32[]{:S(2)}, u32[]{:S(2)}) collective-permute-start(f32[72,2048]{1,0:T(8,128)S(1)} %get-tuple-element.37.last_ref), channel_id=1, source_target_pairs={{31,0},{0,1},{1,2},{2,3},{3,4},{4,5},{5,6},{6,7},{7,8},{8,9},{9,10... | collective-permute-start | bytes 1769480 | tf_op jit(solution)/shard_map/ppermute | solution.py:36
  6.9 18.3 %collective-permute-start.1 = (f32[72,2048]{1,0:T(8,128)S(1)}, f32[72,2048]{1,0:T(8,128)S(1)}, u32[]{:S(2)}, u32[]{:S(2)}) collective-permute-start(f32[72,2048]{1,0:T(8,128)S(1)} %get-tuple-element.38.first_ref), channel_id=1, source_target_pairs={{1,0},{2,1},{3,2},{4,3},{5,4},{6,5},{7,6},{8,7},{9,8},{10,9},{11,1... | collective-permute-start | bytes 1769480 | tf_op jit(solution)/shard_map/ppermute | solution.py:36
  25.2 9.2 %copy-start.1 = (f32[4096]{0:T(1024)S(1)}, f32[4096]{0:T(1024)}, u32[]{:S(2)}) copy-start(f32[4096]{0:T(1024)} %param.14) | copy-start | bytes 49156
  25.2 9.2 %copy-start.2 = (s32[4096]{0:T(1024)S(1)}, s32[4096]{0:T(1024)}, u32[]{:S(2)}) copy-start(s32[4096]{0:T(1024)} %param.17) | copy-start | bytes 49156
  49.6 44.5 %collective-permute-start.4 = (f32[64,1024]{1,0:T(8,128)S(1)}, f32[64,1024]{1,0:T(8,128)S(1)}, u32[]{:S(2)}, u32[]{:S(2)}) collective-permute-start(f32[64,1024]{1,0:T(8,128)S(1)} %get-tuple-element.71), channel_id=1, source_target_pairs={{31,0},{0,1},{1,2},{2,3},{3,4},{4,5},{5,6},{6,7},{7,8},{8,9},{9,10... | collective-permute-start | bytes 786440 | tf_op jit(solution)/shard_map/ppermute | solution.py:36
  49.7 18.8 %collective-permute-start.2 = (f32[64,2048]{1,0:T(8,128)S(1)}, f32[64,2048]{1,0:T(8,128)S(1)}, u32[]{:S(2)}, u32[]{:S(2)}) collective-permute-start(f32[64,2048]{1,0:T(8,128)S(1)} %get-tuple-element.57.imgb_ref), channel_id=1, source_target_pairs={{31,0},{0,1},{1,2},{2,3},{3,4},{4,5},{5,6},{6,7},{7,8},{8,9},{9,10... | collective-permute-start | bytes 1572872 | tf_op jit(solution)/shard_map/ppermute | solution.py:36
  50.4 18.2 %collective-permute-start.3 = (f32[64,2048]{1,0:T(8,128)S(1)}, f32[64,2048]{1,0:T(8,128)S(1)}, u32[]{:S(2)}, u32[]{:S(2)}) collective-permute-start(f32[64,2048]{1,0:T(8,128)S(1)} %get-tuple-element.58.imga_ref), channel_id=1, source_target_pairs={{1,0},{2,1},{3,2},{4,3},{5,4},{6,5},{7,6},{8,7},{9,8},{10,9},{11,1... | collective-permute-start | bytes 1572872 | tf_op jit(solution)/shard_map/ppermute | solution.py:36
  68.6 7.4 %copy-start = (f32[64,4096]{1,0:T(8,128)S(1)}, f32[64,4096]{1,0:T(8,128)}, u32[]{:S(2)}) copy-start(f32[64,4096]{1,0:T(8,128)} %innov_ref.3) | copy-start | bytes 3145732
  68.6 7.4 %copy-start.3 = (s32[4]{0:T(128)S(1)}, s32[4]{0:T(128)}, u32[]{:S(2)}) copy-start(s32[4]{0:T(128)} %count_ref.5) | copy-start | bytes 52
